TPU v7x, 32 devices: a whole 2x2x4 slice. The times are simulated.
32 devices in a mesh: win: 4 (over x, core), tile: 8 (over z, y).
Axes of the slice: x: 2, y: 2, z: 4, core: 2. Of those that a mesh axis runs over, the one named last changes fastest.
Arguments:
- increment: float32 [4, 128, 256, 512], P('win', None, 'tile'), may hold values from -6 to 6
- diffusivity: float32 [4, 256, 512], P('win', 'tile'), may hold values from 0.04 to 0.2
- wind: float32 [4, 128], P('win'), may hold values from -0.3 to 0.3
- vertical_cov: bfloat16 [128, 128], replicated, may hold values from -1 to 2, as said below
- row_cov: bfloat16 [256, 256], replicated, may hold values from -1 to 2, as said below
- column_cov: bfloat16 [512, 512], replicated, may hold values from -1 to 2, as said below
Outputs:
- covaried: float32 [4, 128, 256, 512], P('win', 'tile')
Inputs may be any that keep to these rules, and one draw needn't show every extreme that they name: `vertical_cov`: symmetric and positive definite. `row_cov`: symmetric and positive definite. `column_cov`: symmetric and positive definite.
All inputs are finite; a program needn't handle non-finite values.
Results may differ from a plain program's by a relative error of at most 0.0003.
Values sent between devices are 32-bit elements; how exact they have to be, the bound alone decides.
No kernel may reach another device: no remote copies, remote signals or barrier semaphores. Data moves between devices by JAX's collectives and lax.ppermute only.
A program may use at most 128 MiB of HBM per device.

v0:
```python
import functools

import jax
import jax.numpy as jnp
from jax import lax
from jax.experimental import pallas as pl
from jax.experimental.pallas import tpu as pltpu
from jax.sharding import PartitionSpec as P


STEPS = 6
VMIX = 0.1
SUB = 8
HALO = STEPS
LANES = 128


F32 = jnp.float32
BF16 = jnp.bfloat16
ANY = pl.BlockSpec(memory_space=pl.ANY)
VM = pl.BlockSpec(memory_space=pltpu.VMEM)
SM = pl.BlockSpec(memory_space=pltpu.SMEM)


def params(limit_mib, sem=None):
    return pltpu.CompilerParams(vmem_limit_bytes=limit_mib << 20, dimension_semantics=sem)


def cost(flops, moved):
    return pl.CostEstimate(flops=int(flops), transcendentals=0, bytes_accessed=int(moved))


def iota(shape, dim):
    return lax.broadcasted_iota(jnp.int32, shape, dim)


def turn(parts):
    parts = list(parts)
    sub = iota(parts[0].shape, 0)
    for d in (4, 2, 1):
        low = (sub & d) == 0
        for i in range(SUB):
            if i & d == 0:
                a, b = parts[i], parts[i + d]
                parts[i] = jnp.where(low, a, pltpu.roll(b, d, axis=0))
                parts[i + d] = jnp.where(low, pltpu.roll(a, SUB - d, axis=0), b)
    return parts


def pieces_kernel(me_ref, raw_ref, kap_ref, mid_ref, inner_ref, far_ref, near_ref, buf, sems):
    _, blocks, rows, _ = raw_ref.shape
    parts = sems.shape[0]
    per = blocks // parts
    copies = [
        pltpu.make_async_copy(raw_ref.at[:, pl.ds(i * per, per)], buf.at[:, pl.ds(i * per, per)], sems.at[i])
        for i in range(parts)
    ]
    for c in copies:
        c.start()
    even = (me_ref[0] & 1) == 0

    far_ref[HALO * blocks] = jnp.where(even, kap_ref[:SUB, :], kap_ref[rows - SUB :, :])
    near_ref[HALO * blocks] = jnp.where(even, kap_ref[rows - SUB :, :], kap_ref[:SUB, :])

    def body(at):
        for tile in range(rows // SUB):
            flat = turn([buf[s, at, tile * SUB : (tile + 1) * SUB, :] for s in range(SUB)])
            tops, bottoms = [], []
            for i, part in enumerate(flat):
                row = tile * SUB + i
                if row < HALO:
                    tops.append((row, part))
                elif row < 2 * HALO:
                    inner_ref[(row - HALO) * blocks + at] = part
                elif row < rows - 2 * HALO:
                    mid_ref[(row - 2 * HALO) * blocks + at] = part
                elif row < rows - HALO:
                    inner_ref[(row - rows + 3 * HALO) * blocks + at] = part
                else:
                    bottoms.append((row - rows + HALO, part))
            for is_top, group in ((True, tops), (False, bottoms)):
                if group:

                    @pl.when(even == is_top)
                    def _(group=group):
                        for row, value in group:
                            far_ref[row * blocks + at] = value

                    @pl.when(even != is_top)
                    def _(group=group):
                        for row, value in group:
                            near_ref[row * blocks + at] = value

    for i in range(parts):
        copies[i].wait()

        @pl.loop(i * per, (i + 1) * per)
        def _(at):
            body(at)


def pieces(raw, kappa, me):
    levels, rows, width = raw.shape
    blocks = levels // SUB
    middle = rows - 4 * HALO
    counts = [middle * blocks, 2 * HALO * blocks, HALO * blocks + 1, HALO * blocks + 1]
    return pl.pallas_call(
        pieces_kernel,
        name="pieces",
        in_specs=[SM, pl.BlockSpec(memory_space=pltpu.HBM), VM],
        out_specs=[VM] * 4,
        out_shape=[jax.ShapeDtypeStruct((n, SUB, width), F32) for n in counts],
        scratch_shapes=[pltpu.VMEM((SUB, blocks, rows, width), F32), pltpu.SemaphoreType.DMA((blocks // 2,))],
        compiler_params=params(20),
        cost_estimate=cost(0, 8 * raw.size),
    )(me, raw.reshape(SUB, blocks, rows, width), kappa)


def steps_kernel(plans, firsts, halos, me_ref, inside_ref, hw_ref, kap_ref, *rest):
    extra = 1 if halos else 0
    sources = rest[: len(rest) - 6 - 2 * extra]
    out_ref, ping, pong, kap, keep, sems = rest[len(sources) : len(sources) + 6]
    window, _, _, width = ping.shape
    blocks = ping.shape[1] - 2
    own = window - HALO
    seg = pl.program_id(0)
    even = (me_ref[0] & 1) == 0

    def copies(plan):
        return [
            pltpu.make_async_copy(
                sources[k].at[pl.ds(row * blocks, blocks)], ping.at[to, pl.ds(1, blocks)], sems.at[to]
            )
            for k, row, to in plan
        ]

    def edge_copy(k):
        return pltpu.make_async_copy(sources[k].at[HALO * blocks], rest[-2], rest[-1])

    for (g, parity), (plan, halo) in plans.items():
        here = seg == g if parity is None else (seg == g) & (even == (parity == 0))

        @pl.when(here)
        def _(plan=plan, halo=halo):
            for c in copies(plan):
                c.start()
            if halos:
                edge_copy(halo).start()
                edge_copy(halo).wait()

    def set_rows(r, row):
        row = jnp.broadcast_to(row, (SUB, width))
        kap[r] = row
        keep[r] = (1.0 - 2.0 * VMIX) - 4.0 * row

    first = firsts[0] if len(firsts) == 1 else jnp.where(seg == 0, firsts[0], firsts[1])
    if halos:
        at = jnp.where(seg == 0, HALO, 0)
        for r in range(own):
            set_rows(at + r, kap_ref[pl.ds(first + at + r, 1), :])
        edge_at, skip = jnp.where(seg == 0, 0, own), jnp.where(seg == 0, SUB - HALO, 0)
        for r in range(HALO):
            set_rows(edge_at + r, rest[-2][pl.ds(skip + r, 1), :])
    else:
        for r in range(window):
            set_rows(r, kap_ref[pl.ds(first + r, 1), :])
    sub = iota((SUB, width), 0)
    for (g, parity), (plan, _) in plans.items():
        here = seg == g if parity is None else (seg == g) & (even == (parity == 0))

        @pl.when(here)
        def _(plan=plan):
            for c in copies(plan):
                c.wait()

    def ghosts(ref, r, first_block, last_block):
        ref[r, 0] = jnp.where(sub == 0, 0.0, pltpu.roll(last_block, 1, axis=0))
        ref[r, blocks + 1] = jnp.where(sub == SUB - 1, 0.0, pltpu.roll(first_block, SUB - 1, axis=0))

    def ready(r, _):
        ghosts(ping, r, ping[r, 1], ping[r, blocks])
        return 0

    lax.fori_loop(0, window, ready, 0)

    tiles = width // LANES
    lane = iota((SUB, LANES), 1)
    at_start, at_end = lane == 0, lane == LANES - 1

    def advance(src, dst, r, factor, final):
        def load(row, i):
            return [src[row, i, :, k * LANES : (k + 1) * LANES] for k in range(tiles)]

        before, center = load(r, 0), load(r, 1)
        head = tail = None
        for i in range(1, blocks + 1):
            after, up, down = load(r, i + 1), load(r + 1, i), load(r - 1, i)
            wind = hw_ref[i - 1]
            to_right = [pltpu.roll(c, 1, axis=1) for c in center]
            to_left = [pltpu.roll(c, LANES - 1, axis=1) for c in center]
            new = []
            for k in range(tiles):
                west = jnp.where(at_start, to_right[k - 1], to_right[k])
                east = jnp.where(at_end, to_left[(k + 1) % tiles], to_left[k])
                cols = slice(k * LANES, (k + 1) * LANES)
                value = (
                    keep[r, :, cols] * center[k]
                    + kap[r, :, cols] * ((east + west) + (up[k] + down[k]))
                    + (VMIX * (before[k] + after[k]) + wind * (down[k] - up[k]))
                )
                new.append(value if factor is None else value * factor)
            for k in range(tiles):
                cols = slice(k * LANES, (k + 1) * LANES)
                if final:
                    out_ref[r - HALO, i - 1, :, cols] = new[k]
                else:
                    dst[r, i, :, cols] = new[k]
            head = jnp.concatenate(new, axis=1) if i == 1 else head
            if i == blocks:
                tail = jnp.concatenate(new, axis=1)
            before, center = center, after
        if not final:
            ghosts(dst, r, head, tail)

    refs = (ping, pong)
    for step in range(STEPS):
        src, dst = refs[step % 2], refs[(step + 1) % 2]
        final = step == STEPS - 1
        low, high = step + 1, window - 1 - step

        def body(r, _, src=src, dst=dst, final=final):
            advance(src, dst, r, None, final)
            return 0

        if halos and not final:
            inside = inside_ref[seg]

            def masked(r, _, src=src, dst=dst):
                advance(src, dst, r, inside, False)
                return 0

            up_side = seg == 0
            lax.fori_loop(jnp.where(up_side, low, own), jnp.where(up_side, HALO, high), masked, 0)
            lax.fori_loop(jnp.where(up_side, HALO, low), jnp.where(up_side, high, own), body, 0)
        else:
            lax.fori_loop(low, high, body, 0)


def steps(firsts, count, me, inside, half_wind, kappa, sources, halo_sources=None):
    rows, width = kappa.shape
    blocks = half_wind.shape[0]
    window = count + 2 * HALO
    halos = halo_sources is not None
    arrays = [*sources, *(halo_sources or [])]

    def locate(row, parity):
        if row < 0:
            return (4 if parity == 0 else 5), row + HALO
        if row >= rows:
            return (5 if parity == 0 else 4), row - rows
        if row < HALO:
            return (2 if parity == 0 else 3), row
        if row >= rows - HALO:
            return (3 if parity == 0 else 2), row - rows + HALO
        if row < 2 * HALO:
            return 1, row - HALO
        if row >= rows - 2 * HALO:
            return 1, row - rows + 3 * HALO
        return 0, row - 2 * HALO

    plans = {}
    for g, f in enumerate(firsts):
        for parity in (0, 1):
            plan = [(*locate(f - HALO + r, parity), r) for r in range(window)]
            plans[g, parity] = (plan, (4 if (g == 0) == (parity == 0) else 5))
    used = sorted({k for plan, _ in plans.values() for k, _, _ in plan})
    plans = {
        key: ([(used.index(k), row, to) for k, row, to in plan], used.index(halo) if halos else None)
        for key, (plan, halo) in plans.items()
    }
    n = len(firsts)
    updates = n * sum(window - 2 - 2 * s for s in range(STEPS)) * blocks * SUB * width
    extra = [pltpu.VMEM((SUB, width), F32), pltpu.SemaphoreType.DMA] if halos else []
    return pl.pallas_call(
        functools.partial(steps_kernel, plans, [f - HALO for f in firsts], halos),
        grid=(n,),
        in_specs=[SM, SM, VM, VM] + [ANY] * len(used),
        out_specs=pl.BlockSpec((count, blocks, SUB, width), lambda i: (i, 0, 0, 0)),
        out_shape=jax.ShapeDtypeStruct((n * count, blocks, SUB, width), F32),
        scratch_shapes=[
            pltpu.VMEM((window, blocks + 2, SUB, width), F32),
            pltpu.VMEM((window, blocks + 2, SUB, width), F32),
            pltpu.VMEM((window, SUB, width), F32),
            pltpu.VMEM((window, SUB, width), F32),
            pltpu.SemaphoreType.DMA((window,)),
            *extra,
        ],
        compiler_params=params(24),
        cost_estimate=cost(14 * updates, 4 * n * (window + count) * blocks * SUB * width),
    )(me, inside, half_wind, kappa, *[arrays[k] for k in used])


def split(x):
    hi = x.astype(BF16)
    lo = (x - hi.astype(F32)).astype(BF16)
    return hi, lo


def mm(a, b):
    return jnp.dot(a, b, preferred_element_type=F32)


def one_hot(match):
    return match.astype(F32).astype(BF16)


def order_kernel(chunks, devices, me_ref, vert_ref, row_ref, level_ref, *outs):
    levels, rows = vert_ref.shape[0], row_ref.shape[0]
    me = me_ref[0]
    own = levels // devices
    blocks = levels // SUB
    here = rows // devices
    at = iota((levels, levels), 0)
    partner = sum((at >= s * own).astype(jnp.int32) for s in range(1, devices))
    left = one_hot(iota((levels, levels), 1) == (partner ^ me) * own + (at - partner * own))
    at = iota((levels, levels), 1)
    block, sub = at >> (SUB.bit_length() - 1), at & (SUB - 1)
    right = one_hot(iota((levels, levels), 0) == sub * blocks + block)
    level_ref[...] = mm(mm(left, vert_ref[...]).astype(BF16), right).astype(BF16)
    for segments, ref in zip(chunks, outs):
        count = sum(n for _, n in segments)
        at = iota((rows, 2 * count * devices), 1)
        at = jnp.where(at >= count * devices, at - count * devices, at)
        partner = sum((at >= s * count).astype(jnp.int32) for s in range(1, devices))
        within = at - partner * count
        source = within + segments[0][0]
        base = 0
        for (first, n), (after, _) in zip(segments, segments[1:]):
            base += n
            source = source + jnp.where(within >= base, after - first - n, 0)
        pick = one_hot(iota((rows, 2 * count * devices), 0) == (partner ^ me) * here + source)
        ref[...] = mm(row_ref[...], pick).astype(BF16)


def ordered(chunks, devices, me, vert, row):
    levels, rows = vert.shape[0], row.shape[0]
    widths = [2 * devices * sum(n for _, n in segments) for segments in chunks]
    return pl.pallas_call(
        functools.partial(order_kernel, chunks, devices),
        name="ordered",
        in_specs=[SM, VM, VM],
        out_specs=[VM] * (1 + len(chunks)),
        out_shape=[jax.ShapeDtypeStruct((levels, levels), BF16)]
        + [jax.ShapeDtypeStruct((rows, w), BF16) for w in widths],
        compiler_params=params(16),
        cost_estimate=cost(2 * rows * rows * rows, 4 * rows * rows),
    )(me, vert, row)


def levels_kernel(edges, with_columns, me_ref, ev_ref, mat_ref, *rest):
    fo_refs, rest = rest[: 2 if edges else 1], rest[2 if edges else 1 :]
    col_ref, outs = (rest[0], rest[1:]) if with_columns else (None, rest)
    per, blocks, sub, width = ev_ref.shape
    own = outs[0].shape[1]
    late = (pl.program_id(0) >= pl.num_programs(0) // 2).astype(jnp.int32)
    near = late != (me_ref[0] & 1)
    mat = mat_ref[...]
    for r in range(per):
        following = fo_refs[0][r * blocks : (r + 1) * blocks]
        if edges:
            following = jnp.where(near, fo_refs[1][r * blocks : (r + 1) * blocks], following)
        hi, lo = split((ev_ref[r] - following).reshape(blocks * sub, width))
        mixed = mm(mat, hi) + mm(mat, lo)
        if with_columns:
            hi, lo = split(mixed)
            mixed = mm(hi, col_ref[...]) + mm(lo, col_ref[...])
        for s, ref in enumerate(outs):
            ref[r] = mixed[s * own : (s + 1) * own]


def mix_levels(count, me, evolved, following, mat, col=None):
    rows, blocks, sub, width = evolved.shape
    levels = blocks * sub
    own = levels // count
    per = 2
    edges = len(following) == 2
    half = rows // (2 * per)
    spec = pl.BlockSpec((per * blocks, sub, width), lambda i: (lax.rem(i, half) if edges else i, 0, 0))
    cols = [] if col is None else [col]
    return pl.pallas_call(
        functools.partial(levels_kernel, edges, col is not None),
        name="mix_levels",
        grid=(rows // per,),
        in_specs=[
            SM,
            pl.BlockSpec((per, blocks, sub, width), lambda i: (i, 0, 0, 0)),
            pl.BlockSpec(mat.shape, lambda i: (0, 0)),
        ]
        + [spec] * len(following)
        + [pl.BlockSpec(c.shape, lambda i: (0, 0)) for c in cols],
        out_specs=[pl.BlockSpec((per, own, width), lambda i: (i, 0, 0))] * count,
        out_shape=[jax.ShapeDtypeStruct((rows, own, width), F32)] * count,
        compiler_params=params(16),
        cost_estimate=cost(4 * levels * levels * rows * width, 12 * evolved.size),
    )(me, evolved, mat, *following, *cols)


def by_level(x):
    groups = [turn([x[g + i] for i in range(SUB)]) for g in range(0, x.shape[0], SUB)]
    return [jnp.concatenate([g[z] for g in groups], axis=0) for z in range(SUB)]


def stacked(x):
    return jnp.concatenate(split(x), axis=0)


def rows_kernel(counts, col_ref, *rest):
    mats, xs, out_ref = rest[: len(counts)], rest[len(counts) : -1], rest[-1]
    width = out_ref.shape[2]
    totals = [None] * SUB
    start = 0
    for mat_ref, count in zip(mats, counts):
        x = jnp.concatenate([ref[...] for ref in xs[start : start + count]], axis=0)
        start += count
        depth = x.shape[0]
        hi, lo = split(x.reshape(depth * SUB, width))
        mixed = (mm(hi, col_ref[...]) + mm(lo, col_ref[...])).reshape(depth, SUB, width)
        for z, level in enumerate(by_level(mixed)):
            part = mm(mat_ref[...], stacked(level))
            totals[z] = part if totals[z] is None else totals[z] + part
    for z in range(SUB):
        out_ref[z] = totals[z]


def mix_rows(col, mats, groups):
    blocks = [x for group in groups for x in group]
    own, width = blocks[0].shape[1:]
    rows = mats[0].shape[0]
    depth = sum(x.shape[0] for x in blocks)
    return pl.pallas_call(
        functools.partial(rows_kernel, [len(g) for g in groups]),
        name="mix_rows",
        grid=(own // SUB,),
        in_specs=[pl.BlockSpec(m.shape, lambda i: (0, 0)) for m in [col, *mats]]
        + [pl.BlockSpec((x.shape[0], SUB, width), lambda i: (0, i, 0)) for x in blocks],
        out_specs=pl.BlockSpec((SUB, rows, width), lambda i: (i, 0, 0)),
        out_shape=jax.ShapeDtypeStruct((own, rows, width), F32),
        compiler_params=params(36),
        cost_estimate=cost(4 * own * depth * width * (width + rows), 4 * own * width * (depth + rows)),
    )(col, *mats, *blocks)


def finish_kernel(count, mat_ref, base_ref, *rest):
    out_ref = rest[-1]
    x = jnp.concatenate([ref[...] for ref in rest[:count]], axis=0)
    for z, level in enumerate(by_level(x)):
        out_ref[z] = base_ref[z] + mm(mat_ref[...], stacked(level))


def finish(part, mat, base, blocks, out=None):
    _, rows, width = base.shape
    cols = LANES
    spec = pl.BlockSpec((SUB, rows, cols), lambda j: (part, 0, j))
    rest = [] if out is None else [out]
    depth = sum(x.shape[0] for x in blocks)
    return pl.pallas_call(
        functools.partial(finish_kernel, len(blocks)),
        name="finish",
        grid=(width // cols,),
        in_specs=[pl.BlockSpec(mat.shape, lambda j: (0, 0)), spec]
        + [pl.BlockSpec((x.shape[0], SUB, cols), lambda j: (0, 0, j)) for x in blocks]
        + [ANY] * len(rest),
        out_specs=spec,
        out_shape=jax.ShapeDtypeStruct(base.shape, F32),
        input_output_aliases={2 + len(blocks): 0} if rest else {},
        compiler_params=params(16),
        cost_estimate=cost(4 * SUB * depth * rows * width, 4 * SUB * width * (depth + 2 * rows)),
    )(mat, base, *blocks, *rest)


def tiled_body(increment, diffusivity, wind, vertical_cov, row_cov, column_cov):
    raw, kappa = increment[0], diffusivity[0]
    devices, windows = lax.axis_size("tile"), lax.axis_size("win")
    levels, rows, _ = raw.shape
    blocks = levels // SUB
    me = lax.axis_index("tile").astype(jnp.int32)
    half_wind = jnp.broadcast_to((0.5 * wind[0]).reshape(SUB, blocks).T[:, :, None], (blocks, SUB, LANES))
    inside = jnp.stack([me != 0, me != devices - 1]).astype(F32)
    middle = rows - 4 * HALO
    chunks = (
        ((2 * HALO, middle),),
        ((HALO, HALO), (rows - 2 * HALO, HALO)),
        ((0, HALO), (rows - HALO, HALO)),
    )
    one = me.reshape(1)
    mids, inner, far, near = pieces(raw, kappa, one)

    def earlier(x):
        return lax.ppermute(x, "win", [(i + 1, i) for i in range(windows - 1)])

    apart = [(t, t + 1) for t in range(1, devices - 1, 2)] + [(t + 1, t) for t in range(1, devices - 1, 2)]
    far_in = lax.ppermute(far, "tile", apart)
    follow_mids = earlier(mids)
    near_in = lax.ppermute(near, "tile", [(t, t ^ 1) for t in range(devices)])
    level_mat, *row_mats = ordered(chunks, devices, one, vertical_cov, row_cov)

    def exchange(parts):
        got = {}
        for s in sorted(range(1, devices), key=lambda s: (-(s.bit_length()), s)):
            got[s] = lax.ppermute(parts[s], "tile", [(t, t ^ s) for t in range(devices)])
        return [parts[0]] + [got[s] for s in range(1, devices)]

    own = [mids, inner, far, near]
    ev = steps([2 * HALO], middle, one, inside, half_wind, kappa, own)
    mixed = mix_levels(devices, one, ev, [follow_mids], level_mat)
    first = exchange(mixed)

    *own, _ = lax.optimization_barrier((mids, inner, far, near, mixed[0]))
    follow_inner, follow_far, follow_near = earlier(own[1]), earlier(own[2]), earlier(own[3])
    ev = steps([HALO, rows - 2 * HALO], HALO, one, inside, half_wind, kappa, own)
    mixed = mix_levels(devices, one, ev, [follow_inner], level_mat)
    second = exchange(mixed)

    *own, _ = lax.optimization_barrier((*own, mixed[0]))
    ev = steps([0, rows - HALO], HALO, one, inside, half_wind, kappa, own, [far_in, near_in])
    halves = levels // devices // SUB
    mixed = mix_levels(devices * halves, one, ev, [follow_far, follow_near], level_mat, column_cov)
    base = mix_rows(column_cov, row_mats[:2], [first, second])
    out = None
    for h in range(halves):
        last = exchange(mixed[h::halves])
        out = finish(h, row_mats[2], base, last, out)
    return out[None]


def with_halo(cells, sides, width):
    for axis, dim in sides:
        count = lax.axis_size(axis)
        ends = count - 1
        head = lax.slice_in_dim(cells, 0, width, axis=dim)
        tail = lax.slice_in_dim(cells, cells.shape[dim] - width, cells.shape[dim], axis=dim)
        cells = jnp.concatenate(
            [
                lax.ppermute(tail, axis, [(i, (i + 1) % count) for i in range(ends)]),
                cells,
                lax.ppermute(head, axis, [((i + 1) % count, i) for i in range(ends)]),
            ],
            axis=dim,
        )
    return cells


def tendency(center, north, south, kappa, wind_col):
    east = jnp.roll(center, -1, axis=2)
    west = jnp.roll(center, 1, axis=2)
    stacked = jnp.pad(center, ((1, 1), (0, 0), (0, 0)))
    horiz = north + south + east + west - 4.0 * center
    vert = stacked[2:] + stacked[:-2] - 2.0 * center
    return center + kappa[None] * horiz + VMIX * vert + wind_col * (0.5 * (south - north))


def plain_body(increment, diffusivity, wind, vertical_cov, row_cov, column_cov):
    field, kappa, wind_col = increment[0], diffusivity[0], wind[0][:, None, None]
    current = field
    for _ in range(STEPS):
        padded = with_halo(current, (("tile", 1),), 1)
        current = tendency(current, padded[:, 2:], padded[:, :-2], kappa, wind_col)
    size = lax.axis_size("win")
    defect = current - lax.ppermute(field, "win", [(i + 1, i) for i in range(size - 1)])
    levels, rows, width = defect.shape
    high = lax.Precision.HIGHEST
    mixed = jnp.dot(vertical_cov.astype(F32), defect.reshape(levels, rows * width), precision=high)
    mixed = jnp.dot(mixed.reshape(levels * rows, width), column_cov.astype(F32), precision=high)
    mixed = lax.all_to_all(mixed.reshape(levels, rows, width), "tile", split_axis=0, concat_axis=1, tiled=True)
    return jnp.einsum("yk,zkx->zyx", row_cov.astype(F32), mixed, precision=high)[None]


def body(*args):
    levels, rows, width = args[0].shape[1:]
    devices = lax.axis_size("tile")
    own = levels // devices
    fits = (
        rows > 4 * HALO
        and rows % SUB == 0
        and levels % (2 * SUB) == 0
        and levels % devices == 0
        and own % SUB == 0
        and width % LANES == 0
        and devices & (devices - 1) == 0
        and devices % SUB == 0
    )
    return tiled_body(*args) if fits else plain_body(*args)


def solution(mesh):
    in_specs = (P("win", None, "tile", None), P("win", "tile", None), P("win", None), P(), P(), P())
    out_specs = P("win", "tile", None, None)
    return jax.shard_map(body, mesh=mesh, in_specs=in_specs, out_specs=out_specs, check_vma=False)
```

profile of v0, /device:TPU:10, one launch (start us, length us, event | category | flops | bytes accessed | tf_op | source)
XLA Modules:
  0.0 349.3 jit_solution(17510645945618259813)
XLA Ops:
  0.0 3.4 copy-done
  4.2 3.9 %pieces.1 = (f32[128,8,512]{2,1,0:T(8,128)}, f32[192,8,512]{2,1,0:T(8,128)S(1)}, f32[97,8,512]{2,1,0:T(8,128)S(1)}, f32[97,8,512]{2,1,0:T(8,128)S(1)}) custom-call(s32[1]{0:T(128)} %bitcast.me_ref, f32[8,16,32,512]{3,2,1,0:T(8,128)S(1)} %bitcast.7, f32[32,512]{1,0:T(8,128)S(1)} %bitcast.8), custom_call_target="tpu_custom_call" | custom-call | bytes 16777216 | tf_op jit(solution)/shard_map/pieces/pallas_call | solution.py:107
  13.2 19.0 %shard_map.64.ev_ref = f32[8,16,8,512]{3,2,1,0:T(8,128)S(1)} custom-call(s32[1]{0:T(128)} %bitcast.me_ref, f32[2]{0:T(128)S(1)} %add_convert_fusion.inside_ref, f32[16,8,128]{2,1,0:T(8,128)S(1)} %broadcast_in_dim.4.hw_ref, f32[32,512]{1,0:T(8,128)S(1)} %bitcast.9, f32[128,8,512]{2,1,0:T(8,128)} %get-tuple-element.68.rest_0_, ...), custom_call_target="tpu_custom_call" | custom-call | flops 71565312 | bytes 7340032 | tf_op jit(solution)/shard_map/pallas_call | solution.py:284
  32.2 4.1 %collective-permute-done.rest_0_ = f32[128,8,512]{2,1,0:T(8,128)} collective-permute-done((f32[128,8,512]{2,1,0:T(8,128)}, f32[128,8,512]{2,1,0:T(8,128)}, u32[]{:S(2)}, u32[]{:S(2)}) %collective-permute-start) | collective-permute-done | bytes 2097184 | tf_op jit(solution)/shard_map/ppermute | solution.py:499
  36.3 3.3 mix_levels.3
  39.6 3.8 %collective-permute-start.8 = (f32[192,8,512]{2,1,0:T(8,128)S(1)}, f32[192,8,512]{2,1,0:T(8,128)S(1)}, u32[]{:S(2)}, u32[]{:S(2)}) collective-permute-start(f32[192,8,512]{2,1,0:T(8,128)S(1)} %get-tuple-element.80.rest_1_.rest_0_), channel_id=1, source_target_pairs={{8,0},{16,8},{24,16},{9,1},{17,9},{25,17},{10,2},{18,10},{26,18},{... | collective-permute-start | bytes 9437192 | tf_op jit(solution)/shard_map/ppermute | solution.py:499
  43.5 3.3 collective-permute-start.16
  52.3 29.5 %collective-permute-done.16.rest_3_ = f32[97,8,512]{2,1,0:T(8,128)S(1)} collective-permute-done((f32[97,8,512]{2,1,0:T(8,128)S(1)}, f32[97,8,512]{2,1,0:T(8,128)S(1)}, u32[]{:S(2)}, u32[]{:S(2)}) %collective-permute-start.16) | collective-permute-done | bytes 1589280 | tf_op jit(solution)/shard_map/ppermute | solution.py:502
  83.3 32.5 %collective-permute-done.17.rest_4_ = f32[97,8,512]{2,1,0:T(8,128)S(1)} collective-permute-done((f32[97,8,512]{2,1,0:T(8,128)S(1)}, f32[97,8,512]{2,1,0:T(8,128)S(1)}, u32[]{:S(2)}, u32[]{:S(2)}) %collective-permute-start.17) | collective-permute-done | bytes 1589280 | tf_op jit(solution)/shard_map/ppermute | solution.py:504
  115.8 5.5 %collective-permute-done.1.rest_3_ = f32[8,16,512]{2,1,0:T(8,128)S(1)} collective-permute-done((f32[8,16,512]{2,1,0:T(8,128)S(1)}, f32[8,16,512]{2,1,0:T(8,128)S(1)}, u32[]{:S(2)}, u32[]{:S(2)}) %collective-permute-start.1) | collective-permute-done | bytes 262176 | tf_op jit(solution)/shard_map/ppermute | solution.py:510
  124.0 3.6 %collective-permute-start.4 = (f32[8,16,512]{2,1,0:T(8,128)S(1)}, f32[8,16,512]{2,1,0:T(8,128)S(1)}, u32[]{:S(2)}, u32[]{:S(2)}) collective-permute-start(f32[8,16,512]{2,1,0:T(8,128)S(1)} %get-tuple-element.62), channel_id=1, source_target_pairs={{0,4},{1,5},{2,6},{3,7},{4,0},{5,1},{6,2},{7,3},{8,12},{9,13},{10,... | collective-permute-start | bytes 786440 | tf_op jit(solution)/shard_map/ppermute | solution.py:510
  127.9 31.8 %shard_map.65.ev_ref = f32[12,16,8,512]{3,2,1,0:T(8,128)S(1)} custom-call(s32[1]{0:T(128)} %bitcast.me_ref, f32[2]{0:T(128)S(1)} %add_convert_fusion.inside_ref, f32[16,8,128]{2,1,0:T(8,128)S(1)} %broadcast_in_dim.4.hw_ref, f32[32,512]{1,0:T(8,128)S(1)} %bitcast.10, f32[128,8,512]{2,1,0:T(8,128)} %get-tuple-element.68.rest_0_, ...), custom_call_target="tpu_custom_call" | custom-call | flops 121110528 | bytes 12582912 | tf_op jit(solution)/shard_map/pallas_call | solution.py:284
  164.3 29.9 %shard_map.66.ev_ref = f32[12,16,8,512]{3,2,1,0:T(8,128)S(1)} custom-call(s32[1]{0:T(128)} %bitcast.me_ref, f32[2]{0:T(128)S(1)} %add_convert_fusion.inside_ref, f32[16,8,128]{2,1,0:T(8,128)S(1)} %broadcast_in_dim.4.hw_ref, f32[32,512]{1,0:T(8,128)S(1)} %bitcast.11, f32[192,8,512]{2,1,0:T(8,128)S(1)} %get-tuple-element.80.rest_1_.rest_0_, ...), custom_call_target="tpu_custom_call" | custom-call | flops 121110528 | bytes 12582912 | tf_op jit(solution)/shard_map/pallas_call | solution.py:284
  194.3 5.1 %mix_levels.5 = (f32[12,8,512]{2,1,0:T(8,128)S(1)}, f32[12,8,512]{2,1,0:T(8,128)S(1)}, f32[12,8,512]{2,1,0:T(8,128)S(1)}, f32[12,8,512]{2,1,0:T(8,128)S(1)}, f32...) custom-call(s32[1]{0:T(128)} %bitcast.me_ref, ...), custom_call_target="tpu_custom_call" | custom-call | flops 402653184 | bytes 9437184 | tf_op jit(solution)/shard_map/mix_levels/pallas_call | solution.py:390
  206.8 5.3 %collective-permute-start.30 = (f32[12,8,512]{2,1,0:T(8,128)S(1)}, f32[12,8,512]{2,1,0:T(8,128)S(1)}, u32[]{:S(2)}, u32[]{:S(2)}) collective-permute-start(f32[12,8,512]{2,1,0:T(8,128)S(1)} %get-tuple-element.95), channel_id=1, source_target_pairs={{0,4},{1,5},{2,6},{3,7},{4,0},{5,1},{6,2},{7,3},{8,12},{9,13},{10,... | collective-permute-start | bytes 589832 | tf_op jit(solution)/shard_map/ppermute | solution.py:510
  215.4 3.2 collective-permute-done.28.rest_2_
  218.6 5.4 %collective-permute-start.31 = (f32[12,8,512]{2,1,0:T(8,128)S(1)}, f32[12,8,512]{2,1,0:T(8,128)S(1)}, u32[]{:S(2)}, u32[]{:S(2)}) collective-permute-start(f32[12,8,512]{2,1,0:T(8,128)S(1)} %get-tuple-element.96), channel_id=1, source_target_pairs={{0,5},{1,4},{2,7},{3,6},{4,1},{5,0},{6,3},{7,2},{8,13},{9,12},{10,... | collective-permute-start | bytes 589832 | tf_op jit(solution)/shard_map/ppermute | solution.py:510
  226.4 10.4 %collective-permute-done.31.rest_5_ = f32[12,8,512]{2,1,0:T(8,128)S(1)} collective-permute-done((f32[12,8,512]{2,1,0:T(8,128)S(1)}, f32[12,8,512]{2,1,0:T(8,128)S(1)}, u32[]{:S(2)}, u32[]{:S(2)}) %collective-permute-start.31) | collective-permute-done | bytes 196640 | tf_op jit(solution)/shard_map/ppermute | solution.py:510
  236.8 6.4 %collective-permute-done.32.rest_6_ = f32[12,8,512]{2,1,0:T(8,128)S(1)} collective-permute-done((f32[12,8,512]{2,1,0:T(8,128)S(1)}, f32[12,8,512]{2,1,0:T(8,128)S(1)}, u32[]{:S(2)}, u32[]{:S(2)}) %collective-permute-start.32) | collective-permute-done | bytes 196640 | tf_op jit(solution)/shard_map/ppermute | solution.py:510
  243.2 25.1 %collective-permute-done.33.rest_7_ = f32[12,8,512]{2,1,0:T(8,128)S(1)} collective-permute-done((f32[12,8,512]{2,1,0:T(8,128)S(1)}, f32[12,8,512]{2,1,0:T(8,128)S(1)}, u32[]{:S(2)}, u32[]{:S(2)}) %collective-permute-start.33) | collective-permute-done | bytes 196640 | tf_op jit(solution)/shard_map/ppermute | solution.py:510
  268.3 3.6 %collective-permute-start.15 = (f32[12,16,512]{2,1,0:T(8,128)S(1)}, f32[12,16,512]{2,1,0:T(8,128)S(1)}, u32[]{:S(2)}, u32[]{:S(2)}) collective-permute-start(f32[12,16,512]{2,1,0:T(8,128)S(1)} %get-tuple-element.79), channel_id=1, source_target_pairs={{0,7},{1,6},{2,5},{3,4},{4,3},{5,2},{6,1},{7,0},{8,15},{9,14},{10,... | collective-permute-start | bytes 1179656 | tf_op jit(solution)/shard_map/ppermute | solution.py:510
  271.9 6.1 %collective-permute-start.22 = (f32[12,8,512]{2,1,0:T(8,128)S(1)}, f32[12,8,512]{2,1,0:T(8,128)S(1)}, u32[]{:S(2)}, u32[]{:S(2)}) collective-permute-start(f32[12,8,512]{2,1,0:T(8,128)S(1)} %get-tuple-element.86), channel_id=1, source_target_pairs={{0,3},{1,2},{2,1},{3,0},{4,7},{5,6},{6,5},{7,4},{8,11},{9,10},{10,... | collective-permute-start | bytes 589832 | tf_op jit(solution)/shard_map/ppermute | solution.py:510
  278.0 13.6 %collective-permute-done.12.rest_14_ = f32[12,16,512]{2,1,0:T(8,128)S(1)} collective-permute-done((f32[12,16,512]{2,1,0:T(8,128)S(1)}, f32[12,16,512]{2,1,0:T(8,128)S(1)}, u32[]{:S(2)}, u32[]{:S(2)}) %collective-permute-start.12) | collective-permute-done | bytes 393248 | tf_op jit(solution)/shard_map/ppermute | solution.py:510
  291.6 3.4 collective-permute-start.23
  295.0 13.5 %collective-permute-done.13.rest_15_ = f32[12,16,512]{2,1,0:T(8,128)S(1)} collective-permute-done((f32[12,16,512]{2,1,0:T(8,128)S(1)}, f32[12,16,512]{2,1,0:T(8,128)S(1)}, u32[]{:S(2)}, u32[]{:S(2)}) %collective-permute-start.13) | collective-permute-done | bytes 393248 | tf_op jit(solution)/shard_map/ppermute | solution.py:510
  308.5 4.3 %collective-permute-start.24 = (f32[12,8,512]{2,1,0:T(8,128)S(1)}, f32[12,8,512]{2,1,0:T(8,128)S(1)}, u32[]{:S(2)}, u32[]{:S(2)}) collective-permute-start(f32[12,8,512]{2,1,0:T(8,128)S(1)} %get-tuple-element.88), channel_id=1, source_target_pairs={{0,5},{1,4},{2,7},{3,6},{4,1},{5,0},{6,3},{7,2},{8,13},{9,12},{10,... | collective-permute-start | bytes 589832 | tf_op jit(solution)/shard_map/ppermute | solution.py:510
  312.8 10.5 %collective-permute-done.14.rest_16_ = f32[12,16,512]{2,1,0:T(8,128)S(1)} collective-permute-done((f32[12,16,512]{2,1,0:T(8,128)S(1)}, f32[12,16,512]{2,1,0:T(8,128)S(1)}, u32[]{:S(2)}, u32[]{:S(2)}) %collective-permute-start.14) | collective-permute-done | bytes 393248 | tf_op jit(solution)/shard_map/ppermute | solution.py:510
  325.7 5.9 %collective-permute-done.15.rest_17_ = f32[12,16,512]{2,1,0:T(8,128)S(1)} collective-permute-done((f32[12,16,512]{2,1,0:T(8,128)S(1)}, f32[12,16,512]{2,1,0:T(8,128)S(1)}, u32[]{:S(2)}, u32[]{:S(2)}) %collective-permute-start.15) | collective-permute-done | bytes 393248 | tf_op jit(solution)/shard_map/ppermute | solution.py:510
  331.7 3.4 collective-permute-start.26
  335.0 6.3 %mix_rows.1.base_ref = f32[16,256,512]{2,1,0:T(8,128)S(1)} custom-call(bf16[512,512]{1,0:T(8,128)(2,1)S(1)} %copy-done.7, bf16[256,128]{1,0:T(8,128)(2,1)S(1)} %get-tuple-element.53.rest_0_, bf16[256,192]{1,0:T(8,128)(2,1)S(1)} %get-tuple-element.54.rest_1_, f32[8,16,512]{2,1,0:T(8,128)S(1)} %get-tuple-element.58.rest_2_, ...), custom_call_target="tpu_custom_call" | custom-call | flops 4026531840 | bytes 13631488 | tf_op jit(solution)/shard_map/mix_rows/pallas_call | solution.py:440
  341.3 4.0 %finish.2.rest_8_ = f32[16,256,512]{2,1,0:T(8,128)} custom-call(bf16[256,192]{1,0:T(8,128)(2,1)S(1)} %get-tuple-element.52.mat_ref, f32[16,256,512]{2,1,0:T(8,128)S(1)} %mix_rows.1.base_ref, f32[12,8,512]{2,1,0:T(8,128)S(1)} %get-tuple-element.91.rest_0_, f32[12,8,512]{2,1,0:T(8,128)S(1)} %collective-permute-done.27.rest_1_, ...), custom_call_target="tpu_custom_call" | custom-call | flops 402653184 | bytes 9961472 | tf_op jit(solution)/shard_map/finish/pallas_call | solution.py:466
  345.3 4.0 %finish.3 = f32[16,256,512]{2,1,0:T(8,128)} custom-call(bf16[256,192]{1,0:T(8,128)(2,1)S(1)} %get-tuple-element.52.mat_ref, f32[16,256,512]{2,1,0:T(8,128)S(1)} %mix_rows.1.base_ref, f32[12,8,512]{2,1,0:T(8,128)S(1)} %get-tuple-element.83.rest_0_, f32[12,8,512]{2,1,0:T(8,128)S(1)} %collective-permute-done.20.rest_1_, ...), custom_call_target="tpu_custom_call", output_to_operand_aliasing={{}: (10, {})} | custom-call | flops 402653184 | bytes 9961472 | tf_op jit(solution)/shard_map/finish/pallas_call | solution.py:466
  (74 shorter events, 36.0 us)
Async XLA Ops:
  10.6 25.8 %collective-permute-start = (f32[128,8,512]{2,1,0:T(8,128)}, f32[128,8,512]{2,1,0:T(8,128)}, u32[]{:S(2)}, u32[]{:S(2)}) collective-permute-start(f32[128,8,512]{2,1,0:T(8,128)} %get-tuple-element.68.rest_0_), channel_id=1, source_target_pairs={{8,0},{16,8},{24,16},{9,1},{17,9},{25,17},{10,2},{18,10},{26,18},{... | collective-permute-start | bytes 6291464 | tf_op jit(solution)/shard_map/ppermute | solution.py:499
  39.6 121.8 %collective-permute-start.8 = (f32[192,8,512]{2,1,0:T(8,128)S(1)}, f32[192,8,512]{2,1,0:T(8,128)S(1)}, u32[]{:S(2)}, u32[]{:S(2)}) collective-permute-start(f32[192,8,512]{2,1,0:T(8,128)S(1)} %get-tuple-element.80.rest_1_.rest_0_), channel_id=1, source_target_pairs={{8,0},{16,8},{24,16},{9,1},{17,9},{25,17},{10,2},{18,10},{26,18},{... | collective-permute-start | bytes 9437192 | tf_op jit(solution)/shard_map/ppermute | solution.py:499
  43.5 38.3 %collective-permute-start.16 = (f32[97,8,512]{2,1,0:T(8,128)S(1)}, f32[97,8,512]{2,1,0:T(8,128)S(1)}, u32[]{:S(2)}, u32[]{:S(2)}) collective-permute-start(f32[97,8,512]{2,1,0:T(8,128)S(1)} %copy-done.2), channel_id=1, source_target_pairs={{1,2},{3,4},{5,6},{2,1},{4,3},{6,5},{9,10},{11,12},{13,14},{10,9},... | collective-permute-start | bytes 4767752 | tf_op jit(solution)/shard_map/ppermute | solution.py:502
  46.8 69.1 %collective-permute-start.17 = (f32[97,8,512]{2,1,0:T(8,128)S(1)}, f32[97,8,512]{2,1,0:T(8,128)S(1)}, u32[]{:S(2)}, u32[]{:S(2)}) collective-permute-start(f32[97,8,512]{2,1,0:T(8,128)S(1)} %copy-done.4), channel_id=1, source_target_pairs={{0,1},{1,0},{2,3},{3,2},{4,5},{5,4},{6,7},{7,6},{8,9},{9,8},{10,11... | collective-permute-start | bytes 4767752 | tf_op jit(solution)/shard_map/ppermute | solution.py:504
  48.5 79.1 %collective-permute-start.18 = (f32[97,8,512]{2,1,0:T(8,128)S(1)}, f32[97,8,512]{2,1,0:T(8,128)S(1)}, u32[]{:S(2)}, u32[]{:S(2)}) collective-permute-start(f32[97,8,512]{2,1,0:T(8,128)S(1)} %copy-done.2), channel_id=1, source_target_pairs={{8,0},{16,8},{24,16},{9,1},{17,9},{25,17},{10,2},{18,10},{26,18},{... | collective-permute-start | bytes 4767752 | tf_op jit(solution)/shard_map/ppermute | solution.py:499
  50.4 109.4 %collective-permute-start.19 = (f32[97,8,512]{2,1,0:T(8,128)S(1)}, f32[97,8,512]{2,1,0:T(8,128)S(1)}, u32[]{:S(2)}, u32[]{:S(2)}) collective-permute-start(f32[97,8,512]{2,1,0:T(8,128)S(1)} %copy-done.4), channel_id=1, source_target_pairs={{8,0},{16,8},{24,16},{9,1},{17,9},{25,17},{10,2},{18,10},{26,18},{... | collective-permute-start | bytes 4767752 | tf_op jit(solution)/shard_map/ppermute | solution.py:499
  81.8 39.6 %collective-permute-start.1 = (f32[8,16,512]{2,1,0:T(8,128)S(1)}, f32[8,16,512]{2,1,0:T(8,128)S(1)}, u32[]{:S(2)}, u32[]{:S(2)}) collective-permute-start(f32[8,16,512]{2,1,0:T(8,128)S(1)} %get-tuple-element.59), channel_id=1, source_target_pairs={{0,1},{1,0},{2,3},{3,2},{4,5},{5,4},{6,7},{7,6},{8,9},{9,8},{10,11... | collective-permute-start | bytes 786440 | tf_op jit(solution)/shard_map/ppermute | solution.py:510
  121.4 78.0 %collective-permute-start.3 = (f32[8,16,512]{2,1,0:T(8,128)S(1)}, f32[8,16,512]{2,1,0:T(8,128)S(1)}, u32[]{:S(2)}, u32[]{:S(2)}) collective-permute-start(f32[8,16,512]{2,1,0:T(8,128)S(1)} %get-tuple-element.61), channel_id=1, source_target_pairs={{0,3},{1,2},{2,1},{3,0},{4,7},{5,6},{6,5},{7,4},{8,11},{9,10},{10,... | collective-permute-start | bytes 786440 | tf_op jit(solution)/shard_map/ppermute | solution.py:510
  124.0 76.4 %collective-permute-start.4 = (f32[8,16,512]{2,1,0:T(8,128)S(1)}, f32[8,16,512]{2,1,0:T(8,128)S(1)}, u32[]{:S(2)}, u32[]{:S(2)}) collective-permute-start(f32[8,16,512]{2,1,0:T(8,128)S(1)} %get-tuple-element.62), channel_id=1, source_target_pairs={{0,4},{1,5},{2,6},{3,7},{4,0},{5,1},{6,2},{7,3},{8,12},{9,13},{10,... | collective-permute-start | bytes 786440 | tf_op jit(solution)/shard_map/ppermute | solution.py:510
  127.6 75.1 %collective-permute-start.5 = (f32[8,16,512]{2,1,0:T(8,128)S(1)}, f32[8,16,512]{2,1,0:T(8,128)S(1)}, u32[]{:S(2)}, u32[]{:S(2)}) collective-permute-start(f32[8,16,512]{2,1,0:T(8,128)S(1)} %get-tuple-element.63), channel_id=1, source_target_pairs={{0,5},{1,4},{2,7},{3,6},{4,1},{5,0},{6,3},{7,2},{8,13},{9,12},{10,... | collective-permute-start | bytes 786440 | tf_op jit(solution)/shard_map/ppermute | solution.py:510
  159.8 44.2 %collective-permute-start.6 = (f32[8,16,512]{2,1,0:T(8,128)S(1)}, f32[8,16,512]{2,1,0:T(8,128)S(1)}, u32[]{:S(2)}, u32[]{:S(2)}) collective-permute-start(f32[8,16,512]{2,1,0:T(8,128)S(1)} %get-tuple-element.64), channel_id=1, source_target_pairs={{0,6},{1,7},{2,4},{3,5},{4,2},{5,3},{6,0},{7,1},{8,14},{9,15},{10,... | collective-permute-start | bytes 786440 | tf_op jit(solution)/shard_map/ppermute | solution.py:510
  161.4 42.6 %collective-permute-start.7 = (f32[8,16,512]{2,1,0:T(8,128)S(1)}, f32[8,16,512]{2,1,0:T(8,128)S(1)}, u32[]{:S(2)}, u32[]{:S(2)}) collective-permute-start(f32[8,16,512]{2,1,0:T(8,128)S(1)} %get-tuple-element.65), channel_id=1, source_target_pairs={{0,7},{1,6},{2,5},{3,4},{4,3},{5,2},{6,1},{7,0},{8,15},{9,14},{10,... | collective-permute-start | bytes 786440 | tf_op jit(solution)/shard_map/ppermute | solution.py:510
  200.4 11.7 %collective-permute-start.21 = (f32[12,8,512]{2,1,0:T(8,128)S(1)}, f32[12,8,512]{2,1,0:T(8,128)S(1)}, u32[]{:S(2)}, u32[]{:S(2)}) collective-permute-start(f32[12,8,512]{2,1,0:T(8,128)S(1)} %get-tuple-element.85), channel_id=1, source_target_pairs={{0,2},{1,3},{2,0},{3,1},{4,6},{5,7},{6,4},{7,5},{8,10},{9,11},{10,... | collective-permute-start | bytes 589832 | tf_op jit(solution)/shard_map/ppermute | solution.py:510
  202.7 9.7 %collective-permute-start.27 = (f32[12,8,512]{2,1,0:T(8,128)S(1)}, f32[12,8,512]{2,1,0:T(8,128)S(1)}, u32[]{:S(2)}, u32[]{:S(2)}) collective-permute-start(f32[12,8,512]{2,1,0:T(8,128)S(1)} %get-tuple-element.92), channel_id=1, source_target_pairs={{0,1},{1,0},{2,3},{3,2},{4,5},{5,4},{6,7},{7,6},{8,9},{9,8},{10,11... | collective-permute-start | bytes 589832 | tf_op jit(solution)/shard_map/ppermute | solution.py:510
  204.0 14.6 %collective-permute-start.28 = (f32[12,8,512]{2,1,0:T(8,128)S(1)}, f32[12,8,512]{2,1,0:T(8,128)S(1)}, u32[]{:S(2)}, u32[]{:S(2)}) collective-permute-start(f32[12,8,512]{2,1,0:T(8,128)S(1)} %get-tuple-element.93), channel_id=1, source_target_pairs={{0,2},{1,3},{2,0},{3,1},{4,6},{5,7},{6,4},{7,5},{8,10},{9,11},{10,... | collective-permute-start | bytes 589832 | tf_op jit(solution)/shard_map/ppermute | solution.py:510
  204.0 19.9 %collective-permute-start.29 = (f32[12,8,512]{2,1,0:T(8,128)S(1)}, f32[12,8,512]{2,1,0:T(8,128)S(1)}, u32[]{:S(2)}, u32[]{:S(2)}) collective-permute-start(f32[12,8,512]{2,1,0:T(8,128)S(1)} %get-tuple-element.94), channel_id=1, source_target_pairs={{0,3},{1,2},{2,1},{3,0},{4,7},{5,6},{6,5},{7,4},{8,11},{9,10},{10,... | collective-permute-start | bytes 589832 | tf_op jit(solution)/shard_map/ppermute | solution.py:510
  206.8 18.1 %collective-permute-start.30 = (f32[12,8,512]{2,1,0:T(8,128)S(1)}, f32[12,8,512]{2,1,0:T(8,128)S(1)}, u32[]{:S(2)}, u32[]{:S(2)}) collective-permute-start(f32[12,8,512]{2,1,0:T(8,128)S(1)} %get-tuple-element.95), channel_id=1, source_target_pairs={{0,4},{1,5},{2,6},{3,7},{4,0},{5,1},{6,2},{7,3},{8,12},{9,13},{10,... | collective-permute-start | bytes 589832 | tf_op jit(solution)/shard_map/ppermute | solution.py:510
  212.0 56.3 %collective-permute-start.9 = (f32[12,16,512]{2,1,0:T(8,128)S(1)}, f32[12,16,512]{2,1,0:T(8,128)S(1)}, u32[]{:S(2)}, u32[]{:S(2)}) collective-permute-start(f32[12,16,512]{2,1,0:T(8,128)S(1)} %get-tuple-element.73), channel_id=1, source_target_pairs={{0,1},{1,0},{2,3},{3,2},{4,5},{5,4},{6,7},{7,6},{8,9},{9,8},{10,11... | collective-permute-start | bytes 1179656 | tf_op jit(solution)/shard_map/ppermute | solution.py:510
  212.5 55.8 %collective-permute-start.10 = (f32[12,16,512]{2,1,0:T(8,128)S(1)}, f32[12,16,512]{2,1,0:T(8,128)S(1)}, u32[]{:S(2)}, u32[]{:S(2)}) collective-permute-start(f32[12,16,512]{2,1,0:T(8,128)S(1)} %get-tuple-element.74), channel_id=1, source_target_pairs={{0,2},{1,3},{2,0},{3,1},{4,6},{5,7},{6,4},{7,5},{8,10},{9,11},{10,... | collective-permute-start | bytes 1179656 | tf_op jit(solution)/shard_map/ppermute | solution.py:510
  218.6 18.2 %collective-permute-start.31 = (f32[12,8,512]{2,1,0:T(8,128)S(1)}, f32[12,8,512]{2,1,0:T(8,128)S(1)}, u32[]{:S(2)}, u32[]{:S(2)}) collective-permute-start(f32[12,8,512]{2,1,0:T(8,128)S(1)} %get-tuple-element.96), channel_id=1, source_target_pairs={{0,5},{1,4},{2,7},{3,6},{4,1},{5,0},{6,3},{7,2},{8,13},{9,12},{10,... | collective-permute-start | bytes 589832 | tf_op jit(solution)/shard_map/ppermute | solution.py:510
  223.9 19.2 %collective-permute-start.32 = (f32[12,8,512]{2,1,0:T(8,128)S(1)}, f32[12,8,512]{2,1,0:T(8,128)S(1)}, u32[]{:S(2)}, u32[]{:S(2)}) collective-permute-start(f32[12,8,512]{2,1,0:T(8,128)S(1)} %get-tuple-element.97), channel_id=1, source_target_pairs={{0,6},{1,7},{2,4},{3,5},{4,2},{5,3},{6,0},{7,1},{8,14},{9,15},{10,... | collective-permute-start | bytes 589832 | tf_op jit(solution)/shard_map/ppermute | solution.py:510
  224.9 43.4 %collective-permute-start.33 = (f32[12,8,512]{2,1,0:T(8,128)S(1)}, f32[12,8,512]{2,1,0:T(8,128)S(1)}, u32[]{:S(2)}, u32[]{:S(2)}) collective-permute-start(f32[12,8,512]{2,1,0:T(8,128)S(1)} %get-tuple-element.98), channel_id=1, source_target_pairs={{0,7},{1,6},{2,5},{3,4},{4,3},{5,2},{6,1},{7,0},{8,15},{9,14},{10,... | collective-permute-start | bytes 589832 | tf_op jit(solution)/shard_map/ppermute | solution.py:510
  236.8 35.1 %collective-permute-start.11 = (f32[12,16,512]{2,1,0:T(8,128)S(1)}, f32[12,16,512]{2,1,0:T(8,128)S(1)}, u32[]{:S(2)}, u32[]{:S(2)}) collective-permute-start(f32[12,16,512]{2,1,0:T(8,128)S(1)} %get-tuple-element.75), channel_id=1, source_target_pairs={{0,3},{1,2},{2,1},{3,0},{4,7},{5,6},{6,5},{7,4},{8,11},{9,10},{10,... | collective-permute-start | bytes 1179656 | tf_op jit(solution)/shard_map/ppermute | solution.py:510
  243.2 48.5 %collective-permute-start.12 = (f32[12,16,512]{2,1,0:T(8,128)S(1)}, f32[12,16,512]{2,1,0:T(8,128)S(1)}, u32[]{:S(2)}, u32[]{:S(2)}) collective-permute-start(f32[12,16,512]{2,1,0:T(8,128)S(1)} %get-tuple-element.76), channel_id=1, source_target_pairs={{0,4},{1,5},{2,6},{3,7},{4,0},{5,1},{6,2},{7,3},{8,12},{9,13},{10,... | collective-permute-start | bytes 1179656 | tf_op jit(solution)/shard_map/ppermute | solution.py:510
  268.3 40.2 %collective-permute-start.13 = (f32[12,16,512]{2,1,0:T(8,128)S(1)}, f32[12,16,512]{2,1,0:T(8,128)S(1)}, u32[]{:S(2)}, u32[]{:S(2)}) collective-permute-start(f32[12,16,512]{2,1,0:T(8,128)S(1)} %get-tuple-element.77), channel_id=1, source_target_pairs={{0,5},{1,4},{2,7},{3,6},{4,1},{5,0},{6,3},{7,2},{8,13},{9,12},{10,... | collective-permute-start | bytes 1179656 | tf_op jit(solution)/shard_map/ppermute | solution.py:510
  268.3 54.9 %collective-permute-start.14 = (f32[12,16,512]{2,1,0:T(8,128)S(1)}, f32[12,16,512]{2,1,0:T(8,128)S(1)}, u32[]{:S(2)}, u32[]{:S(2)}) collective-permute-start(f32[12,16,512]{2,1,0:T(8,128)S(1)} %get-tuple-element.78), channel_id=1, source_target_pairs={{0,6},{1,7},{2,4},{3,5},{4,2},{5,3},{6,0},{7,1},{8,14},{9,15},{10,... | collective-permute-start | bytes 1179656 | tf_op jit(solution)/shard_map/ppermute | solution.py:510
  268.3 63.3 %collective-permute-start.15 = (f32[12,16,512]{2,1,0:T(8,128)S(1)}, f32[12,16,512]{2,1,0:T(8,128)S(1)}, u32[]{:S(2)}, u32[]{:S(2)}) collective-permute-start(f32[12,16,512]{2,1,0:T(8,128)S(1)} %get-tuple-element.79), channel_id=1, source_target_pairs={{0,7},{1,6},{2,5},{3,4},{4,3},{5,2},{6,1},{7,0},{8,15},{9,14},{10,... | collective-permute-start | bytes 1179656 | tf_op jit(solution)/shard_map/ppermute | solution.py:510
  271.9 73.4 %collective-permute-start.22 = (f32[12,8,512]{2,1,0:T(8,128)S(1)}, f32[12,8,512]{2,1,0:T(8,128)S(1)}, u32[]{:S(2)}, u32[]{:S(2)}) collective-permute-start(f32[12,8,512]{2,1,0:T(8,128)S(1)} %get-tuple-element.86), channel_id=1, source_target_pairs={{0,3},{1,2},{2,1},{3,0},{4,7},{5,6},{6,5},{7,4},{8,11},{9,10},{10,... | collective-permute-start | bytes 589832 | tf_op jit(solution)/shard_map/ppermute | solution.py:510
  291.6 53.7 %collective-permute-start.23 = (f32[12,8,512]{2,1,0:T(8,128)S(1)}, f32[12,8,512]{2,1,0:T(8,128)S(1)}, u32[]{:S(2)}, u32[]{:S(2)}) collective-permute-start(f32[12,8,512]{2,1,0:T(8,128)S(1)} %get-tuple-element.87), channel_id=1, source_target_pairs={{0,4},{1,5},{2,6},{3,7},{4,0},{5,1},{6,2},{7,3},{8,12},{9,13},{10,... | collective-permute-start | bytes 589832 | tf_op jit(solution)/shard_map/ppermute | solution.py:510
  308.5 36.8 %collective-permute-start.24 = (f32[12,8,512]{2,1,0:T(8,128)S(1)}, f32[12,8,512]{2,1,0:T(8,128)S(1)}, u32[]{:S(2)}, u32[]{:S(2)}) collective-permute-start(f32[12,8,512]{2,1,0:T(8,128)S(1)} %get-tuple-element.88), channel_id=1, source_target_pairs={{0,5},{1,4},{2,7},{3,6},{4,1},{5,0},{6,3},{7,2},{8,13},{9,12},{10,... | collective-permute-start | bytes 589832 | tf_op jit(solution)/shard_map/ppermute | solution.py:510
  323.2 22.1 %collective-permute-start.25 = (f32[12,8,512]{2,1,0:T(8,128)S(1)}, f32[12,8,512]{2,1,0:T(8,128)S(1)}, u32[]{:S(2)}, u32[]{:S(2)}) collective-permute-start(f32[12,8,512]{2,1,0:T(8,128)S(1)} %get-tuple-element.89), channel_id=1, source_target_pairs={{0,6},{1,7},{2,4},{3,5},{4,2},{5,3},{6,0},{7,1},{8,14},{9,15},{10,... | collective-permute-start | bytes 589832 | tf_op jit(solution)/shard_map/ppermute | solution.py:510
  331.7 13.7 %collective-permute-start.26 = (f32[12,8,512]{2,1,0:T(8,128)S(1)}, f32[12,8,512]{2,1,0:T(8,128)S(1)}, u32[]{:S(2)}, u32[]{:S(2)}) collective-permute-start(f32[12,8,512]{2,1,0:T(8,128)S(1)} %get-tuple-element.90), channel_id=1, source_target_pairs={{0,7},{1,6},{2,5},{3,4},{4,3},{5,2},{6,1},{7,0},{8,15},{9,14},{10,... | collective-permute-start | bytes 589832 | tf_op jit(solution)/shard_map/ppermute | solution.py:510
  (13 other events, 103.7 us)
where the time goes:
time: 350 us; the launch traced here: 349 us
  waiting for transfers between devices  163 us (47%)
  Pallas kernels  110 us (31%)
  starting transfers between devices  70 us (20%)
  local copies, waits for them, and re-layouts  6.85 us (2%)
    ppermute x28, waiting for transfers between devices, exchange(): lax.ppermute(parts[s], 'tile', [(t, t ^ s) for t in range(devices)])  96.4 us
    pallas_call x3, Pallas kernels, steps(): pl.pallas_call(functools.partial(steps_kernel, plans, [f - HALO for f in...  80.7 us
    ppermute x28, starting transfers between devices, exchange(): lax.ppermute(parts[s], 'tile', [(t, t ^ s) for t in range(devices)])  55.5 us
    ppermute x1, waiting for transfers between devices, tiled_body(): near_in = lax.ppermute(near, 'tile', [(t, t ^ 1) for t in range(devices)])  32.5 us
    ppermute x1, waiting for transfers between devices, tiled_body(): far_in = lax.ppermute(far, 'tile', apart)  29.5 us
    pallas_call x3, Pallas kernels, mix_levels(): pl.pallas_call(functools.partial(levels_kernel, edges, col is not None),...  10.3 us
    ppermute x4, starting transfers between devices, earlier(): return lax.ppermute(x, 'win', [(i + 1, i) for i in range(windows - 1)])  9.55 us
    pallas_call x2, Pallas kernels, finish(): pl.pallas_call(functools.partial(finish_kernel, len(blocks)), name='finis...  7.96 us
  transfers between devices with their start and end apart: 34, of which 15 were waited for; matrix products, arithmetic and copies ran while one was open for 0% of the time, Pallas kernels for 28%

commit v1 on v0

--- a/solution.py
+++ b/solution.py
@@ -47,16 +47,8 @@
     return parts
 
 
-def pieces_kernel(me_ref, raw_ref, kap_ref, mid_ref, inner_ref, far_ref, near_ref, buf, sems):
+def pieces_kernel(me_ref, raw_ref, kap_ref, mid_ref, inner_ref, far_ref, near_ref):
     _, blocks, rows, _ = raw_ref.shape
-    parts = sems.shape[0]
-    per = blocks // parts
-    copies = [
-        pltpu.make_async_copy(raw_ref.at[:, pl.ds(i * per, per)], buf.at[:, pl.ds(i * per, per)], sems.at[i])
-        for i in range(parts)
-    ]
-    for c in copies:
-        c.start()
     even = (me_ref[0] & 1) == 0
 
     far_ref[HALO * blocks] = jnp.where(even, kap_ref[:SUB, :], kap_ref[rows - SUB :, :])
@@ -64,7 +56,7 @@
 
     def body(at):
         for tile in range(rows // SUB):
-            flat = turn([buf[s, at, tile * SUB : (tile + 1) * SUB, :] for s in range(SUB)])
+            flat = turn([raw_ref[s, at, tile * SUB : (tile + 1) * SUB, :] for s in range(SUB)])
             tops, bottoms = [], []
             for i, part in enumerate(flat):
                 row = tile * SUB + i
@@ -91,12 +83,9 @@
                         for row, value in group:
                             near_ref[row * blocks + at] = value
 
-    for i in range(parts):
-        copies[i].wait()
-
-        @pl.loop(i * per, (i + 1) * per)
-        def _(at):
-            body(at)
+    @pl.loop(0, blocks)
+    def _(at):
+        body(at)
 
 
 def pieces(raw, kappa, me):
@@ -107,10 +96,9 @@
     return pl.pallas_call(
         pieces_kernel,
         name="pieces",
-        in_specs=[SM, pl.BlockSpec(memory_space=pltpu.HBM), VM],
+        in_specs=[SM, VM, VM],
         out_specs=[VM] * 4,
         out_shape=[jax.ShapeDtypeStruct((n, SUB, width), F32) for n in counts],
-        scratch_shapes=[pltpu.VMEM((SUB, blocks, rows, width), F32), pltpu.SemaphoreType.DMA((blocks // 2,))],
         compiler_params=params(20),
         cost_estimate=cost(0, 8 * raw.size),
     )(me, raw.reshape(SUB, blocks, rows, width), kappa)
@@ -459,7 +447,7 @@
 
 def finish(part, mat, base, blocks, out=None):
     _, rows, width = base.shape
-    cols = LANES
+    cols = 2 * LANES if width % (2 * LANES) == 0 else LANES
     spec = pl.BlockSpec((SUB, rows, cols), lambda j: (part, 0, j))
     rest = [] if out is None else [out]
     depth = sum(x.shape[0] for x in blocks)
@@ -505,10 +493,11 @@
     level_mat, *row_mats = ordered(chunks, devices, one, vertical_cov, row_cov)
 
     def exchange(parts):
-        got = {}
-        for s in sorted(range(1, devices), key=lambda s: (-(s.bit_length()), s)):
-            got[s] = lax.ppermute(parts[s], "tile", [(t, t ^ s) for t in range(devices)])
-        return [parts[0]] + [got[s] for s in range(1, devices)]
+        got = [parts[0]] + [None] * (devices - 1)
+        for span in (range(devices // 2, devices), range(devices // 2 - 1, 0, -1)):
+            for s in span:
+                got[s] = lax.ppermute(parts[s], "tile", [(t, t ^ s) for t in range(devices)])
+        return got
 
     own = [mids, inner, far, near]
     ev = steps([2 * HALO], middle, one, inside, half_wind, kappa, own)
@@ -516,7 +505,8 @@
     first = exchange(mixed)
 
     *own, _ = lax.optimization_barrier((mids, inner, far, near, mixed[0]))
-    follow_inner, follow_far, follow_near = earlier(own[1]), earlier(own[2]), earlier(own[3])
+    follow_inner = earlier(own[1])
+    follow_far, follow_near = earlier(own[2]), earlier(own[3])
     ev = steps([HALO, rows - 2 * HALO], HALO, one, inside, half_wind, kappa, own)
     mixed = mix_levels(devices, one, ev, [follow_inner], level_mat)
     second = exchange(mixed)

time: 350 us -> 348 us (level)
  the two profiles are of different devices: /device:TPU:10 before, /device:TPU:14 now
where the time goes in v1:
time: 348 us; the launch traced here: 347 us
  waiting for transfers between devices  152 us (44%)
  Pallas kernels  107 us (31%)
  starting transfers between devices  80.8 us (23%)
  local copies, waits for them, and re-layouts  6.85 us (2%)
    ppermute x28, waiting for transfers between devices, exchange(): lax.ppermute(parts[s], 'tile', [(t, t ^ s) for t in range(devices)])  84 us
    pallas_call x3, Pallas kernels, steps(): pl.pallas_call(functools.partial(steps_kernel, plans, [f - HALO for f in...  80.7 us
    ppermute x28, starting transfers between devices, exchange(): lax.ppermute(parts[s], 'tile', [(t, t ^ s) for t in range(devices)])  67.3 us
    ppermute x1, waiting for transfers between devices, tiled_body(): near_in = lax.ppermute(near, 'tile', [(t, t ^ 1) for t in range(devices)])  33.5 us
    ppermute x1, waiting for transfers between devices, tiled_body(): far_in = lax.ppermute(far, 'tile', apart)  30.6 us
    pallas_call x3, Pallas kernels, mix_levels(): pl.pallas_call(functools.partial(levels_kernel, edges, col is not None),...  10.3 us
    ppermute x4, starting transfers between devices, earlier(): return lax.ppermute(x, 'win', [(i + 1, i) for i in range(windows - 1)])  9.56 us
  transfers between devices with their start and end apart: 34, of which 16 were waited for; matrix products, arithmetic and copies ran while one was open for 0% of the time, Pallas kernels for 28%

profile of v1, /device:TPU:14, one launch (start us, length us, event | category | flops | bytes accessed | tf_op | source)
XLA Modules:
  0.0 347.2 jit_solution(8481769667622316959)
XLA Ops:
  0.0 3.4 copy-done
  4.2 3.3 pieces.1
  12.6 19.0 %shard_map.64.ev_ref = f32[8,16,8,512]{3,2,1,0:T(8,128)S(1)} custom-call(s32[1]{0:T(128)} %bitcast.me_ref, f32[2]{0:T(128)S(1)} %add_convert_fusion.inside_ref, f32[16,8,128]{2,1,0:T(8,128)S(1)} %broadcast_in_dim.4.hw_ref, f32[32,512]{1,0:T(8,128)S(1)} %bitcast.9, f32[128,8,512]{2,1,0:T(8,128)} %get-tuple-element.68.rest_0_, ...), custom_call_target="tpu_custom_call" | custom-call | flops 71565312 | bytes 7340032 | tf_op jit(solution)/shard_map/pallas_call | solution.py:272
  31.6 4.1 %collective-permute-done.rest_0_ = f32[128,8,512]{2,1,0:T(8,128)} collective-permute-done((f32[128,8,512]{2,1,0:T(8,128)}, f32[128,8,512]{2,1,0:T(8,128)}, u32[]{:S(2)}, u32[]{:S(2)}) %collective-permute-start) | collective-permute-done | bytes 2097184 | tf_op jit(solution)/shard_map/ppermute | solution.py:487
  35.7 3.3 mix_levels.3
  39.0 3.8 %collective-permute-start.8 = (f32[192,8,512]{2,1,0:T(8,128)S(1)}, f32[192,8,512]{2,1,0:T(8,128)S(1)}, u32[]{:S(2)}, u32[]{:S(2)}) collective-permute-start(f32[192,8,512]{2,1,0:T(8,128)S(1)} %get-tuple-element.80.rest_1_.rest_0_), channel_id=1, source_target_pairs={{8,0},{16,8},{24,16},{9,1},{17,9},{25,17},{10,2},{18,10},{26,18},{... | collective-permute-start | bytes 9437192 | tf_op jit(solution)/shard_map/ppermute | solution.py:487
  42.8 3.5 collective-permute-start.16
  50.6 30.6 %collective-permute-done.16.rest_3_ = f32[97,8,512]{2,1,0:T(8,128)S(1)} collective-permute-done((f32[97,8,512]{2,1,0:T(8,128)S(1)}, f32[97,8,512]{2,1,0:T(8,128)S(1)}, u32[]{:S(2)}, u32[]{:S(2)}) %collective-permute-start.16) | collective-permute-done | bytes 1589280 | tf_op jit(solution)/shard_map/ppermute | solution.py:490
  81.7 33.5 %collective-permute-done.17.rest_4_ = f32[97,8,512]{2,1,0:T(8,128)S(1)} collective-permute-done((f32[97,8,512]{2,1,0:T(8,128)S(1)}, f32[97,8,512]{2,1,0:T(8,128)S(1)}, u32[]{:S(2)}, u32[]{:S(2)}) %collective-permute-start.17) | collective-permute-done | bytes 1589280 | tf_op jit(solution)/shard_map/ppermute | solution.py:492
  115.7 5.1 %collective-permute-done.1.rest_3_ = f32[8,16,512]{2,1,0:T(8,128)S(1)} collective-permute-done((f32[8,16,512]{2,1,0:T(8,128)S(1)}, f32[8,16,512]{2,1,0:T(8,128)S(1)}, u32[]{:S(2)}, u32[]{:S(2)}) %collective-permute-start.1) | collective-permute-done | bytes 262176 | tf_op jit(solution)/shard_map/ppermute | solution.py:499
  120.8 2.6 collective-permute-done.2.rest_4_
  127.0 31.8 %shard_map.65.ev_ref = f32[12,16,8,512]{3,2,1,0:T(8,128)S(1)} custom-call(s32[1]{0:T(128)} %bitcast.me_ref, f32[2]{0:T(128)S(1)} %add_convert_fusion.inside_ref, f32[16,8,128]{2,1,0:T(8,128)S(1)} %broadcast_in_dim.4.hw_ref, f32[32,512]{1,0:T(8,128)S(1)} %bitcast.10, f32[128,8,512]{2,1,0:T(8,128)} %get-tuple-element.68.rest_0_, ...), custom_call_target="tpu_custom_call" | custom-call | flops 121110528 | bytes 12582912 | tf_op jit(solution)/shard_map/pallas_call | solution.py:272
  163.1 29.9 %shard_map.66.ev_ref = f32[12,16,8,512]{3,2,1,0:T(8,128)S(1)} custom-call(s32[1]{0:T(128)} %bitcast.me_ref, f32[2]{0:T(128)S(1)} %add_convert_fusion.inside_ref, f32[16,8,128]{2,1,0:T(8,128)S(1)} %broadcast_in_dim.4.hw_ref, f32[32,512]{1,0:T(8,128)S(1)} %bitcast.11, f32[192,8,512]{2,1,0:T(8,128)S(1)} %get-tuple-element.80.rest_1_.rest_0_, ...), custom_call_target="tpu_custom_call" | custom-call | flops 121110528 | bytes 12582912 | tf_op jit(solution)/shard_map/pallas_call | solution.py:272
  193.0 5.1 %mix_levels.5 = (f32[12,8,512]{2,1,0:T(8,128)S(1)}, f32[12,8,512]{2,1,0:T(8,128)S(1)}, f32[12,8,512]{2,1,0:T(8,128)S(1)}, f32[12,8,512]{2,1,0:T(8,128)S(1)}, f32...) custom-call(s32[1]{0:T(128)} %bitcast.me_ref, ...), custom_call_target="tpu_custom_call" | custom-call | flops 402653184 | bytes 9437184 | tf_op jit(solution)/shard_map/mix_levels/pallas_call | solution.py:378
  205.7 3.7 %collective-permute-start.30 = (f32[12,8,512]{2,1,0:T(8,128)S(1)}, f32[12,8,512]{2,1,0:T(8,128)S(1)}, u32[]{:S(2)}, u32[]{:S(2)}) collective-permute-start(f32[12,8,512]{2,1,0:T(8,128)S(1)} %get-tuple-element.95), channel_id=1, source_target_pairs={{0,4},{1,5},{2,6},{3,7},{4,0},{5,1},{6,2},{7,3},{8,12},{9,13},{10,... | collective-permute-start | bytes 589832 | tf_op jit(solution)/shard_map/ppermute | solution.py:499
  213.1 4.6 %collective-permute-done.28.rest_2_ = f32[12,8,512]{2,1,0:T(8,128)S(1)} collective-permute-done((f32[12,8,512]{2,1,0:T(8,128)S(1)}, f32[12,8,512]{2,1,0:T(8,128)S(1)}, u32[]{:S(2)}, u32[]{:S(2)}) %collective-permute-start.28) | collective-permute-done | bytes 196640 | tf_op jit(solution)/shard_map/ppermute | solution.py:499
  217.7 4.1 %collective-permute-start.31 = (f32[12,8,512]{2,1,0:T(8,128)S(1)}, f32[12,8,512]{2,1,0:T(8,128)S(1)}, u32[]{:S(2)}, u32[]{:S(2)}) collective-permute-start(f32[12,8,512]{2,1,0:T(8,128)S(1)} %get-tuple-element.96), channel_id=1, source_target_pairs={{0,5},{1,4},{2,7},{3,6},{4,1},{5,0},{6,3},{7,2},{8,13},{9,12},{10,... | collective-permute-start | bytes 589832 | tf_op jit(solution)/shard_map/ppermute | solution.py:499
  221.9 2.9 collective-permute-start.32
  225.3 9.5 %collective-permute-done.31.rest_5_ = f32[12,8,512]{2,1,0:T(8,128)S(1)} collective-permute-done((f32[12,8,512]{2,1,0:T(8,128)S(1)}, f32[12,8,512]{2,1,0:T(8,128)S(1)}, u32[]{:S(2)}, u32[]{:S(2)}) %collective-permute-start.31) | collective-permute-done | bytes 196640 | tf_op jit(solution)/shard_map/ppermute | solution.py:499
  234.8 5.8 %collective-permute-done.32.rest_6_ = f32[12,8,512]{2,1,0:T(8,128)S(1)} collective-permute-done((f32[12,8,512]{2,1,0:T(8,128)S(1)}, f32[12,8,512]{2,1,0:T(8,128)S(1)}, u32[]{:S(2)}, u32[]{:S(2)}) %collective-permute-start.32) | collective-permute-done | bytes 196640 | tf_op jit(solution)/shard_map/ppermute | solution.py:499
  240.6 6.5 %collective-permute-done.33.rest_7_ = f32[12,8,512]{2,1,0:T(8,128)S(1)} collective-permute-done((f32[12,8,512]{2,1,0:T(8,128)S(1)}, f32[12,8,512]{2,1,0:T(8,128)S(1)}, u32[]{:S(2)}, u32[]{:S(2)}) %collective-permute-start.33) | collective-permute-done | bytes 196640 | tf_op jit(solution)/shard_map/ppermute | solution.py:499
  247.0 23.2 %collective-permute-start.14 = (f32[12,16,512]{2,1,0:T(8,128)S(1)}, f32[12,16,512]{2,1,0:T(8,128)S(1)}, u32[]{:S(2)}, u32[]{:S(2)}) collective-permute-start(f32[12,16,512]{2,1,0:T(8,128)S(1)} %get-tuple-element.78), channel_id=1, source_target_pairs={{0,6},{1,7},{2,4},{3,5},{4,2},{5,3},{6,0},{7,1},{8,14},{9,15},{10,... | collective-permute-start | bytes 1179656 | tf_op jit(solution)/shard_map/ppermute | solution.py:499
  270.3 2.7 collective-permute-start.22
  273.0 16.2 %collective-permute-done.12.rest_14_ = f32[12,16,512]{2,1,0:T(8,128)S(1)} collective-permute-done((f32[12,16,512]{2,1,0:T(8,128)S(1)}, f32[12,16,512]{2,1,0:T(8,128)S(1)}, u32[]{:S(2)}, u32[]{:S(2)}) %collective-permute-start.12) | collective-permute-done | bytes 393248 | tf_op jit(solution)/shard_map/ppermute | solution.py:499
  289.2 3.4 collective-permute-start.23
  292.6 13.4 %collective-permute-done.13.rest_15_ = f32[12,16,512]{2,1,0:T(8,128)S(1)} collective-permute-done((f32[12,16,512]{2,1,0:T(8,128)S(1)}, f32[12,16,512]{2,1,0:T(8,128)S(1)}, u32[]{:S(2)}, u32[]{:S(2)}) %collective-permute-start.13) | collective-permute-done | bytes 393248 | tf_op jit(solution)/shard_map/ppermute | solution.py:499
  306.0 4.3 %collective-permute-start.24 = (f32[12,8,512]{2,1,0:T(8,128)S(1)}, f32[12,8,512]{2,1,0:T(8,128)S(1)}, u32[]{:S(2)}, u32[]{:S(2)}) collective-permute-start(f32[12,8,512]{2,1,0:T(8,128)S(1)} %get-tuple-element.88), channel_id=1, source_target_pairs={{0,5},{1,4},{2,7},{3,6},{4,1},{5,0},{6,3},{7,2},{8,13},{9,12},{10,... | collective-permute-start | bytes 589832 | tf_op jit(solution)/shard_map/ppermute | solution.py:499
  310.3 10.5 %collective-permute-done.14.rest_16_ = f32[12,16,512]{2,1,0:T(8,128)S(1)} collective-permute-done((f32[12,16,512]{2,1,0:T(8,128)S(1)}, f32[12,16,512]{2,1,0:T(8,128)S(1)}, u32[]{:S(2)}, u32[]{:S(2)}) %collective-permute-start.14) | collective-permute-done | bytes 393248 | tf_op jit(solution)/shard_map/ppermute | solution.py:499
  323.3 7.1 %collective-permute-done.15.rest_17_ = f32[12,16,512]{2,1,0:T(8,128)S(1)} collective-permute-done((f32[12,16,512]{2,1,0:T(8,128)S(1)}, f32[12,16,512]{2,1,0:T(8,128)S(1)}, u32[]{:S(2)}, u32[]{:S(2)}) %collective-permute-start.15) | collective-permute-done | bytes 393248 | tf_op jit(solution)/shard_map/ppermute | solution.py:499
  332.6 6.2 %mix_rows.1.base_ref = f32[16,256,512]{2,1,0:T(8,128)S(1)} custom-call(bf16[512,512]{1,0:T(8,128)(2,1)S(1)} %copy-done.7, bf16[256,128]{1,0:T(8,128)(2,1)S(1)} %get-tuple-element.53.rest_0_, bf16[256,192]{1,0:T(8,128)(2,1)S(1)} %get-tuple-element.54.rest_1_, f32[8,16,512]{2,1,0:T(8,128)S(1)} %get-tuple-element.58.rest_2_, ...), custom_call_target="tpu_custom_call" | custom-call | flops 4026531840 | bytes 13631488 | tf_op jit(solution)/shard_map/mix_rows/pallas_call | solution.py:428
  338.8 3.0 finish.2.rest_8_
  344.2 3.0 finish.3
  (74 shorter events, 37.9 us)
Async XLA Ops:
  10.0 25.8 %collective-permute-start = (f32[128,8,512]{2,1,0:T(8,128)}, f32[128,8,512]{2,1,0:T(8,128)}, u32[]{:S(2)}, u32[]{:S(2)}) collective-permute-start(f32[128,8,512]{2,1,0:T(8,128)} %get-tuple-element.68.rest_0_), channel_id=1, source_target_pairs={{8,0},{16,8},{24,16},{9,1},{17,9},{25,17},{10,2},{18,10},{26,18},{... | collective-permute-start | bytes 6291464 | tf_op jit(solution)/shard_map/ppermute | solution.py:487
  39.0 120.9 %collective-permute-start.8 = (f32[192,8,512]{2,1,0:T(8,128)S(1)}, f32[192,8,512]{2,1,0:T(8,128)S(1)}, u32[]{:S(2)}, u32[]{:S(2)}) collective-permute-start(f32[192,8,512]{2,1,0:T(8,128)S(1)} %get-tuple-element.80.rest_1_.rest_0_), channel_id=1, source_target_pairs={{8,0},{16,8},{24,16},{9,1},{17,9},{25,17},{10,2},{18,10},{26,18},{... | collective-permute-start | bytes 9437192 | tf_op jit(solution)/shard_map/ppermute | solution.py:487
  42.8 38.3 %collective-permute-start.16 = (f32[97,8,512]{2,1,0:T(8,128)S(1)}, f32[97,8,512]{2,1,0:T(8,128)S(1)}, u32[]{:S(2)}, u32[]{:S(2)}) collective-permute-start(f32[97,8,512]{2,1,0:T(8,128)S(1)} %copy-done.2), channel_id=1, source_target_pairs={{1,2},{3,4},{5,6},{2,1},{4,3},{6,5},{9,10},{11,12},{13,14},{10,9},... | collective-permute-start | bytes 4767752 | tf_op jit(solution)/shard_map/ppermute | solution.py:490
  46.3 68.9 %collective-permute-start.17 = (f32[97,8,512]{2,1,0:T(8,128)S(1)}, f32[97,8,512]{2,1,0:T(8,128)S(1)}, u32[]{:S(2)}, u32[]{:S(2)}) collective-permute-start(f32[97,8,512]{2,1,0:T(8,128)S(1)} %copy-done.4), channel_id=1, source_target_pairs={{0,1},{1,0},{2,3},{3,2},{4,5},{5,4},{6,7},{7,6},{8,9},{9,8},{10,11... | collective-permute-start | bytes 4767752 | tf_op jit(solution)/shard_map/ppermute | solution.py:492
  46.7 77.9 %collective-permute-start.18 = (f32[97,8,512]{2,1,0:T(8,128)S(1)}, f32[97,8,512]{2,1,0:T(8,128)S(1)}, u32[]{:S(2)}, u32[]{:S(2)}) collective-permute-start(f32[97,8,512]{2,1,0:T(8,128)S(1)} %copy-done.2), channel_id=1, source_target_pairs={{8,0},{16,8},{24,16},{9,1},{17,9},{25,17},{10,2},{18,10},{26,18},{... | collective-permute-start | bytes 4767752 | tf_op jit(solution)/shard_map/ppermute | solution.py:487
  48.7 110.1 %collective-permute-start.19 = (f32[97,8,512]{2,1,0:T(8,128)S(1)}, f32[97,8,512]{2,1,0:T(8,128)S(1)}, u32[]{:S(2)}, u32[]{:S(2)}) collective-permute-start(f32[97,8,512]{2,1,0:T(8,128)S(1)} %copy-done.4), channel_id=1, source_target_pairs={{8,0},{16,8},{24,16},{9,1},{17,9},{25,17},{10,2},{18,10},{26,18},{... | collective-permute-start | bytes 4767752 | tf_op jit(solution)/shard_map/ppermute | solution.py:487
  81.2 39.6 %collective-permute-start.1 = (f32[8,16,512]{2,1,0:T(8,128)S(1)}, f32[8,16,512]{2,1,0:T(8,128)S(1)}, u32[]{:S(2)}, u32[]{:S(2)}) collective-permute-start(f32[8,16,512]{2,1,0:T(8,128)S(1)} %get-tuple-element.59), channel_id=1, source_target_pairs={{0,1},{1,0},{2,3},{3,2},{4,5},{5,4},{6,7},{7,6},{8,9},{9,8},{10,11... | collective-permute-start | bytes 786440 | tf_op jit(solution)/shard_map/ppermute | solution.py:499
  120.8 77.4 %collective-permute-start.3 = (f32[8,16,512]{2,1,0:T(8,128)S(1)}, f32[8,16,512]{2,1,0:T(8,128)S(1)}, u32[]{:S(2)}, u32[]{:S(2)}) collective-permute-start(f32[8,16,512]{2,1,0:T(8,128)S(1)} %get-tuple-element.61), channel_id=1, source_target_pairs={{0,3},{1,2},{2,1},{3,0},{4,7},{5,6},{6,5},{7,4},{8,11},{9,10},{10,... | collective-permute-start | bytes 786440 | tf_op jit(solution)/shard_map/ppermute | solution.py:499
  123.4 76.0 %collective-permute-start.4 = (f32[8,16,512]{2,1,0:T(8,128)S(1)}, f32[8,16,512]{2,1,0:T(8,128)S(1)}, u32[]{:S(2)}, u32[]{:S(2)}) collective-permute-start(f32[8,16,512]{2,1,0:T(8,128)S(1)} %get-tuple-element.62), channel_id=1, source_target_pairs={{0,4},{1,5},{2,6},{3,7},{4,0},{5,1},{6,2},{7,3},{8,12},{9,13},{10,... | collective-permute-start | bytes 786440 | tf_op jit(solution)/shard_map/ppermute | solution.py:499
  124.7 77.2 %collective-permute-start.5 = (f32[8,16,512]{2,1,0:T(8,128)S(1)}, f32[8,16,512]{2,1,0:T(8,128)S(1)}, u32[]{:S(2)}, u32[]{:S(2)}) collective-permute-start(f32[8,16,512]{2,1,0:T(8,128)S(1)} %get-tuple-element.63), channel_id=1, source_target_pairs={{0,5},{1,4},{2,7},{3,6},{4,1},{5,0},{6,3},{7,2},{8,13},{9,12},{10,... | collective-permute-start | bytes 786440 | tf_op jit(solution)/shard_map/ppermute | solution.py:499
  158.8 43.9 %collective-permute-start.6 = (f32[8,16,512]{2,1,0:T(8,128)S(1)}, f32[8,16,512]{2,1,0:T(8,128)S(1)}, u32[]{:S(2)}, u32[]{:S(2)}) collective-permute-start(f32[8,16,512]{2,1,0:T(8,128)S(1)} %get-tuple-element.64), channel_id=1, source_target_pairs={{0,6},{1,7},{2,4},{3,5},{4,2},{5,3},{6,0},{7,1},{8,14},{9,15},{10,... | collective-permute-start | bytes 786440 | tf_op jit(solution)/shard_map/ppermute | solution.py:499
  159.9 42.9 %collective-permute-start.7 = (f32[8,16,512]{2,1,0:T(8,128)S(1)}, f32[8,16,512]{2,1,0:T(8,128)S(1)}, u32[]{:S(2)}, u32[]{:S(2)}) collective-permute-start(f32[8,16,512]{2,1,0:T(8,128)S(1)} %get-tuple-element.65), channel_id=1, source_target_pairs={{0,7},{1,6},{2,5},{3,4},{4,3},{5,2},{6,1},{7,0},{8,15},{9,14},{10,... | collective-permute-start | bytes 786440 | tf_op jit(solution)/shard_map/ppermute | solution.py:499
  199.4 10.0 %collective-permute-start.21 = (f32[12,8,512]{2,1,0:T(8,128)S(1)}, f32[12,8,512]{2,1,0:T(8,128)S(1)}, u32[]{:S(2)}, u32[]{:S(2)}) collective-permute-start(f32[12,8,512]{2,1,0:T(8,128)S(1)} %get-tuple-element.85), channel_id=1, source_target_pairs={{0,2},{1,3},{2,0},{3,1},{4,6},{5,7},{6,4},{7,5},{8,10},{9,11},{10,... | collective-permute-start | bytes 589832 | tf_op jit(solution)/shard_map/ppermute | solution.py:499
  201.8 10.1 %collective-permute-start.27 = (f32[12,8,512]{2,1,0:T(8,128)S(1)}, f32[12,8,512]{2,1,0:T(8,128)S(1)}, u32[]{:S(2)}, u32[]{:S(2)}) collective-permute-start(f32[12,8,512]{2,1,0:T(8,128)S(1)} %get-tuple-element.92), channel_id=1, source_target_pairs={{0,1},{1,0},{2,3},{3,2},{4,5},{5,4},{6,7},{7,6},{8,9},{9,8},{10,11... | collective-permute-start | bytes 589832 | tf_op jit(solution)/shard_map/ppermute | solution.py:499
  202.7 15.0 %collective-permute-start.28 = (f32[12,8,512]{2,1,0:T(8,128)S(1)}, f32[12,8,512]{2,1,0:T(8,128)S(1)}, u32[]{:S(2)}, u32[]{:S(2)}) collective-permute-start(f32[12,8,512]{2,1,0:T(8,128)S(1)} %get-tuple-element.93), channel_id=1, source_target_pairs={{0,2},{1,3},{2,0},{3,1},{4,6},{5,7},{6,4},{7,5},{8,10},{9,11},{10,... | collective-permute-start | bytes 589832 | tf_op jit(solution)/shard_map/ppermute | solution.py:499
  202.7 19.2 %collective-permute-start.29 = (f32[12,8,512]{2,1,0:T(8,128)S(1)}, f32[12,8,512]{2,1,0:T(8,128)S(1)}, u32[]{:S(2)}, u32[]{:S(2)}) collective-permute-start(f32[12,8,512]{2,1,0:T(8,128)S(1)} %get-tuple-element.94), channel_id=1, source_target_pairs={{0,3},{1,2},{2,1},{3,0},{4,7},{5,6},{6,5},{7,4},{8,11},{9,10},{10,... | collective-permute-start | bytes 589832 | tf_op jit(solution)/shard_map/ppermute | solution.py:499
  205.7 19.1 %collective-permute-start.30 = (f32[12,8,512]{2,1,0:T(8,128)S(1)}, f32[12,8,512]{2,1,0:T(8,128)S(1)}, u32[]{:S(2)}, u32[]{:S(2)}) collective-permute-start(f32[12,8,512]{2,1,0:T(8,128)S(1)} %get-tuple-element.95), channel_id=1, source_target_pairs={{0,4},{1,5},{2,6},{3,7},{4,0},{5,1},{6,2},{7,3},{8,12},{9,13},{10,... | collective-permute-start | bytes 589832 | tf_op jit(solution)/shard_map/ppermute | solution.py:499
  209.4 37.6 %collective-permute-start.9 = (f32[12,16,512]{2,1,0:T(8,128)S(1)}, f32[12,16,512]{2,1,0:T(8,128)S(1)}, u32[]{:S(2)}, u32[]{:S(2)}) collective-permute-start(f32[12,16,512]{2,1,0:T(8,128)S(1)} %get-tuple-element.73), channel_id=1, source_target_pairs={{0,1},{1,0},{2,3},{3,2},{4,5},{5,4},{6,7},{7,6},{8,9},{9,8},{10,11... | collective-permute-start | bytes 1179656 | tf_op jit(solution)/shard_map/ppermute | solution.py:499
  212.0 58.3 %collective-permute-start.10 = (f32[12,16,512]{2,1,0:T(8,128)S(1)}, f32[12,16,512]{2,1,0:T(8,128)S(1)}, u32[]{:S(2)}, u32[]{:S(2)}) collective-permute-start(f32[12,16,512]{2,1,0:T(8,128)S(1)} %get-tuple-element.74), channel_id=1, source_target_pairs={{0,2},{1,3},{2,0},{3,1},{4,6},{5,7},{6,4},{7,5},{8,10},{9,11},{10,... | collective-permute-start | bytes 1179656 | tf_op jit(solution)/shard_map/ppermute | solution.py:499
  217.7 17.1 %collective-permute-start.31 = (f32[12,8,512]{2,1,0:T(8,128)S(1)}, f32[12,8,512]{2,1,0:T(8,128)S(1)}, u32[]{:S(2)}, u32[]{:S(2)}) collective-permute-start(f32[12,8,512]{2,1,0:T(8,128)S(1)} %get-tuple-element.96), channel_id=1, source_target_pairs={{0,5},{1,4},{2,7},{3,6},{4,1},{5,0},{6,3},{7,2},{8,13},{9,12},{10,... | collective-permute-start | bytes 589832 | tf_op jit(solution)/shard_map/ppermute | solution.py:499
  221.9 18.7 %collective-permute-start.32 = (f32[12,8,512]{2,1,0:T(8,128)S(1)}, f32[12,8,512]{2,1,0:T(8,128)S(1)}, u32[]{:S(2)}, u32[]{:S(2)}) collective-permute-start(f32[12,8,512]{2,1,0:T(8,128)S(1)} %get-tuple-element.97), channel_id=1, source_target_pairs={{0,6},{1,7},{2,4},{3,5},{4,2},{5,3},{6,0},{7,1},{8,14},{9,15},{10,... | collective-permute-start | bytes 589832 | tf_op jit(solution)/shard_map/ppermute | solution.py:499
  224.8 22.2 %collective-permute-start.33 = (f32[12,8,512]{2,1,0:T(8,128)S(1)}, f32[12,8,512]{2,1,0:T(8,128)S(1)}, u32[]{:S(2)}, u32[]{:S(2)}) collective-permute-start(f32[12,8,512]{2,1,0:T(8,128)S(1)} %get-tuple-element.98), channel_id=1, source_target_pairs={{0,7},{1,6},{2,5},{3,4},{4,3},{5,2},{6,1},{7,0},{8,15},{9,14},{10,... | collective-permute-start | bytes 589832 | tf_op jit(solution)/shard_map/ppermute | solution.py:499
  234.8 35.5 %collective-permute-start.11 = (f32[12,16,512]{2,1,0:T(8,128)S(1)}, f32[12,16,512]{2,1,0:T(8,128)S(1)}, u32[]{:S(2)}, u32[]{:S(2)}) collective-permute-start(f32[12,16,512]{2,1,0:T(8,128)S(1)} %get-tuple-element.75), channel_id=1, source_target_pairs={{0,3},{1,2},{2,1},{3,0},{4,7},{5,6},{6,5},{7,4},{8,11},{9,10},{10,... | collective-permute-start | bytes 1179656 | tf_op jit(solution)/shard_map/ppermute | solution.py:499
  240.5 48.6 %collective-permute-start.12 = (f32[12,16,512]{2,1,0:T(8,128)S(1)}, f32[12,16,512]{2,1,0:T(8,128)S(1)}, u32[]{:S(2)}, u32[]{:S(2)}) collective-permute-start(f32[12,16,512]{2,1,0:T(8,128)S(1)} %get-tuple-element.76), channel_id=1, source_target_pairs={{0,4},{1,5},{2,6},{3,7},{4,0},{5,1},{6,2},{7,3},{8,12},{9,13},{10,... | collective-permute-start | bytes 1179656 | tf_op jit(solution)/shard_map/ppermute | solution.py:499
  247.0 59.0 %collective-permute-start.13 = (f32[12,16,512]{2,1,0:T(8,128)S(1)}, f32[12,16,512]{2,1,0:T(8,128)S(1)}, u32[]{:S(2)}, u32[]{:S(2)}) collective-permute-start(f32[12,16,512]{2,1,0:T(8,128)S(1)} %get-tuple-element.77), channel_id=1, source_target_pairs={{0,5},{1,4},{2,7},{3,6},{4,1},{5,0},{6,3},{7,2},{8,13},{9,12},{10,... | collective-permute-start | bytes 1179656 | tf_op jit(solution)/shard_map/ppermute | solution.py:499
  247.0 73.7 %collective-permute-start.14 = (f32[12,16,512]{2,1,0:T(8,128)S(1)}, f32[12,16,512]{2,1,0:T(8,128)S(1)}, u32[]{:S(2)}, u32[]{:S(2)}) collective-permute-start(f32[12,16,512]{2,1,0:T(8,128)S(1)} %get-tuple-element.78), channel_id=1, source_target_pairs={{0,6},{1,7},{2,4},{3,5},{4,2},{5,3},{6,0},{7,1},{8,14},{9,15},{10,... | collective-permute-start | bytes 1179656 | tf_op jit(solution)/shard_map/ppermute | solution.py:499
  270.3 60.1 %collective-permute-start.15 = (f32[12,16,512]{2,1,0:T(8,128)S(1)}, f32[12,16,512]{2,1,0:T(8,128)S(1)}, u32[]{:S(2)}, u32[]{:S(2)}) collective-permute-start(f32[12,16,512]{2,1,0:T(8,128)S(1)} %get-tuple-element.79), channel_id=1, source_target_pairs={{0,7},{1,6},{2,5},{3,4},{4,3},{5,2},{6,1},{7,0},{8,15},{9,14},{10,... | collective-permute-start | bytes 1179656 | tf_op jit(solution)/shard_map/ppermute | solution.py:499
  270.3 71.6 %collective-permute-start.22 = (f32[12,8,512]{2,1,0:T(8,128)S(1)}, f32[12,8,512]{2,1,0:T(8,128)S(1)}, u32[]{:S(2)}, u32[]{:S(2)}) collective-permute-start(f32[12,8,512]{2,1,0:T(8,128)S(1)} %get-tuple-element.86), channel_id=1, source_target_pairs={{0,3},{1,2},{2,1},{3,0},{4,7},{5,6},{6,5},{7,4},{8,11},{9,10},{10,... | collective-permute-start | bytes 589832 | tf_op jit(solution)/shard_map/ppermute | solution.py:499
  289.2 52.6 %collective-permute-start.23 = (f32[12,8,512]{2,1,0:T(8,128)S(1)}, f32[12,8,512]{2,1,0:T(8,128)S(1)}, u32[]{:S(2)}, u32[]{:S(2)}) collective-permute-start(f32[12,8,512]{2,1,0:T(8,128)S(1)} %get-tuple-element.87), channel_id=1, source_target_pairs={{0,4},{1,5},{2,6},{3,7},{4,0},{5,1},{6,2},{7,3},{8,12},{9,13},{10,... | collective-permute-start | bytes 589832 | tf_op jit(solution)/shard_map/ppermute | solution.py:499
  306.0 35.8 %collective-permute-start.24 = (f32[12,8,512]{2,1,0:T(8,128)S(1)}, f32[12,8,512]{2,1,0:T(8,128)S(1)}, u32[]{:S(2)}, u32[]{:S(2)}) collective-permute-start(f32[12,8,512]{2,1,0:T(8,128)S(1)} %get-tuple-element.88), channel_id=1, source_target_pairs={{0,5},{1,4},{2,7},{3,6},{4,1},{5,0},{6,3},{7,2},{8,13},{9,12},{10,... | collective-permute-start | bytes 589832 | tf_op jit(solution)/shard_map/ppermute | solution.py:499
  320.8 21.1 %collective-permute-start.25 = (f32[12,8,512]{2,1,0:T(8,128)S(1)}, f32[12,8,512]{2,1,0:T(8,128)S(1)}, u32[]{:S(2)}, u32[]{:S(2)}) collective-permute-start(f32[12,8,512]{2,1,0:T(8,128)S(1)} %get-tuple-element.89), channel_id=1, source_target_pairs={{0,6},{1,7},{2,4},{3,5},{4,2},{5,3},{6,0},{7,1},{8,14},{9,15},{10,... | collective-permute-start | bytes 589832 | tf_op jit(solution)/shard_map/ppermute | solution.py:499
  330.4 13.8 %collective-permute-start.26 = (f32[12,8,512]{2,1,0:T(8,128)S(1)}, f32[12,8,512]{2,1,0:T(8,128)S(1)}, u32[]{:S(2)}, u32[]{:S(2)}) collective-permute-start(f32[12,8,512]{2,1,0:T(8,128)S(1)} %get-tuple-element.90), channel_id=1, source_target_pairs={{0,7},{1,6},{2,5},{3,4},{4,3},{5,2},{6,1},{7,0},{8,15},{9,14},{10,... | collective-permute-start | bytes 589832 | tf_op jit(solution)/shard_map/ppermute | solution.py:499
  (13 other events, 101.7 us)

commit v2 on v1

--- a/solution.py
+++ b/solution.py
@@ -13,6 +13,8 @@
 SUB = 8
 HALO = STEPS
 LANES = 128
+FIRST = 4
+RELAY = False
 
 
 F32 = jnp.float32
@@ -32,6 +34,20 @@
 
 def iota(shape, dim):
     return lax.broadcasted_iota(jnp.int32, shape, dim)
+
+
+def split(x):
+    hi = x.astype(BF16)
+    lo = (x - hi.astype(F32)).astype(BF16)
+    return hi, lo
+
+
+def mm(a, b):
+    return jnp.dot(a, b, preferred_element_type=F32)
+
+
+def one_hot(match):
+    return match.astype(F32).astype(BF16)
 
 
 def turn(parts):
@@ -47,61 +63,126 @@
     return parts
 
 
-def pieces_kernel(me_ref, raw_ref, kap_ref, mid_ref, inner_ref, far_ref, near_ref):
-    _, blocks, rows, _ = raw_ref.shape
+def column_order(width):
+    tiles = width // LANES
+    at = iota((width, width), 1)
+    return one_hot(iota((width, width), 0) == (at & (LANES - 1)) * tiles + (at >> (LANES.bit_length() - 1)))
+
+
+def reorder(x, order):
+    hi, lo = split(x)
+    return mm(hi, order) + mm(lo, order)
+
+
+def edge_rows(source, is_top):
+    flat = turn(source)
+    return flat[:HALO] if is_top else flat[SUB - HALO :]
+
+
+def far_kernel(me_ref, top_ref, bottom_ref, kap_ref, far_ref, order):
+    _, per, _, width = top_ref.shape
+    rows = kap_ref.shape[0]
+    blocks = per * pl.num_programs(0)
+    step = pl.program_id(0)
     even = (me_ref[0] & 1) == 0
 
-    far_ref[HALO * blocks] = jnp.where(even, kap_ref[:SUB, :], kap_ref[rows - SUB :, :])
-    near_ref[HALO * blocks] = jnp.where(even, kap_ref[rows - SUB :, :], kap_ref[:SUB, :])
-
-    def body(at):
-        for tile in range(rows // SUB):
-            flat = turn([raw_ref[s, at, tile * SUB : (tile + 1) * SUB, :] for s in range(SUB)])
-            tops, bottoms = [], []
-            for i, part in enumerate(flat):
-                row = tile * SUB + i
-                if row < HALO:
-                    tops.append((row, part))
-                elif row < 2 * HALO:
-                    inner_ref[(row - HALO) * blocks + at] = part
-                elif row < rows - 2 * HALO:
-                    mid_ref[(row - 2 * HALO) * blocks + at] = part
-                elif row < rows - HALO:
-                    inner_ref[(row - rows + 3 * HALO) * blocks + at] = part
-                else:
-                    bottoms.append((row - rows + HALO, part))
-            for is_top, group in ((True, tops), (False, bottoms)):
-                if group:
-
-                    @pl.when(even == is_top)
-                    def _(group=group):
-                        for row, value in group:
-                            far_ref[row * blocks + at] = value
-
-                    @pl.when(even != is_top)
-                    def _(group=group):
-                        for row, value in group:
-                            near_ref[row * blocks + at] = value
-
-    @pl.loop(0, blocks)
-    def _(at):
-        body(at)
-
-
-def pieces(raw, kappa, me):
+    @pl.when(step == 0)
+    def _():
+        order[...] = column_order(width)
+        kapx = reorder(kap_ref[...], order[...])
+        far_ref[HALO * blocks] = jnp.where(even, kapx[:SUB, :], kapx[rows - SUB :, :])
+
+    for is_top, source in ((True, top_ref), (False, bottom_ref)):
+
+        @pl.when(even == is_top)
+        def _(is_top=is_top, source=source):
+            flat = []
+            for p in range(per):
+                flat += edge_rows([source[s, p] for s in range(SUB)], is_top)
+            moved = reorder(jnp.concatenate(flat, axis=0), order[...])
+            for p in range(per):
+                for row in range(HALO):
+                    at = (p * HALO + row) * SUB
+                    far_ref[row * blocks + step * per + p] = moved[at : at + SUB]
+
+
+def far_edge(raw, kappa, me):
     levels, rows, width = raw.shape
     blocks = levels // SUB
-    middle = rows - 4 * HALO
-    counts = [middle * blocks, 2 * HALO * blocks, HALO * blocks + 1, HALO * blocks + 1]
+    per = 4 if blocks % 4 == 0 else 2
+    count = HALO * blocks + 1
+    parts = raw.reshape(SUB, blocks, rows, width)
+    last = rows // SUB - 1
     return pl.pallas_call(
-        pieces_kernel,
+        far_kernel,
+        name="far_edge",
+        grid=(blocks // per,),
+        in_specs=[
+            SM,
+            pl.BlockSpec((SUB, per, SUB, width), lambda i: (0, i, 0, 0)),
+            pl.BlockSpec((SUB, per, SUB, width), lambda i: (0, i, last, 0)),
+            pl.BlockSpec((rows, width), lambda i: (0, 0)),
+        ],
+        out_specs=pl.BlockSpec((count, SUB, width), lambda i: (0, 0, 0)),
+        out_shape=jax.ShapeDtypeStruct((count, SUB, width), F32),
+        scratch_shapes=[pltpu.VMEM((width, width), BF16)],
+        compiler_params=params(60),
+        cost_estimate=cost(0, 3 * raw.size),
+    )(me, parts, parts, kappa)
+
+
+def pieces_kernel(cuts, me_ref, raw_ref, kap_ref, *rest):
+    refs, near_ref, kapx_ref, order = rest[:-3], rest[-3], rest[-2], rest[-1]
+    _, per, rows, width = raw_ref.shape
+    step = pl.program_id(0)
+    blocks = per * pl.num_programs(0)
+    even = (me_ref[0] & 1) == 0
+
+    @pl.when(step == 0)
+    def _():
+        order[...] = column_order(width)
+        kapx = reorder(kap_ref[...], order[...])
+        kapx_ref[...] = kapx
+        near_ref[HALO * blocks] = jnp.where(even, kapx[rows - SUB :, :], kapx[:SUB, :])
+
+    for p in range(per):
+        flat = []
+        for tile in range(rows // SUB):
+            flat += turn([raw_ref[s, p, tile * SUB : (tile + 1) * SUB, :] for s in range(SUB)])
+        edge = [jnp.where(even, b, a) for a, b in zip(flat[:HALO], flat[rows - HALO :])]
+        moved = reorder(jnp.concatenate(flat[HALO : rows - HALO] + edge, axis=0), order[...])
+        for (first, count), ref in zip(cuts, refs):
+            for i in range(count):
+                at = (first - HALO + i) * SUB
+                ref[i, p] = moved[at : at + SUB]
+        for i in range(HALO):
+            at = (rows - 2 * HALO + i) * SUB
+            near_ref[i * blocks + step * per + p] = moved[at : at + SUB]
+
+
+def pieces(raw, kappa, cuts, me):
+    levels, rows, width = raw.shape
+    blocks = levels // SUB
+    per = 2
+    near = (HALO * blocks + 1, SUB, width)
+    *parts, near, kapx = pl.pallas_call(
+        functools.partial(pieces_kernel, cuts),
         name="pieces",
-        in_specs=[SM, VM, VM],
-        out_specs=[VM] * 4,
-        out_shape=[jax.ShapeDtypeStruct((n, SUB, width), F32) for n in counts],
-        compiler_params=params(20),
-        cost_estimate=cost(0, 8 * raw.size),
+        grid=(blocks // per,),
+        in_specs=[
+            SM,
+            pl.BlockSpec((SUB, per, rows, width), lambda i: (0, i, 0, 0)),
+            pl.BlockSpec((rows, width), lambda i: (0, 0)),
+        ],
+        out_specs=[pl.BlockSpec((n, per, SUB, width), lambda i: (0, i, 0, 0)) for _, n in cuts]
+        + [pl.BlockSpec(near, lambda i: (0, 0, 0)), pl.BlockSpec((rows, width), lambda i: (0, 0))],
+        out_shape=[jax.ShapeDtypeStruct((n, blocks, SUB, width), F32) for _, n in cuts]
+        + [jax.ShapeDtypeStruct(near, F32), jax.ShapeDtypeStruct((rows, width), F32)],
+        scratch_shapes=[pltpu.VMEM((width, width), BF16)],
+        compiler_params=params(60),
+        cost_estimate=cost(4 * raw.size * width, 8 * raw.size),
     )(me, raw.reshape(SUB, blocks, rows, width), kappa)
+    return *[x.reshape(x.shape[0] * blocks, SUB, width) for x in parts], near, kapx
 
 
 def steps_kernel(plans, firsts, halos, me_ref, inside_ref, hw_ref, kap_ref, *rest):
@@ -172,8 +253,6 @@
     lax.fori_loop(0, window, ready, 0)
 
     tiles = width // LANES
-    lane = iota((SUB, LANES), 1)
-    at_start, at_end = lane == 0, lane == LANES - 1
 
     def advance(src, dst, r, factor, final):
         def load(row, i):
@@ -184,12 +263,10 @@
         for i in range(1, blocks + 1):
             after, up, down = load(r, i + 1), load(r + 1, i), load(r - 1, i)
             wind = hw_ref[i - 1]
-            to_right = [pltpu.roll(c, 1, axis=1) for c in center]
-            to_left = [pltpu.roll(c, LANES - 1, axis=1) for c in center]
+            line = [pltpu.roll(center[-1], 1, axis=1), *center, pltpu.roll(center[0], LANES - 1, axis=1)]
             new = []
             for k in range(tiles):
-                west = jnp.where(at_start, to_right[k - 1], to_right[k])
-                east = jnp.where(at_end, to_left[(k + 1) % tiles], to_left[k])
+                west, east = line[k], line[k + 2]
                 cols = slice(k * LANES, (k + 1) * LANES)
                 value = (
                     keep[r, :, cols] * center[k]
@@ -234,7 +311,7 @@
             lax.fori_loop(low, high, body, 0)
 
 
-def steps(firsts, count, me, inside, half_wind, kappa, sources, halo_sources=None):
+def steps(firsts, count, me, inside, half_wind, kappa, cuts, sources, halo_sources=None, limit=24):
     rows, width = kappa.shape
     blocks = half_wind.shape[0]
     window = count + 2 * HALO
@@ -242,25 +319,23 @@
     arrays = [*sources, *(halo_sources or [])]
 
     def locate(row, parity):
+        far, near = len(cuts), len(cuts) + 1
+        first, second = (far, near) if parity == 0 else (near, far)
         if row < 0:
-            return (4 if parity == 0 else 5), row + HALO
+            return first + 2, row + HALO
         if row >= rows:
-            return (5 if parity == 0 else 4), row - rows
+            return second + 2, row - rows
         if row < HALO:
-            return (2 if parity == 0 else 3), row
+            return first, row
         if row >= rows - HALO:
-            return (3 if parity == 0 else 2), row - rows + HALO
-        if row < 2 * HALO:
-            return 1, row - HALO
-        if row >= rows - 2 * HALO:
-            return 1, row - rows + 3 * HALO
-        return 0, row - 2 * HALO
+            return second, row - rows + HALO
+        return next((k, row - start) for k, (start, n) in enumerate(cuts) if start <= row < start + n)
 
     plans = {}
     for g, f in enumerate(firsts):
         for parity in (0, 1):
             plan = [(*locate(f - HALO + r, parity), r) for r in range(window)]
-            plans[g, parity] = (plan, (4 if (g == 0) == (parity == 0) else 5))
+            plans[g, parity] = (plan, len(cuts) + (2 if (g == 0) == (parity == 0) else 3))
     used = sorted({k for plan, _ in plans.values() for k, _, _ in plan})
     plans = {
         key: ([(used.index(k), row, to) for k, row, to in plan], used.index(halo) if halos else None)
@@ -283,38 +358,41 @@
             pltpu.SemaphoreType.DMA((window,)),
             *extra,
         ],
-        compiler_params=params(24),
+        compiler_params=params(limit),
         cost_estimate=cost(14 * updates, 4 * n * (window + count) * blocks * SUB * width),
     )(me, inside, half_wind, kappa, *[arrays[k] for k in used])
 
 
-def split(x):
-    hi = x.astype(BF16)
-    lo = (x - hi.astype(F32)).astype(BF16)
-    return hi, lo
-
-
-def mm(a, b):
-    return jnp.dot(a, b, preferred_element_type=F32)
-
-
-def one_hot(match):
-    return match.astype(F32).astype(BF16)
-
-
-def order_kernel(chunks, devices, me_ref, vert_ref, row_ref, level_ref, *outs):
-    levels, rows = vert_ref.shape[0], row_ref.shape[0]
-    me = me_ref[0]
-    own = levels // devices
-    blocks = levels // SUB
-    here = rows // devices
+def order_levels_kernel(devices, me_ref, vert_ref, out_ref):
+    levels = vert_ref.shape[0]
+    own, blocks = levels // devices, levels // SUB
     at = iota((levels, levels), 0)
     partner = sum((at >= s * own).astype(jnp.int32) for s in range(1, devices))
-    left = one_hot(iota((levels, levels), 1) == (partner ^ me) * own + (at - partner * own))
+    left = one_hot(iota((levels, levels), 1) == (partner ^ me_ref[0]) * own + (at - partner * own))
     at = iota((levels, levels), 1)
     block, sub = at >> (SUB.bit_length() - 1), at & (SUB - 1)
     right = one_hot(iota((levels, levels), 0) == sub * blocks + block)
-    level_ref[...] = mm(mm(left, vert_ref[...]).astype(BF16), right).astype(BF16)
+    out_ref[...] = mm(mm(left, vert_ref[...]).astype(BF16), right).astype(BF16)
+
+
+def order_levels(devices, me, vert):
+    return pl.pallas_call(
+        functools.partial(order_levels_kernel, devices),
+        name="order_levels",
+        in_specs=[SM, VM],
+        out_specs=VM,
+        out_shape=jax.ShapeDtypeStruct(vert.shape, BF16),
+        compiler_params=params(8),
+        cost_estimate=cost(4 * vert.size * vert.shape[0], 4 * vert.size),
+    )(me, vert)
+
+
+def order_rest_kernel(chunks, devices, me_ref, row_ref, col_ref, colx_ref, *outs):
+    rows = row_ref.shape[0]
+    here = rows // devices
+    flip = (((0,), (0,)), ((), ()))
+    pick = column_order(col_ref.shape[0])
+    colx_ref[...] = lax.dot_general(pick, col_ref[...], flip, preferred_element_type=F32).astype(BF16)
     for segments, ref in zip(chunks, outs):
         count = sum(n for _, n in segments)
         at = iota((rows, 2 * count * devices), 1)
@@ -326,23 +404,23 @@
         for (first, n), (after, _) in zip(segments, segments[1:]):
             base += n
             source = source + jnp.where(within >= base, after - first - n, 0)
-        pick = one_hot(iota((rows, 2 * count * devices), 0) == (partner ^ me) * here + source)
+        pick = one_hot(iota((rows, 2 * count * devices), 0) == (partner ^ me_ref[0]) * here + source)
         ref[...] = mm(row_ref[...], pick).astype(BF16)
 
 
-def ordered(chunks, devices, me, vert, row):
-    levels, rows = vert.shape[0], row.shape[0]
+def order_rest(chunks, devices, me, row, col):
+    rows = row.shape[0]
     widths = [2 * devices * sum(n for _, n in segments) for segments in chunks]
     return pl.pallas_call(
-        functools.partial(order_kernel, chunks, devices),
-        name="ordered",
+        functools.partial(order_rest_kernel, chunks, devices),
+        name="order_rest",
         in_specs=[SM, VM, VM],
         out_specs=[VM] * (1 + len(chunks)),
-        out_shape=[jax.ShapeDtypeStruct((levels, levels), BF16)]
+        out_shape=[jax.ShapeDtypeStruct(col.shape, BF16)]
         + [jax.ShapeDtypeStruct((rows, w), BF16) for w in widths],
         compiler_params=params(16),
         cost_estimate=cost(2 * rows * rows * rows, 4 * rows * rows),
-    )(me, vert, row)
+    )(me, row, col)
 
 
 def levels_kernel(edges, with_columns, me_ref, ev_ref, mat_ref, *rest):
@@ -402,13 +480,15 @@
     return jnp.concatenate(split(x), axis=0)
 
 
-def rows_kernel(counts, col_ref, *rest):
+def rows_kernel(counts, added, col_ref, *rest):
     mats, xs, out_ref = rest[: len(counts)], rest[len(counts) : -1], rest[-1]
+    extra = dict(zip(added, xs[sum(counts) :]))
     width = out_ref.shape[2]
     totals = [None] * SUB
     start = 0
     for mat_ref, count in zip(mats, counts):
-        x = jnp.concatenate([ref[...] for ref in xs[start : start + count]], axis=0)
+        parts = [xs[i][...] + extra[i][...] if i in extra else xs[i][...] for i in range(start, start + count)]
+        x = jnp.concatenate(parts, axis=0)
         start += count
         depth = x.shape[0]
         hi, lo = split(x.reshape(depth * SUB, width))
@@ -420,22 +500,22 @@
         out_ref[z] = totals[z]
 
 
-def mix_rows(col, mats, groups):
+def mix_rows(col, mats, groups, moved):
     blocks = [x for group in groups for x in group]
     own, width = blocks[0].shape[1:]
     rows = mats[0].shape[0]
     depth = sum(x.shape[0] for x in blocks)
     return pl.pallas_call(
-        functools.partial(rows_kernel, [len(g) for g in groups]),
+        functools.partial(rows_kernel, [len(g) for g in groups], list(moved)),
         name="mix_rows",
         grid=(own // SUB,),
         in_specs=[pl.BlockSpec(m.shape, lambda i: (0, 0)) for m in [col, *mats]]
-        + [pl.BlockSpec((x.shape[0], SUB, width), lambda i: (0, i, 0)) for x in blocks],
+        + [pl.BlockSpec((x.shape[0], SUB, width), lambda i: (0, i, 0)) for x in [*blocks, *moved.values()]],
         out_specs=pl.BlockSpec((SUB, rows, width), lambda i: (i, 0, 0)),
         out_shape=jax.ShapeDtypeStruct((own, rows, width), F32),
         compiler_params=params(36),
         cost_estimate=cost(4 * own * depth * width * (width + rows), 4 * own * width * (depth + rows)),
-    )(col, *mats, *blocks)
+    )(col, *mats, *blocks, *moved.values())
 
 
 def finish_kernel(count, mat_ref, base_ref, *rest):
@@ -474,52 +554,62 @@
     me = lax.axis_index("tile").astype(jnp.int32)
     half_wind = jnp.broadcast_to((0.5 * wind[0]).reshape(SUB, blocks).T[:, :, None], (blocks, SUB, LANES))
     inside = jnp.stack([me != 0, me != devices - 1]).astype(F32)
-    middle = rows - 4 * HALO
-    chunks = (
-        ((2 * HALO, middle),),
-        ((HALO, HALO), (rows - 2 * HALO, HALO)),
-        ((0, HALO), (rows - HALO, HALO)),
-    )
+    half = rows // 2
+    side = half - FIRST // 2 - HALO
+    cuts = ((half - FIRST // 2, FIRST), (HALO, side), (half + FIRST // 2, side))
+    chunks = tuple((c,) for c in cuts) + (((0, HALO), (rows - HALO, HALO)),)
     one = me.reshape(1)
-    mids, inner, far, near = pieces(raw, kappa, one)
+    far = far_edge(raw, kappa, one)
+    *parts, near, kappa = pieces(raw, kappa, cuts, one)
 
     def earlier(x):
         return lax.ppermute(x, "win", [(i + 1, i) for i in range(windows - 1)])
 
     apart = [(t, t + 1) for t in range(1, devices - 1, 2)] + [(t + 1, t) for t in range(1, devices - 1, 2)]
     far_in = lax.ppermute(far, "tile", apart)
-    follow_mids = earlier(mids)
+    follow = [earlier(parts[0])]
+    follow.append(earlier(parts[1]))
     near_in = lax.ppermute(near, "tile", [(t, t ^ 1) for t in range(devices)])
-    level_mat, *row_mats = ordered(chunks, devices, one, vertical_cov, row_cov)
-
-    def exchange(parts):
-        got = [parts[0]] + [None] * (devices - 1)
+    level_mat = order_levels(devices, one, vertical_cov)
+
+    def exchange(mixed, without={}):
+        got = [mixed[0]] + [None] * (devices - 1)
         for span in (range(devices // 2, devices), range(devices // 2 - 1, 0, -1)):
             for s in span:
-                got[s] = lax.ppermute(parts[s], "tile", [(t, t ^ s) for t in range(devices)])
+                pairs = [(t, t ^ s) for t in range(devices) if t not in without.get(s, ())]
+                got[s] = lax.ppermute(mixed[s], "tile", pairs)
         return got
 
-    own = [mids, inner, far, near]
-    ev = steps([2 * HALO], middle, one, inside, half_wind, kappa, own)
-    mixed = mix_levels(devices, one, ev, [follow_mids], level_mat)
-    first = exchange(mixed)
-
-    *own, _ = lax.optimization_barrier((mids, inner, far, near, mixed[0]))
-    follow_inner = earlier(own[1])
-    follow_far, follow_near = earlier(own[2]), earlier(own[3])
-    ev = steps([HALO, rows - 2 * HALO], HALO, one, inside, half_wind, kappa, own)
-    mixed = mix_levels(devices, one, ev, [follow_inner], level_mat)
-    second = exchange(mixed)
-
-    *own, _ = lax.optimization_barrier((*own, mixed[0]))
-    ev = steps([0, rows - HALO], HALO, one, inside, half_wind, kappa, own, [far_in, near_in])
+    cross = devices // 2 + 1
+    movers = [devices // 2 - 1, devices // 2] if devices == 8 and RELAY else []
+    groups = []
+    own = [*parts, far, near]
+    for j, (first, count) in enumerate(cuts):
+        ev = steps([first], count, one, inside, half_wind, kappa, cuts, own)
+        mixed = mix_levels(devices, one, ev, [follow[j]], level_mat)
+        groups.append(exchange(mixed, {cross: movers} if j == 1 else {}))
+        if j == 1 and movers:
+            aside = lax.ppermute(mixed[cross], "tile", [(t, t ^ 1) for t in movers])
+        *own, _ = lax.optimization_barrier((*own, mixed[0]))
+        if j == 0:
+            follow.append(earlier(own[2]))
+        elif j == 1:
+            row, col, _ = lax.optimization_barrier((row_cov, column_cov, mixed[0]))
+            col_mat, *row_mats = order_rest(chunks, devices, one, row, col)
+            follow_edges = [earlier(own[3]), earlier(own[4])]
+    moved = {}
+    if movers:
+        aside = lax.ppermute(aside, "tile", [(t ^ 1, t ^ cross) for t in movers])
+        moved = {devices + cross: aside}
+
+    ev = steps([0, rows - HALO], HALO, one, inside, half_wind, kappa, cuts, own, [far_in, near_in])
     halves = levels // devices // SUB
-    mixed = mix_levels(devices * halves, one, ev, [follow_far, follow_near], level_mat, column_cov)
-    base = mix_rows(column_cov, row_mats[:2], [first, second])
+    mixed = mix_levels(devices * halves, one, ev, follow_edges, level_mat, col_mat)
+    base = mix_rows(col_mat, row_mats[:3], groups, moved)
     out = None
     for h in range(halves):
         last = exchange(mixed[h::halves])
-        out = finish(h, row_mats[2], base, last, out)
+        out = finish(h, row_mats[3], base, last, out)
     return out[None]
 
 
@@ -570,7 +660,7 @@
     devices = lax.axis_size("tile")
     own = levels // devices
     fits = (
-        rows > 4 * HALO
+        rows >= 2 * HALO + 2 * SUB + FIRST
         and rows % SUB == 0
         and levels % (2 * SUB) == 0
         and levels % devices == 0
@@ -585,4 +675,6 @@
 def solution(mesh):
     in_specs = (P("win", None, "tile", None), P("win", "tile", None), P("win", None), P(), P(), P())
     out_specs = P("win", "tile", None, None)
+
+
     return jax.shard_map(body, mesh=mesh, in_specs=in_specs, out_specs=out_specs, check_vma=False)

time: 348 us -> 330 us (0.948)
  the two profiles are of different devices: /device:TPU:14 before, /device:TPU:10 now
where the time goes in v2:
time: 330 us; the launch traced here: 329 us
  waiting for transfers between devices  170 us (52%)
  Pallas kernels  89.7 us (27%)
  starting transfers between devices  67 us (20%)
    ppermute x35, waiting for transfers between devices, exchange(): got[s] = lax.ppermute(mixed[s], 'tile', pairs)  157 us
    ppermute x35, starting transfers between devices, exchange(): got[s] = lax.ppermute(mixed[s], 'tile', pairs)  49.4 us
    pallas_call x4, Pallas kernels, steps(): pl.pallas_call(functools.partial(steps_kernel, plans, [f - HALO for f in...  47.6 us
    ppermute x5, waiting for transfers between devices, earlier(): return lax.ppermute(x, 'win', [(i + 1, i) for i in range(windows - 1)])  13.8 us
    ppermute x5, starting transfers between devices, earlier(): return lax.ppermute(x, 'win', [(i + 1, i) for i in range(windows - 1)])  12.7 us
    pallas_call x4, Pallas kernels, mix_levels(): pl.pallas_call(functools.partial(levels_kernel, edges, col is not None),...  11.3 us
    pallas_call x1, Pallas kernels, pieces(): pl.pallas_call(functools.partial(pieces_kernel, cuts), name='pieces', gri...  11 us
    pallas_call x1, Pallas kernels, mix_rows(): pl.pallas_call(functools.partial(rows_kernel, [len(g) for g in groups], l...  7.64 us
  transfers between devices with their start and end apart: 42, of which 24 were waited for; matrix products, arithmetic and copies ran while one was open for 0% of the time, Pallas kernels for 23%

profile of v2, /device:TPU:10, one launch (start us, length us, event | category | flops | bytes accessed | tf_op | source)
XLA Modules:
  0.0 329.3 jit_solution(5754033481066404402)
XLA Ops:
  0.0 11.0 %pieces.1 = (f32[4,16,8,512]{3,2,1,0:T(8,128)}, f32[8,16,8,512]{3,2,1,0:T(8,128)}, f32[8,16,8,512]{3,2,1,0:T(8,128)}, f32[97,8,512]{2,1,0:T(8,128)}, f32[32,512]{1,0:T(8,128)}) custom-call(s32[1]{0:T(128)} %bitcast.me_ref, f32[8,16,32,512]{3,2,1,0:T(8,128)} %bitcast.24, f32[32,512]{1,0:T(8,128)} %bitcast.27), custom_call_target="tpu_custom_call" | custom-call | flops 4294967296 | bytes 16777216 | tf_op jit(solution)/shard_map/pieces/pallas_call | solution.py:168
  15.8 5.3 %far_edge.1.rest_3_.rest_2_ = f32[97,8,512]{2,1,0:T(8,128)} custom-call(s32[1]{0:T(128)} %bitcast.me_ref, f32[8,16,32,512]{3,2,1,0:T(8,128)} %bitcast.25, f32[8,16,32,512]{3,2,1,0:T(8,128)} %bitcast.26, f32[32,512]{1,0:T(8,128)} %bitcast.28), custom_call_target="tpu_custom_call" | custom-call | bytes 6291456 | tf_op jit(solution)/shard_map/far_edge/pallas_call | solution.py:116
  21.1 3.3 collective-permute-start.24
  26.7 7.6 %shard_map.64.ev_ref = f32[4,16,8,512]{3,2,1,0:T(8,128)S(1)} custom-call(s32[1]{0:T(128)} %bitcast.me_ref, f32[2]{0:T(128)S(1)} %add_convert_fusion.inside_ref, f32[16,8,128]{2,1,0:T(8,128)S(1)} %broadcast_in_dim.4.hw_ref, f32[32,512]{1,0:T(8,128)S(1)} %copy-done.5, f32[64,8,512]{2,1,0:T(8,128)S(1)} %bitcast.21, f32[128,8,512]{2,1,0:T(8,128)S(1)} %bitcast.11, ...), custom_call_target="tpu_custom_call" | custom-call | flops 49545216 | bytes 5242880 | tf_op jit(solution)/shard_map/pallas_call | solution.py:347
  34.2 13.8 %collective-permute-done.rest_0_ = f32[64,8,512]{2,1,0:T(8,128)} collective-permute-done((f32[64,8,512]{2,1,0:T(8,128)}, f32[64,8,512]{2,1,0:T(8,128)}, u32[]{:S(2)}, u32[]{:S(2)}) %collective-permute-start) | collective-permute-done | bytes 1048608 | tf_op jit(solution)/shard_map/ppermute | solution.py:566
  49.7 4.1 %collective-permute-start.16 = (f32[128,8,512]{2,1,0:T(8,128)S(1)}, f32[128,8,512]{2,1,0:T(8,128)S(1)}, u32[]{:S(2)}, u32[]{:S(2)}) collective-permute-start(f32[128,8,512]{2,1,0:T(8,128)S(1)} %bitcast.16), channel_id=1, source_target_pairs={{8,0},{16,8},{24,16},{9,1},{17,9},{25,17},{10,2},{18,10},{26,18},{... | collective-permute-start | bytes 6291464 | tf_op jit(solution)/shard_map/ppermute | solution.py:566
  55.9 42.6 %collective-permute-done.2.rest_4_ = f32[4,16,512]{2,1,0:T(8,128)S(1)} collective-permute-done((f32[4,16,512]{2,1,0:T(8,128)S(1)}, f32[4,16,512]{2,1,0:T(8,128)S(1)}, u32[]{:S(2)}, u32[]{:S(2)}) %collective-permute-start.2) | collective-permute-done | bytes 131104 | tf_op jit(solution)/shard_map/ppermute | solution.py:580
  98.6 5.4 %collective-permute-done.3.rest_5_ = f32[4,16,512]{2,1,0:T(8,128)S(1)} collective-permute-done((f32[4,16,512]{2,1,0:T(8,128)S(1)}, f32[4,16,512]{2,1,0:T(8,128)S(1)}, u32[]{:S(2)}, u32[]{:S(2)}) %collective-permute-start.3) | collective-permute-done | bytes 131104 | tf_op jit(solution)/shard_map/ppermute | solution.py:580
  105.4 4.5 %collective-permute-done.4.rest_6_ = f32[4,16,512]{2,1,0:T(8,128)S(1)} collective-permute-done((f32[4,16,512]{2,1,0:T(8,128)S(1)}, f32[4,16,512]{2,1,0:T(8,128)S(1)}, u32[]{:S(2)}, u32[]{:S(2)}) %collective-permute-start.4) | collective-permute-done | bytes 131104 | tf_op jit(solution)/shard_map/ppermute | solution.py:580
  112.5 3.8 %collective-permute-done.5.rest_7_ = f32[4,16,512]{2,1,0:T(8,128)S(1)} collective-permute-done((f32[4,16,512]{2,1,0:T(8,128)S(1)}, f32[4,16,512]{2,1,0:T(8,128)S(1)}, u32[]{:S(2)}, u32[]{:S(2)}) %collective-permute-start.5) | collective-permute-done | bytes 131104 | tf_op jit(solution)/shard_map/ppermute | solution.py:580
  116.2 3.3 collective-permute-start.6
  120.0 10.6 %shard_map.65.ev_ref = f32[8,16,8,512]{3,2,1,0:T(8,128)S(1)} custom-call(s32[1]{0:T(128)} %bitcast.me_ref, f32[2]{0:T(128)S(1)} %add_convert_fusion.inside_ref, f32[16,8,128]{2,1,0:T(8,128)S(1)} %broadcast_in_dim.4.hw_ref, f32[32,512]{1,0:T(8,128)S(1)} %copy-done.5, f32[64,8,512]{2,1,0:T(8,128)S(1)} %bitcast.22, f32[128,8,512]{2,1,0:T(8,128)S(1)} %bitcast.12, ...), custom_call_target="tpu_custom_call" | custom-call | flops 71565312 | bytes 7340032 | tf_op jit(solution)/shard_map/pallas_call | solution.py:347
  130.6 3.1 mix_levels.5
  138.2 7.2 %collective-permute-done.8.rest_10_ = f32[4,16,512]{2,1,0:T(8,128)S(1)} collective-permute-done((f32[4,16,512]{2,1,0:T(8,128)S(1)}, f32[4,16,512]{2,1,0:T(8,128)S(1)}, u32[]{:S(2)}, u32[]{:S(2)}) %collective-permute-start.8) | collective-permute-done | bytes 131104 | tf_op jit(solution)/shard_map/ppermute | solution.py:580
  148.6 7.6 %collective-permute-done.9.rest_12_ = f32[8,16,512]{2,1,0:T(8,128)S(1)} collective-permute-done((f32[8,16,512]{2,1,0:T(8,128)S(1)}, f32[8,16,512]{2,1,0:T(8,128)S(1)}, u32[]{:S(2)}, u32[]{:S(2)}) %collective-permute-start.9) | collective-permute-done | bytes 262176 | tf_op jit(solution)/shard_map/ppermute | solution.py:580
  157.0 3.2 collective-permute-start.12
  160.2 7.7 %collective-permute-done.11.rest_14_ = f32[8,16,512]{2,1,0:T(8,128)S(1)} collective-permute-done((f32[8,16,512]{2,1,0:T(8,128)S(1)}, f32[8,16,512]{2,1,0:T(8,128)S(1)}, u32[]{:S(2)}, u32[]{:S(2)}) %collective-permute-start.11) | collective-permute-done | bytes 262176 | tf_op jit(solution)/shard_map/ppermute | solution.py:580
  172.8 10.8 %shard_map.66.ev_ref = f32[8,16,8,512]{3,2,1,0:T(8,128)S(1)} custom-call(s32[1]{0:T(128)} %bitcast.me_ref, f32[2]{0:T(128)S(1)} %add_convert_fusion.inside_ref, f32[16,8,128]{2,1,0:T(8,128)S(1)} %broadcast_in_dim.4.hw_ref, f32[32,512]{1,0:T(8,128)S(1)} %copy-done.5, f32[64,8,512]{2,1,0:T(8,128)S(1)} %bitcast.23, f32[128,8,512]{2,1,0:T(8,128)S(1)} %bitcast.13, ...), custom_call_target="tpu_custom_call" | custom-call | flops 71565312 | bytes 7340032 | tf_op jit(solution)/shard_map/pallas_call | solution.py:347
  185.9 9.1 %collective-permute-done.13.rest_16_ = f32[8,16,512]{2,1,0:T(8,128)S(1)} collective-permute-done((f32[8,16,512]{2,1,0:T(8,128)S(1)}, f32[8,16,512]{2,1,0:T(8,128)S(1)}, u32[]{:S(2)}, u32[]{:S(2)}) %collective-permute-start.13) | collective-permute-done | bytes 262176 | tf_op jit(solution)/shard_map/ppermute | solution.py:580
  195.0 5.6 %collective-permute-done.14.rest_17_ = f32[8,16,512]{2,1,0:T(8,128)S(1)} collective-permute-done((f32[8,16,512]{2,1,0:T(8,128)S(1)}, f32[8,16,512]{2,1,0:T(8,128)S(1)}, u32[]{:S(2)}, u32[]{:S(2)}) %collective-permute-start.14) | collective-permute-done | bytes 262176 | tf_op jit(solution)/shard_map/ppermute | solution.py:580
  200.6 5.1 %collective-permute-done.15.rest_18_ = f32[8,16,512]{2,1,0:T(8,128)S(1)} collective-permute-done((f32[8,16,512]{2,1,0:T(8,128)S(1)}, f32[8,16,512]{2,1,0:T(8,128)S(1)}, u32[]{:S(2)}, u32[]{:S(2)}) %collective-permute-start.15) | collective-permute-done | bytes 262176 | tf_op jit(solution)/shard_map/ppermute | solution.py:580
  213.5 18.7 %shard_map.67.ev_ref = f32[12,16,8,512]{3,2,1,0:T(8,128)S(1)} custom-call(s32[1]{0:T(128)} %bitcast.me_ref, f32[2]{0:T(128)S(1)} %add_convert_fusion.inside_ref, f32[16,8,128]{2,1,0:T(8,128)S(1)} %broadcast_in_dim.4.hw_ref, f32[32,512]{1,0:T(8,128)S(1)} %copy-done.5, f32[128,8,512]{2,1,0:T(8,128)S(1)} %bitcast.14, f32[128,8,512]{2,1,0:T(8,128)S(1)} %bitcast.19, ...), custom_call_target="tpu_custom_call" | custom-call | flops 121110528 | bytes 12582912 | tf_op jit(solution)/shard_map/pallas_call | solution.py:347
  232.2 5.2 %mix_levels.7 = (f32[12,8,512]{2,1,0:T(8,128)S(1)}, f32[12,8,512]{2,1,0:T(8,128)S(1)}, f32[12,8,512]{2,1,0:T(8,128)S(1)}, f32[12,8,512]{2,1,0:T(8,128)S(1)}, f32...) custom-call(s32[1]{0:T(128)} %bitcast.me_ref, ...), custom_call_target="tpu_custom_call" | custom-call | flops 402653184 | bytes 9437184 | tf_op jit(solution)/shard_map/mix_levels/pallas_call | solution.py:456
  245.0 5.8 %collective-permute-done.22.rest_25_ = f32[8,16,512]{2,1,0:T(8,128)S(1)} collective-permute-done((f32[8,16,512]{2,1,0:T(8,128)S(1)}, f32[8,16,512]{2,1,0:T(8,128)S(1)}, u32[]{:S(2)}, u32[]{:S(2)}) %collective-permute-start.22) | collective-permute-done | bytes 262176 | tf_op jit(solution)/shard_map/ppermute | solution.py:580
  250.8 4.6 %collective-permute-done.23.rest_26_ = f32[8,16,512]{2,1,0:T(8,128)S(1)} collective-permute-done((f32[8,16,512]{2,1,0:T(8,128)S(1)}, f32[8,16,512]{2,1,0:T(8,128)S(1)}, u32[]{:S(2)}, u32[]{:S(2)}) %collective-permute-start.23) | collective-permute-done | bytes 262176 | tf_op jit(solution)/shard_map/ppermute | solution.py:580
  266.0 13.6 %collective-permute-done.38.rest_4_ = f32[12,8,512]{2,1,0:T(8,128)S(1)} collective-permute-done((f32[12,8,512]{2,1,0:T(8,128)S(1)}, f32[12,8,512]{2,1,0:T(8,128)S(1)}, u32[]{:S(2)}, u32[]{:S(2)}) %collective-permute-start.38) | collective-permute-done | bytes 196640 | tf_op jit(solution)/shard_map/ppermute | solution.py:580
  279.6 3.9 %collective-permute-start.31 = (f32[12,8,512]{2,1,0:T(8,128)S(1)}, f32[12,8,512]{2,1,0:T(8,128)S(1)}, u32[]{:S(2)}, u32[]{:S(2)}) collective-permute-start(f32[12,8,512]{2,1,0:T(8,128)S(1)} %get-tuple-element.125), channel_id=1, source_target_pairs={{0,4},{1,5},{2,6},{3,7},{4,0},{5,1},{6,2},{7,3},{8,12},{9,13},{10,... | collective-permute-start | bytes 589832 | tf_op jit(solution)/shard_map/ppermute | solution.py:580
  283.4 11.2 %collective-permute-done.39.rest_5_ = f32[12,8,512]{2,1,0:T(8,128)S(1)} collective-permute-done((f32[12,8,512]{2,1,0:T(8,128)S(1)}, f32[12,8,512]{2,1,0:T(8,128)S(1)}, u32[]{:S(2)}, u32[]{:S(2)}) %collective-permute-start.39) | collective-permute-done | bytes 196640 | tf_op jit(solution)/shard_map/ppermute | solution.py:580
  294.7 4.3 %collective-permute-start.32 = (f32[12,8,512]{2,1,0:T(8,128)S(1)}, f32[12,8,512]{2,1,0:T(8,128)S(1)}, u32[]{:S(2)}, u32[]{:S(2)}) collective-permute-start(f32[12,8,512]{2,1,0:T(8,128)S(1)} %get-tuple-element.126), channel_id=1, source_target_pairs={{0,5},{1,4},{2,7},{3,6},{4,1},{5,0},{6,3},{7,2},{8,13},{9,12},{10,... | collective-permute-start | bytes 589832 | tf_op jit(solution)/shard_map/ppermute | solution.py:580
  299.0 7.9 %collective-permute-done.40.rest_6_ = f32[12,8,512]{2,1,0:T(8,128)S(1)} collective-permute-done((f32[12,8,512]{2,1,0:T(8,128)S(1)}, f32[12,8,512]{2,1,0:T(8,128)S(1)}, u32[]{:S(2)}, u32[]{:S(2)}) %collective-permute-start.40) | collective-permute-done | bytes 196640 | tf_op jit(solution)/shard_map/ppermute | solution.py:580
  306.9 4.1 %collective-permute-done.41.rest_7_ = f32[12,8,512]{2,1,0:T(8,128)S(1)} collective-permute-done((f32[12,8,512]{2,1,0:T(8,128)S(1)}, f32[12,8,512]{2,1,0:T(8,128)S(1)}, u32[]{:S(2)}, u32[]{:S(2)}) %collective-permute-start.41) | collective-permute-done | bytes 196640 | tf_op jit(solution)/shard_map/ppermute | solution.py:580
  312.8 7.6 %mix_rows.1.base_ref = f32[16,256,512]{2,1,0:T(8,128)S(1)} custom-call(bf16[512,512]{1,0:T(8,128)(2,1)S(1)} %get-tuple-element.86.col_ref.rest_2_, bf16[256,64]{1,0:T(8,128)(2,1)S(1)} %get-tuple-element.87.rest_0_, bf16[256,128]{1,0:T(8,128)(2,1)S(1)} %get-tuple-element.88.rest_1_, bf16[256,128]{1,0:T(8,128)(2,1)S(1)} %get-tuple-element.89.rest_2_, ...), custom_call_target="tpu_custom_call" | custom-call | flops 4026531840 | bytes 13631488 | tf_op jit(solution)/shard_map/mix_rows/pallas_call | solution.py:508
  (92 shorter events, 67.4 us)
Async XLA Ops:
  11.0 108.5 %collective-permute-start.1 = (f32[128,8,512]{2,1,0:T(8,128)}, f32[128,8,512]{2,1,0:T(8,128)}, u32[]{:S(2)}, u32[]{:S(2)}) collective-permute-start(f32[128,8,512]{2,1,0:T(8,128)} %bitcast.10), channel_id=1, source_target_pairs={{8,0},{16,8},{24,16},{9,1},{17,9},{25,17},{10,2},{18,10},{26,18},{... | collective-permute-start | bytes 6291464 | tf_op jit(solution)/shard_map/ppermute | solution.py:566
  13.0 35.0 %collective-permute-start = (f32[64,8,512]{2,1,0:T(8,128)}, f32[64,8,512]{2,1,0:T(8,128)}, u32[]{:S(2)}, u32[]{:S(2)}) collective-permute-start(f32[64,8,512]{2,1,0:T(8,128)} %bitcast.20), channel_id=1, source_target_pairs={{8,0},{16,8},{24,16},{9,1},{17,9},{25,17},{10,2},{18,10},{26,18},{... | collective-permute-start | bytes 3145736 | tf_op jit(solution)/shard_map/ppermute | solution.py:566
  21.1 126.2 %collective-permute-start.24 = (f32[97,8,512]{2,1,0:T(8,128)}, f32[97,8,512]{2,1,0:T(8,128)}, u32[]{:S(2)}, u32[]{:S(2)}) collective-permute-start(f32[97,8,512]{2,1,0:T(8,128)} %far_edge.1.rest_3_.rest_2_), channel_id=1, source_target_pairs={{1,2},{3,4},{5,6},{2,1},{4,3},{6,5},{9,10},{11,12},{13,14},{10,9},... | collective-permute-start | bytes 4767752 | tf_op jit(solution)/shard_map/ppermute | solution.py:569
  49.7 120.5 %collective-permute-start.16 = (f32[128,8,512]{2,1,0:T(8,128)S(1)}, f32[128,8,512]{2,1,0:T(8,128)S(1)}, u32[]{:S(2)}, u32[]{:S(2)}) collective-permute-start(f32[128,8,512]{2,1,0:T(8,128)S(1)} %bitcast.16), channel_id=1, source_target_pairs={{8,0},{16,8},{24,16},{9,1},{17,9},{25,17},{10,2},{18,10},{26,18},{... | collective-permute-start | bytes 6291464 | tf_op jit(solution)/shard_map/ppermute | solution.py:566
  53.9 94.6 %collective-permute-start.25 = (f32[97,8,512]{2,1,0:T(8,128)S(1)}, f32[97,8,512]{2,1,0:T(8,128)S(1)}, u32[]{:S(2)}, u32[]{:S(2)}) collective-permute-start(f32[97,8,512]{2,1,0:T(8,128)S(1)} %copy-done.3), channel_id=1, source_target_pairs={{0,1},{1,0},{2,3},{3,2},{4,5},{5,4},{6,7},{7,6},{8,9},{9,8},{10,11... | collective-permute-start | bytes 4767752 | tf_op jit(solution)/shard_map/ppermute | solution.py:572
  55.4 43.2 %collective-permute-start.2 = (f32[4,16,512]{2,1,0:T(8,128)S(1)}, f32[4,16,512]{2,1,0:T(8,128)S(1)}, u32[]{:S(2)}, u32[]{:S(2)}) collective-permute-start(f32[4,16,512]{2,1,0:T(8,128)S(1)} %get-tuple-element.90), channel_id=1, source_target_pairs={{0,1},{1,0},{2,3},{3,2},{4,5},{5,4},{6,7},{7,6},{8,9},{9,8},{10,11... | collective-permute-start | bytes 393224 | tf_op jit(solution)/shard_map/ppermute | solution.py:580
  116.2 17.5 %collective-permute-start.6 = (f32[4,16,512]{2,1,0:T(8,128)S(1)}, f32[4,16,512]{2,1,0:T(8,128)S(1)}, u32[]{:S(2)}, u32[]{:S(2)}) collective-permute-start(f32[4,16,512]{2,1,0:T(8,128)S(1)} %get-tuple-element.94), channel_id=1, source_target_pairs={{0,5},{1,4},{2,7},{3,6},{4,1},{5,0},{6,3},{7,2},{8,13},{9,12},{10,... | collective-permute-start | bytes 393224 | tf_op jit(solution)/shard_map/ppermute | solution.py:580
  119.5 16.1 %collective-permute-start.7 = (f32[4,16,512]{2,1,0:T(8,128)S(1)}, f32[4,16,512]{2,1,0:T(8,128)S(1)}, u32[]{:S(2)}, u32[]{:S(2)}) collective-permute-start(f32[4,16,512]{2,1,0:T(8,128)S(1)} %get-tuple-element.95), channel_id=1, source_target_pairs={{0,6},{1,7},{2,4},{3,5},{4,2},{5,3},{6,0},{7,1},{8,14},{9,15},{10,... | collective-permute-start | bytes 393224 | tf_op jit(solution)/shard_map/ppermute | solution.py:580
  133.7 76.0 %collective-permute-start.26 = (f32[97,8,512]{2,1,0:T(8,128)S(1)}, f32[97,8,512]{2,1,0:T(8,128)S(1)}, u32[]{:S(2)}, u32[]{:S(2)}) collective-permute-start(f32[97,8,512]{2,1,0:T(8,128)S(1)} %copy-done.2), channel_id=1, source_target_pairs={{8,0},{16,8},{24,16},{9,1},{17,9},{25,17},{10,2},{18,10},{26,18},{... | collective-permute-start | bytes 4767752 | tf_op jit(solution)/shard_map/ppermute | solution.py:566
  145.4 65.7 %collective-permute-start.27 = (f32[97,8,512]{2,1,0:T(8,128)S(1)}, f32[97,8,512]{2,1,0:T(8,128)S(1)}, u32[]{:S(2)}, u32[]{:S(2)}) collective-permute-start(f32[97,8,512]{2,1,0:T(8,128)S(1)} %copy-done.3), channel_id=1, source_target_pairs={{8,0},{16,8},{24,16},{9,1},{17,9},{25,17},{10,2},{18,10},{26,18},{... | collective-permute-start | bytes 4767752 | tf_op jit(solution)/shard_map/ppermute | solution.py:566
  157.0 27.8 %collective-permute-start.12 = (f32[8,16,512]{2,1,0:T(8,128)S(1)}, f32[8,16,512]{2,1,0:T(8,128)S(1)}, u32[]{:S(2)}, u32[]{:S(2)}) collective-permute-start(f32[8,16,512]{2,1,0:T(8,128)S(1)} %get-tuple-element.100), channel_id=1, source_target_pairs={{0,4},{1,5},{2,6},{3,7},{4,0},{5,1},{6,2},{7,3},{8,12},{9,13},{10,... | collective-permute-start | bytes 786440 | tf_op jit(solution)/shard_map/ppermute | solution.py:580
  167.9 27.1 %collective-permute-start.13 = (f32[8,16,512]{2,1,0:T(8,128)S(1)}, f32[8,16,512]{2,1,0:T(8,128)S(1)}, u32[]{:S(2)}, u32[]{:S(2)}) collective-permute-start(f32[8,16,512]{2,1,0:T(8,128)S(1)} %get-tuple-element.101), channel_id=1, source_target_pairs={{0,5},{1,4},{2,7},{3,6},{4,1},{5,0},{6,3},{7,2},{8,13},{9,12},{10,... | collective-permute-start | bytes 786440 | tf_op jit(solution)/shard_map/ppermute | solution.py:580
  170.2 30.4 %collective-permute-start.14 = (f32[8,16,512]{2,1,0:T(8,128)S(1)}, f32[8,16,512]{2,1,0:T(8,128)S(1)}, u32[]{:S(2)}, u32[]{:S(2)}) collective-permute-start(f32[8,16,512]{2,1,0:T(8,128)S(1)} %get-tuple-element.102), channel_id=1, source_target_pairs={{0,6},{1,7},{2,4},{3,5},{4,2},{5,3},{6,0},{7,1},{8,14},{9,15},{10,... | collective-permute-start | bytes 786440 | tf_op jit(solution)/shard_map/ppermute | solution.py:580
  184.8 20.9 %collective-permute-start.15 = (f32[8,16,512]{2,1,0:T(8,128)S(1)}, f32[8,16,512]{2,1,0:T(8,128)S(1)}, u32[]{:S(2)}, u32[]{:S(2)}) collective-permute-start(f32[8,16,512]{2,1,0:T(8,128)S(1)} %get-tuple-element.103), channel_id=1, source_target_pairs={{0,7},{1,6},{2,5},{3,4},{4,3},{5,2},{6,1},{7,0},{8,15},{9,14},{10,... | collective-permute-start | bytes 786440 | tf_op jit(solution)/shard_map/ppermute | solution.py:580
  195.0 12.0 %collective-permute-start.17 = (f32[8,16,512]{2,1,0:T(8,128)S(1)}, f32[8,16,512]{2,1,0:T(8,128)S(1)}, u32[]{:S(2)}, u32[]{:S(2)}) collective-permute-start(f32[8,16,512]{2,1,0:T(8,128)S(1)} %get-tuple-element.110), channel_id=1, source_target_pairs={{0,1},{1,0},{2,3},{3,2},{4,5},{5,4},{6,7},{7,6},{8,9},{9,8},{10,11... | collective-permute-start | bytes 786440 | tf_op jit(solution)/shard_map/ppermute | solution.py:580
  205.7 31.7 %collective-permute-start.19 = (f32[8,16,512]{2,1,0:T(8,128)S(1)}, f32[8,16,512]{2,1,0:T(8,128)S(1)}, u32[]{:S(2)}, u32[]{:S(2)}) collective-permute-start(f32[8,16,512]{2,1,0:T(8,128)S(1)} %get-tuple-element.112), channel_id=1, source_target_pairs={{0,3},{1,2},{2,1},{3,0},{4,7},{5,6},{6,5},{7,4},{8,11},{9,10},{10,... | collective-permute-start | bytes 786440 | tf_op jit(solution)/shard_map/ppermute | solution.py:580
  207.0 31.8 %collective-permute-start.20 = (f32[8,16,512]{2,1,0:T(8,128)S(1)}, f32[8,16,512]{2,1,0:T(8,128)S(1)}, u32[]{:S(2)}, u32[]{:S(2)}) collective-permute-start(f32[8,16,512]{2,1,0:T(8,128)S(1)} %get-tuple-element.113), channel_id=1, source_target_pairs={{0,4},{1,5},{2,6},{3,7},{4,0},{5,1},{6,2},{7,3},{8,12},{9,13},{10,... | collective-permute-start | bytes 786440 | tf_op jit(solution)/shard_map/ppermute | solution.py:580
  209.6 34.8 %collective-permute-start.21 = (f32[8,16,512]{2,1,0:T(8,128)S(1)}, f32[8,16,512]{2,1,0:T(8,128)S(1)}, u32[]{:S(2)}, u32[]{:S(2)}) collective-permute-start(f32[8,16,512]{2,1,0:T(8,128)S(1)} %get-tuple-element.114), channel_id=1, source_target_pairs={{0,5},{1,4},{2,7},{3,6},{4,1},{5,0},{6,3},{7,2},{8,13},{9,12},{10,... | collective-permute-start | bytes 786440 | tf_op jit(solution)/shard_map/ppermute | solution.py:580
  209.7 41.1 %collective-permute-start.22 = (f32[8,16,512]{2,1,0:T(8,128)S(1)}, f32[8,16,512]{2,1,0:T(8,128)S(1)}, u32[]{:S(2)}, u32[]{:S(2)}) collective-permute-start(f32[8,16,512]{2,1,0:T(8,128)S(1)} %get-tuple-element.115), channel_id=1, source_target_pairs={{0,6},{1,7},{2,4},{3,5},{4,2},{5,3},{6,0},{7,1},{8,14},{9,15},{10,... | collective-permute-start | bytes 786440 | tf_op jit(solution)/shard_map/ppermute | solution.py:580
  211.1 44.3 %collective-permute-start.23 = (f32[8,16,512]{2,1,0:T(8,128)S(1)}, f32[8,16,512]{2,1,0:T(8,128)S(1)}, u32[]{:S(2)}, u32[]{:S(2)}) collective-permute-start(f32[8,16,512]{2,1,0:T(8,128)S(1)} %get-tuple-element.116), channel_id=1, source_target_pairs={{0,7},{1,6},{2,5},{3,4},{4,3},{5,2},{6,1},{7,0},{8,15},{9,14},{10,... | collective-permute-start | bytes 786440 | tf_op jit(solution)/shard_map/ppermute | solution.py:580
  237.4 18.0 %collective-permute-start.28 = (f32[12,8,512]{2,1,0:T(8,128)S(1)}, f32[12,8,512]{2,1,0:T(8,128)S(1)}, u32[]{:S(2)}, u32[]{:S(2)}) collective-permute-start(f32[12,8,512]{2,1,0:T(8,128)S(1)} %get-tuple-element.122), channel_id=1, source_target_pairs={{0,1},{1,0},{2,3},{3,2},{4,5},{5,4},{6,7},{7,6},{8,9},{9,8},{10,11... | collective-permute-start | bytes 589832 | tf_op jit(solution)/shard_map/ppermute | solution.py:580
  238.8 19.1 %collective-permute-start.29 = (f32[12,8,512]{2,1,0:T(8,128)S(1)}, f32[12,8,512]{2,1,0:T(8,128)S(1)}, u32[]{:S(2)}, u32[]{:S(2)}) collective-permute-start(f32[12,8,512]{2,1,0:T(8,128)S(1)} %get-tuple-element.123), channel_id=1, source_target_pairs={{0,2},{1,3},{2,0},{3,1},{4,6},{5,7},{6,4},{7,5},{8,10},{9,11},{10,... | collective-permute-start | bytes 589832 | tf_op jit(solution)/shard_map/ppermute | solution.py:580
  244.4 14.6 %collective-permute-start.35 = (f32[12,8,512]{2,1,0:T(8,128)S(1)}, f32[12,8,512]{2,1,0:T(8,128)S(1)}, u32[]{:S(2)}, u32[]{:S(2)}) collective-permute-start(f32[12,8,512]{2,1,0:T(8,128)S(1)} %get-tuple-element.130), channel_id=1, source_target_pairs={{0,1},{1,0},{2,3},{3,2},{4,5},{5,4},{6,7},{7,6},{8,9},{9,8},{10,11... | collective-permute-start | bytes 589832 | tf_op jit(solution)/shard_map/ppermute | solution.py:580
  255.4 24.2 %collective-permute-start.38 = (f32[12,8,512]{2,1,0:T(8,128)S(1)}, f32[12,8,512]{2,1,0:T(8,128)S(1)}, u32[]{:S(2)}, u32[]{:S(2)}) collective-permute-start(f32[12,8,512]{2,1,0:T(8,128)S(1)} %get-tuple-element.133), channel_id=1, source_target_pairs={{0,4},{1,5},{2,6},{3,7},{4,0},{5,1},{6,2},{7,3},{8,12},{9,13},{10,... | collective-permute-start | bytes 589832 | tf_op jit(solution)/shard_map/ppermute | solution.py:580
  257.9 36.7 %collective-permute-start.39 = (f32[12,8,512]{2,1,0:T(8,128)S(1)}, f32[12,8,512]{2,1,0:T(8,128)S(1)}, u32[]{:S(2)}, u32[]{:S(2)}) collective-permute-start(f32[12,8,512]{2,1,0:T(8,128)S(1)} %get-tuple-element.134), channel_id=1, source_target_pairs={{0,5},{1,4},{2,7},{3,6},{4,1},{5,0},{6,3},{7,2},{8,13},{9,12},{10,... | collective-permute-start | bytes 589832 | tf_op jit(solution)/shard_map/ppermute | solution.py:580
  259.0 47.9 %collective-permute-start.40 = (f32[12,8,512]{2,1,0:T(8,128)S(1)}, f32[12,8,512]{2,1,0:T(8,128)S(1)}, u32[]{:S(2)}, u32[]{:S(2)}) collective-permute-start(f32[12,8,512]{2,1,0:T(8,128)S(1)} %get-tuple-element.135), channel_id=1, source_target_pairs={{0,6},{1,7},{2,4},{3,5},{4,2},{5,3},{6,0},{7,1},{8,14},{9,15},{10,... | collective-permute-start | bytes 589832 | tf_op jit(solution)/shard_map/ppermute | solution.py:580
  259.9 51.2 %collective-permute-start.41 = (f32[12,8,512]{2,1,0:T(8,128)S(1)}, f32[12,8,512]{2,1,0:T(8,128)S(1)}, u32[]{:S(2)}, u32[]{:S(2)}) collective-permute-start(f32[12,8,512]{2,1,0:T(8,128)S(1)} %get-tuple-element.136), channel_id=1, source_target_pairs={{0,7},{1,6},{2,5},{3,4},{4,3},{5,2},{6,1},{7,0},{8,15},{9,14},{10,... | collective-permute-start | bytes 589832 | tf_op jit(solution)/shard_map/ppermute | solution.py:580
  264.1 59.4 %collective-permute-start.30 = (f32[12,8,512]{2,1,0:T(8,128)S(1)}, f32[12,8,512]{2,1,0:T(8,128)S(1)}, u32[]{:S(2)}, u32[]{:S(2)}) collective-permute-start(f32[12,8,512]{2,1,0:T(8,128)S(1)} %get-tuple-element.124), channel_id=1, source_target_pairs={{0,3},{1,2},{2,1},{3,0},{4,7},{5,6},{6,5},{7,4},{8,11},{9,10},{10,... | collective-permute-start | bytes 589832 | tf_op jit(solution)/shard_map/ppermute | solution.py:580
  279.6 43.9 %collective-permute-start.31 = (f32[12,8,512]{2,1,0:T(8,128)S(1)}, f32[12,8,512]{2,1,0:T(8,128)S(1)}, u32[]{:S(2)}, u32[]{:S(2)}) collective-permute-start(f32[12,8,512]{2,1,0:T(8,128)S(1)} %get-tuple-element.125), channel_id=1, source_target_pairs={{0,4},{1,5},{2,6},{3,7},{4,0},{5,1},{6,2},{7,3},{8,12},{9,13},{10,... | collective-permute-start | bytes 589832 | tf_op jit(solution)/shard_map/ppermute | solution.py:580
  294.7 28.8 %collective-permute-start.32 = (f32[12,8,512]{2,1,0:T(8,128)S(1)}, f32[12,8,512]{2,1,0:T(8,128)S(1)}, u32[]{:S(2)}, u32[]{:S(2)}) collective-permute-start(f32[12,8,512]{2,1,0:T(8,128)S(1)} %get-tuple-element.126), channel_id=1, source_target_pairs={{0,5},{1,4},{2,7},{3,6},{4,1},{5,0},{6,3},{7,2},{8,13},{9,12},{10,... | collective-permute-start | bytes 589832 | tf_op jit(solution)/shard_map/ppermute | solution.py:580
  306.9 16.9 %collective-permute-start.33 = (f32[12,8,512]{2,1,0:T(8,128)S(1)}, f32[12,8,512]{2,1,0:T(8,128)S(1)}, u32[]{:S(2)}, u32[]{:S(2)}) collective-permute-start(f32[12,8,512]{2,1,0:T(8,128)S(1)} %get-tuple-element.127), channel_id=1, source_target_pairs={{0,6},{1,7},{2,4},{3,5},{4,2},{5,3},{6,0},{7,1},{8,14},{9,15},{10,... | collective-permute-start | bytes 589832 | tf_op jit(solution)/shard_map/ppermute | solution.py:580
  311.0 15.3 %collective-permute-start.34 = (f32[12,8,512]{2,1,0:T(8,128)S(1)}, f32[12,8,512]{2,1,0:T(8,128)S(1)}, u32[]{:S(2)}, u32[]{:S(2)}) collective-permute-start(f32[12,8,512]{2,1,0:T(8,128)S(1)} %get-tuple-element.128), channel_id=1, source_target_pairs={{0,7},{1,6},{2,5},{3,4},{4,3},{5,2},{6,1},{7,0},{8,15},{9,14},{10,... | collective-permute-start | bytes 589832 | tf_op jit(solution)/shard_map/ppermute | solution.py:580
  (20 other events, 315.8 us)

commit v3 on v2

--- a/solution.py
+++ b/solution.py
@@ -14,7 +14,6 @@
 HALO = STEPS
 LANES = 128
 FIRST = 4
-RELAY = False
 
 
 F32 = jnp.float32
@@ -74,13 +73,8 @@
     return mm(hi, order) + mm(lo, order)
 
 
-def edge_rows(source, is_top):
-    flat = turn(source)
-    return flat[:HALO] if is_top else flat[SUB - HALO :]
-
-
-def far_kernel(me_ref, top_ref, bottom_ref, kap_ref, far_ref, order):
-    _, per, _, width = top_ref.shape
+def far_kernel(me_ref, tile_ref, kap_ref, far_ref, order):
+    _, per, _, width = tile_ref.shape
     rows = kap_ref.shape[0]
     blocks = per * pl.num_programs(0)
     step = pl.program_id(0)
@@ -92,18 +86,15 @@
         kapx = reorder(kap_ref[...], order[...])
         far_ref[HALO * blocks] = jnp.where(even, kapx[:SUB, :], kapx[rows - SUB :, :])
 
-    for is_top, source in ((True, top_ref), (False, bottom_ref)):
-
-        @pl.when(even == is_top)
-        def _(is_top=is_top, source=source):
-            flat = []
-            for p in range(per):
-                flat += edge_rows([source[s, p] for s in range(SUB)], is_top)
-            moved = reorder(jnp.concatenate(flat, axis=0), order[...])
-            for p in range(per):
-                for row in range(HALO):
-                    at = (p * HALO + row) * SUB
-                    far_ref[row * blocks + step * per + p] = moved[at : at + SUB]
+    flat = []
+    for p in range(per):
+        turned = turn([tile_ref[s, p] for s in range(SUB)])
+        flat += [jnp.where(even, turned[i], turned[i + SUB - HALO]) for i in range(HALO)]
+    moved = reorder(jnp.concatenate(flat, axis=0), order[...])
+    for p in range(per):
+        for row in range(HALO):
+            at = (p * HALO + row) * SUB
+            far_ref[row * blocks + step * per + p] = moved[at : at + SUB]
 
 
 def far_edge(raw, kappa, me):
@@ -116,19 +107,20 @@
     return pl.pallas_call(
         far_kernel,
         name="far_edge",
-        grid=(blocks // per,),
-        in_specs=[
-            SM,
-            pl.BlockSpec((SUB, per, SUB, width), lambda i: (0, i, 0, 0)),
-            pl.BlockSpec((SUB, per, SUB, width), lambda i: (0, i, last, 0)),
-            pl.BlockSpec((rows, width), lambda i: (0, 0)),
-        ],
-        out_specs=pl.BlockSpec((count, SUB, width), lambda i: (0, 0, 0)),
+        grid_spec=pltpu.PrefetchScalarGridSpec(
+            num_scalar_prefetch=1,
+            grid=(blocks // per,),
+            in_specs=[
+                pl.BlockSpec((SUB, per, SUB, width), lambda i, at: (0, i, (at[0] & 1) * last, 0)),
+                pl.BlockSpec((rows, width), lambda i, at: (0, 0)),
+            ],
+            out_specs=pl.BlockSpec((count, SUB, width), lambda i, at: (0, 0, 0)),
+            scratch_shapes=[pltpu.VMEM((width, width), BF16)],
+        ),
         out_shape=jax.ShapeDtypeStruct((count, SUB, width), F32),
-        scratch_shapes=[pltpu.VMEM((width, width), BF16)],
         compiler_params=params(60),
         cost_estimate=cost(0, 3 * raw.size),
-    )(me, parts, parts, kappa)
+    )(me, parts, kappa)
 
 
 def pieces_kernel(cuts, me_ref, raw_ref, kap_ref, *rest):
@@ -480,15 +472,13 @@
     return jnp.concatenate(split(x), axis=0)
 
 
-def rows_kernel(counts, added, col_ref, *rest):
+def rows_kernel(counts, col_ref, *rest):
     mats, xs, out_ref = rest[: len(counts)], rest[len(counts) : -1], rest[-1]
-    extra = dict(zip(added, xs[sum(counts) :]))
     width = out_ref.shape[2]
     totals = [None] * SUB
     start = 0
     for mat_ref, count in zip(mats, counts):
-        parts = [xs[i][...] + extra[i][...] if i in extra else xs[i][...] for i in range(start, start + count)]
-        x = jnp.concatenate(parts, axis=0)
+        x = jnp.concatenate([ref[...] for ref in xs[start : start + count]], axis=0)
         start += count
         depth = x.shape[0]
         hi, lo = split(x.reshape(depth * SUB, width))
@@ -500,22 +490,22 @@
         out_ref[z] = totals[z]
 
 
-def mix_rows(col, mats, groups, moved):
+def mix_rows(col, mats, groups):
     blocks = [x for group in groups for x in group]
     own, width = blocks[0].shape[1:]
     rows = mats[0].shape[0]
     depth = sum(x.shape[0] for x in blocks)
     return pl.pallas_call(
-        functools.partial(rows_kernel, [len(g) for g in groups], list(moved)),
+        functools.partial(rows_kernel, [len(g) for g in groups]),
         name="mix_rows",
         grid=(own // SUB,),
         in_specs=[pl.BlockSpec(m.shape, lambda i: (0, 0)) for m in [col, *mats]]
-        + [pl.BlockSpec((x.shape[0], SUB, width), lambda i: (0, i, 0)) for x in [*blocks, *moved.values()]],
+        + [pl.BlockSpec((x.shape[0], SUB, width), lambda i: (0, i, 0)) for x in blocks],
         out_specs=pl.BlockSpec((SUB, rows, width), lambda i: (i, 0, 0)),
         out_shape=jax.ShapeDtypeStruct((own, rows, width), F32),
         compiler_params=params(36),
         cost_estimate=cost(4 * own * depth * width * (width + rows), 4 * own * width * (depth + rows)),
-    )(col, *mats, *blocks, *moved.values())
+    )(col, *mats, *blocks)
 
 
 def finish_kernel(count, mat_ref, base_ref, *rest):
@@ -572,24 +562,19 @@
     near_in = lax.ppermute(near, "tile", [(t, t ^ 1) for t in range(devices)])
     level_mat = order_levels(devices, one, vertical_cov)
 
-    def exchange(mixed, without={}):
+    def exchange(mixed):
         got = [mixed[0]] + [None] * (devices - 1)
         for span in (range(devices // 2, devices), range(devices // 2 - 1, 0, -1)):
             for s in span:
-                pairs = [(t, t ^ s) for t in range(devices) if t not in without.get(s, ())]
-                got[s] = lax.ppermute(mixed[s], "tile", pairs)
+                got[s] = lax.ppermute(mixed[s], "tile", [(t, t ^ s) for t in range(devices)])
         return got
 
-    cross = devices // 2 + 1
-    movers = [devices // 2 - 1, devices // 2] if devices == 8 and RELAY else []
     groups = []
     own = [*parts, far, near]
     for j, (first, count) in enumerate(cuts):
         ev = steps([first], count, one, inside, half_wind, kappa, cuts, own)
         mixed = mix_levels(devices, one, ev, [follow[j]], level_mat)
-        groups.append(exchange(mixed, {cross: movers} if j == 1 else {}))
-        if j == 1 and movers:
-            aside = lax.ppermute(mixed[cross], "tile", [(t, t ^ 1) for t in movers])
+        groups.append(exchange(mixed))
         *own, _ = lax.optimization_barrier((*own, mixed[0]))
         if j == 0:
             follow.append(earlier(own[2]))
@@ -597,15 +582,10 @@
             row, col, _ = lax.optimization_barrier((row_cov, column_cov, mixed[0]))
             col_mat, *row_mats = order_rest(chunks, devices, one, row, col)
             follow_edges = [earlier(own[3]), earlier(own[4])]
-    moved = {}
-    if movers:
-        aside = lax.ppermute(aside, "tile", [(t ^ 1, t ^ cross) for t in movers])
-        moved = {devices + cross: aside}
-
     ev = steps([0, rows - HALO], HALO, one, inside, half_wind, kappa, cuts, own, [far_in, near_in])
     halves = levels // devices // SUB
     mixed = mix_levels(devices * halves, one, ev, follow_edges, level_mat, col_mat)
-    base = mix_rows(col_mat, row_mats[:3], groups, moved)
+    base = mix_rows(col_mat, row_mats[:3], groups)
     out = None
     for h in range(halves):
         last = exchange(mixed[h::halves])

time: 330 us -> 330 us (level)
  no operation moved by 1% of the time
where the time goes in v3:
time: 330 us; the launch traced here: 329 us
  waiting for transfers between devices  170 us (52%)
  Pallas kernels  89.4 us (27%)
  starting transfers between devices  67 us (20%)
    ppermute x35, waiting for transfers between devices, exchange(): lax.ppermute(mixed[s], 'tile', [(t, t ^ s) for t in range(devices)])  156 us
    ppermute x35, starting transfers between devices, exchange(): lax.ppermute(mixed[s], 'tile', [(t, t ^ s) for t in range(devices)])  49.4 us
    pallas_call x4, Pallas kernels, steps(): pl.pallas_call(functools.partial(steps_kernel, plans, [f - HALO for f in...  47.6 us
    ppermute x5, waiting for transfers between devices, earlier(): return lax.ppermute(x, 'win', [(i + 1, i) for i in range(windows - 1)])  14.1 us
    ppermute x5, starting transfers between devices, earlier(): return lax.ppermute(x, 'win', [(i + 1, i) for i in range(windows - 1)])  12.7 us
    pallas_call x4, Pallas kernels, mix_levels(): pl.pallas_call(functools.partial(levels_kernel, edges, col is not None),...  11.3 us
    pallas_call x1, Pallas kernels, pieces(): pl.pallas_call(functools.partial(pieces_kernel, cuts), name='pieces', gri...  11 us
    pallas_call x1, Pallas kernels, mix_rows(): pl.pallas_call(functools.partial(rows_kernel, [len(g) for g in groups]),...  7.64 us
  transfers between devices with their start and end apart: 42, of which 24 were waited for; matrix products, arithmetic and copies ran while one was open for 0% of the time, Pallas kernels for 23%

profile of v3, /device:TPU:10, one launch (start us, length us, event | category | flops | bytes accessed | tf_op | source)
XLA Modules:
  0.0 329.0 jit_solution(8029568966627956164)
XLA Ops:
  0.0 11.0 %pieces.1 = (f32[4,16,8,512]{3,2,1,0:T(8,128)}, f32[8,16,8,512]{3,2,1,0:T(8,128)}, f32[8,16,8,512]{3,2,1,0:T(8,128)}, f32[97,8,512]{2,1,0:T(8,128)}, f32[32,512]{1,0:T(8,128)}) custom-call(s32[1]{0:T(128)} %bitcast.me_ref, f32[8,16,32,512]{3,2,1,0:T(8,128)} %bitcast.24, f32[32,512]{1,0:T(8,128)} %bitcast.26), custom_call_target="tpu_custom_call" | custom-call | flops 4294967296 | bytes 16777216 | tf_op jit(solution)/shard_map/pieces/pallas_call | solution.py:160
  15.8 5.0 %far_edge.1.rest_3_.rest_2_ = f32[97,8,512]{2,1,0:T(8,128)} custom-call(s32[1]{0:T(128)} %bitcast.me_ref, f32[8,16,32,512]{3,2,1,0:T(8,128)} %bitcast.25, f32[32,512]{1,0:T(8,128)} %bitcast.27), custom_call_target="tpu_custom_call" | custom-call | bytes 6291456 | tf_op jit(solution)/shard_map/far_edge/pallas_call | solution.py:107
  20.8 3.3 %collective-permute-start.24 = (f32[97,8,512]{2,1,0:T(8,128)}, f32[97,8,512]{2,1,0:T(8,128)}, u32[]{:S(2)}, u32[]{:S(2)}) collective-permute-start(f32[97,8,512]{2,1,0:T(8,128)} %far_edge.1.rest_3_.rest_2_), channel_id=1, source_target_pairs={{1,2},{3,4},{5,6},{2,1},{4,3},{6,5},{9,10},{11,12},{13,14},{10,9},... | collective-permute-start | bytes 4767752 | tf_op jit(solution)/shard_map/ppermute | solution.py:559
  26.4 7.6 %shard_map.64.ev_ref = f32[4,16,8,512]{3,2,1,0:T(8,128)S(1)} custom-call(s32[1]{0:T(128)} %bitcast.me_ref, f32[2]{0:T(128)S(1)} %add_convert_fusion.inside_ref, f32[16,8,128]{2,1,0:T(8,128)S(1)} %broadcast_in_dim.4.hw_ref, f32[32,512]{1,0:T(8,128)S(1)} %copy-done.5, f32[64,8,512]{2,1,0:T(8,128)S(1)} %bitcast.21, f32[128,8,512]{2,1,0:T(8,128)S(1)} %bitcast.11, ...), custom_call_target="tpu_custom_call" | custom-call | flops 49545216 | bytes 5242880 | tf_op jit(solution)/shard_map/pallas_call | solution.py:339
  34.0 14.1 %collective-permute-done.rest_0_ = f32[64,8,512]{2,1,0:T(8,128)} collective-permute-done((f32[64,8,512]{2,1,0:T(8,128)}, f32[64,8,512]{2,1,0:T(8,128)}, u32[]{:S(2)}, u32[]{:S(2)}) %collective-permute-start) | collective-permute-done | bytes 1048608 | tf_op jit(solution)/shard_map/ppermute | solution.py:556
  49.7 4.1 %collective-permute-start.16 = (f32[128,8,512]{2,1,0:T(8,128)S(1)}, f32[128,8,512]{2,1,0:T(8,128)S(1)}, u32[]{:S(2)}, u32[]{:S(2)}) collective-permute-start(f32[128,8,512]{2,1,0:T(8,128)S(1)} %bitcast.16), channel_id=1, source_target_pairs={{8,0},{16,8},{24,16},{9,1},{17,9},{25,17},{10,2},{18,10},{26,18},{... | collective-permute-start | bytes 6291464 | tf_op jit(solution)/shard_map/ppermute | solution.py:556
  55.9 42.4 %collective-permute-done.2.rest_4_ = f32[4,16,512]{2,1,0:T(8,128)S(1)} collective-permute-done((f32[4,16,512]{2,1,0:T(8,128)S(1)}, f32[4,16,512]{2,1,0:T(8,128)S(1)}, u32[]{:S(2)}, u32[]{:S(2)}) %collective-permute-start.2) | collective-permute-done | bytes 131104 | tf_op jit(solution)/shard_map/ppermute | solution.py:569
  98.3 5.4 %collective-permute-done.3.rest_5_ = f32[4,16,512]{2,1,0:T(8,128)S(1)} collective-permute-done((f32[4,16,512]{2,1,0:T(8,128)S(1)}, f32[4,16,512]{2,1,0:T(8,128)S(1)}, u32[]{:S(2)}, u32[]{:S(2)}) %collective-permute-start.3) | collective-permute-done | bytes 131104 | tf_op jit(solution)/shard_map/ppermute | solution.py:569
  105.1 4.5 %collective-permute-done.4.rest_6_ = f32[4,16,512]{2,1,0:T(8,128)S(1)} collective-permute-done((f32[4,16,512]{2,1,0:T(8,128)S(1)}, f32[4,16,512]{2,1,0:T(8,128)S(1)}, u32[]{:S(2)}, u32[]{:S(2)}) %collective-permute-start.4) | collective-permute-done | bytes 131104 | tf_op jit(solution)/shard_map/ppermute | solution.py:569
  112.2 3.8 %collective-permute-done.5.rest_7_ = f32[4,16,512]{2,1,0:T(8,128)S(1)} collective-permute-done((f32[4,16,512]{2,1,0:T(8,128)S(1)}, f32[4,16,512]{2,1,0:T(8,128)S(1)}, u32[]{:S(2)}, u32[]{:S(2)}) %collective-permute-start.5) | collective-permute-done | bytes 131104 | tf_op jit(solution)/shard_map/ppermute | solution.py:569
  115.9 3.3 %collective-permute-start.6 = (f32[4,16,512]{2,1,0:T(8,128)S(1)}, f32[4,16,512]{2,1,0:T(8,128)S(1)}, u32[]{:S(2)}, u32[]{:S(2)}) collective-permute-start(f32[4,16,512]{2,1,0:T(8,128)S(1)} %get-tuple-element.94), channel_id=1, source_target_pairs={{0,5},{1,4},{2,7},{3,6},{4,1},{5,0},{6,3},{7,2},{8,13},{9,12},{10,... | collective-permute-start | bytes 393224 | tf_op jit(solution)/shard_map/ppermute | solution.py:569
  119.7 10.6 %shard_map.65.ev_ref = f32[8,16,8,512]{3,2,1,0:T(8,128)S(1)} custom-call(s32[1]{0:T(128)} %bitcast.me_ref, f32[2]{0:T(128)S(1)} %add_convert_fusion.inside_ref, f32[16,8,128]{2,1,0:T(8,128)S(1)} %broadcast_in_dim.4.hw_ref, f32[32,512]{1,0:T(8,128)S(1)} %copy-done.5, f32[64,8,512]{2,1,0:T(8,128)S(1)} %bitcast.22, f32[128,8,512]{2,1,0:T(8,128)S(1)} %bitcast.12, ...), custom_call_target="tpu_custom_call" | custom-call | flops 71565312 | bytes 7340032 | tf_op jit(solution)/shard_map/pallas_call | solution.py:339
  130.3 3.1 mix_levels.5
  137.9 7.2 %collective-permute-done.8.rest_10_ = f32[4,16,512]{2,1,0:T(8,128)S(1)} collective-permute-done((f32[4,16,512]{2,1,0:T(8,128)S(1)}, f32[4,16,512]{2,1,0:T(8,128)S(1)}, u32[]{:S(2)}, u32[]{:S(2)}) %collective-permute-start.8) | collective-permute-done | bytes 131104 | tf_op jit(solution)/shard_map/ppermute | solution.py:569
  148.3 7.6 %collective-permute-done.9.rest_12_ = f32[8,16,512]{2,1,0:T(8,128)S(1)} collective-permute-done((f32[8,16,512]{2,1,0:T(8,128)S(1)}, f32[8,16,512]{2,1,0:T(8,128)S(1)}, u32[]{:S(2)}, u32[]{:S(2)}) %collective-permute-start.9) | collective-permute-done | bytes 262176 | tf_op jit(solution)/shard_map/ppermute | solution.py:569
  156.7 3.2 collective-permute-start.12
  159.9 7.7 %collective-permute-done.11.rest_14_ = f32[8,16,512]{2,1,0:T(8,128)S(1)} collective-permute-done((f32[8,16,512]{2,1,0:T(8,128)S(1)}, f32[8,16,512]{2,1,0:T(8,128)S(1)}, u32[]{:S(2)}, u32[]{:S(2)}) %collective-permute-start.11) | collective-permute-done | bytes 262176 | tf_op jit(solution)/shard_map/ppermute | solution.py:569
  172.5 10.8 %shard_map.66.ev_ref = f32[8,16,8,512]{3,2,1,0:T(8,128)S(1)} custom-call(s32[1]{0:T(128)} %bitcast.me_ref, f32[2]{0:T(128)S(1)} %add_convert_fusion.inside_ref, f32[16,8,128]{2,1,0:T(8,128)S(1)} %broadcast_in_dim.4.hw_ref, f32[32,512]{1,0:T(8,128)S(1)} %copy-done.5, f32[64,8,512]{2,1,0:T(8,128)S(1)} %bitcast.23, f32[128,8,512]{2,1,0:T(8,128)S(1)} %bitcast.13, ...), custom_call_target="tpu_custom_call" | custom-call | flops 71565312 | bytes 7340032 | tf_op jit(solution)/shard_map/pallas_call | solution.py:339
  185.6 9.1 %collective-permute-done.13.rest_16_ = f32[8,16,512]{2,1,0:T(8,128)S(1)} collective-permute-done((f32[8,16,512]{2,1,0:T(8,128)S(1)}, f32[8,16,512]{2,1,0:T(8,128)S(1)}, u32[]{:S(2)}, u32[]{:S(2)}) %collective-permute-start.13) | collective-permute-done | bytes 262176 | tf_op jit(solution)/shard_map/ppermute | solution.py:569
  194.7 5.6 %collective-permute-done.14.rest_17_ = f32[8,16,512]{2,1,0:T(8,128)S(1)} collective-permute-done((f32[8,16,512]{2,1,0:T(8,128)S(1)}, f32[8,16,512]{2,1,0:T(8,128)S(1)}, u32[]{:S(2)}, u32[]{:S(2)}) %collective-permute-start.14) | collective-permute-done | bytes 262176 | tf_op jit(solution)/shard_map/ppermute | solution.py:569
  200.3 5.1 %collective-permute-done.15.rest_18_ = f32[8,16,512]{2,1,0:T(8,128)S(1)} collective-permute-done((f32[8,16,512]{2,1,0:T(8,128)S(1)}, f32[8,16,512]{2,1,0:T(8,128)S(1)}, u32[]{:S(2)}, u32[]{:S(2)}) %collective-permute-start.15) | collective-permute-done | bytes 262176 | tf_op jit(solution)/shard_map/ppermute | solution.py:569
  213.2 18.7 %shard_map.67.ev_ref = f32[12,16,8,512]{3,2,1,0:T(8,128)S(1)} custom-call(s32[1]{0:T(128)} %bitcast.me_ref, f32[2]{0:T(128)S(1)} %add_convert_fusion.inside_ref, f32[16,8,128]{2,1,0:T(8,128)S(1)} %broadcast_in_dim.4.hw_ref, f32[32,512]{1,0:T(8,128)S(1)} %copy-done.5, f32[128,8,512]{2,1,0:T(8,128)S(1)} %bitcast.14, f32[128,8,512]{2,1,0:T(8,128)S(1)} %bitcast.19, ...), custom_call_target="tpu_custom_call" | custom-call | flops 121110528 | bytes 12582912 | tf_op jit(solution)/shard_map/pallas_call | solution.py:339
  231.9 5.2 %mix_levels.7 = (f32[12,8,512]{2,1,0:T(8,128)S(1)}, f32[12,8,512]{2,1,0:T(8,128)S(1)}, f32[12,8,512]{2,1,0:T(8,128)S(1)}, f32[12,8,512]{2,1,0:T(8,128)S(1)}, f32...) custom-call(s32[1]{0:T(128)} %bitcast.me_ref, ...), custom_call_target="tpu_custom_call" | custom-call | flops 402653184 | bytes 9437184 | tf_op jit(solution)/shard_map/mix_levels/pallas_call | solution.py:448
  244.7 5.8 %collective-permute-done.22.rest_25_ = f32[8,16,512]{2,1,0:T(8,128)S(1)} collective-permute-done((f32[8,16,512]{2,1,0:T(8,128)S(1)}, f32[8,16,512]{2,1,0:T(8,128)S(1)}, u32[]{:S(2)}, u32[]{:S(2)}) %collective-permute-start.22) | collective-permute-done | bytes 262176 | tf_op jit(solution)/shard_map/ppermute | solution.py:569
  250.5 4.6 %collective-permute-done.23.rest_26_ = f32[8,16,512]{2,1,0:T(8,128)S(1)} collective-permute-done((f32[8,16,512]{2,1,0:T(8,128)S(1)}, f32[8,16,512]{2,1,0:T(8,128)S(1)}, u32[]{:S(2)}, u32[]{:S(2)}) %collective-permute-start.23) | collective-permute-done | bytes 262176 | tf_op jit(solution)/shard_map/ppermute | solution.py:569
  265.7 13.6 %collective-permute-done.38.rest_4_ = f32[12,8,512]{2,1,0:T(8,128)S(1)} collective-permute-done((f32[12,8,512]{2,1,0:T(8,128)S(1)}, f32[12,8,512]{2,1,0:T(8,128)S(1)}, u32[]{:S(2)}, u32[]{:S(2)}) %collective-permute-start.38) | collective-permute-done | bytes 196640 | tf_op jit(solution)/shard_map/ppermute | solution.py:569
  279.3 3.9 %collective-permute-start.31 = (f32[12,8,512]{2,1,0:T(8,128)S(1)}, f32[12,8,512]{2,1,0:T(8,128)S(1)}, u32[]{:S(2)}, u32[]{:S(2)}) collective-permute-start(f32[12,8,512]{2,1,0:T(8,128)S(1)} %get-tuple-element.125), channel_id=1, source_target_pairs={{0,4},{1,5},{2,6},{3,7},{4,0},{5,1},{6,2},{7,3},{8,12},{9,13},{10,... | collective-permute-start | bytes 589832 | tf_op jit(solution)/shard_map/ppermute | solution.py:569
  283.1 11.2 %collective-permute-done.39.rest_5_ = f32[12,8,512]{2,1,0:T(8,128)S(1)} collective-permute-done((f32[12,8,512]{2,1,0:T(8,128)S(1)}, f32[12,8,512]{2,1,0:T(8,128)S(1)}, u32[]{:S(2)}, u32[]{:S(2)}) %collective-permute-start.39) | collective-permute-done | bytes 196640 | tf_op jit(solution)/shard_map/ppermute | solution.py:569
  294.4 4.3 %collective-permute-start.32 = (f32[12,8,512]{2,1,0:T(8,128)S(1)}, f32[12,8,512]{2,1,0:T(8,128)S(1)}, u32[]{:S(2)}, u32[]{:S(2)}) collective-permute-start(f32[12,8,512]{2,1,0:T(8,128)S(1)} %get-tuple-element.126), channel_id=1, source_target_pairs={{0,5},{1,4},{2,7},{3,6},{4,1},{5,0},{6,3},{7,2},{8,13},{9,12},{10,... | collective-permute-start | bytes 589832 | tf_op jit(solution)/shard_map/ppermute | solution.py:569
  298.7 7.9 %collective-permute-done.40.rest_6_ = f32[12,8,512]{2,1,0:T(8,128)S(1)} collective-permute-done((f32[12,8,512]{2,1,0:T(8,128)S(1)}, f32[12,8,512]{2,1,0:T(8,128)S(1)}, u32[]{:S(2)}, u32[]{:S(2)}) %collective-permute-start.40) | collective-permute-done | bytes 196640 | tf_op jit(solution)/shard_map/ppermute | solution.py:569
  306.6 4.2 %collective-permute-done.41.rest_7_ = f32[12,8,512]{2,1,0:T(8,128)S(1)} collective-permute-done((f32[12,8,512]{2,1,0:T(8,128)S(1)}, f32[12,8,512]{2,1,0:T(8,128)S(1)}, u32[]{:S(2)}, u32[]{:S(2)}) %collective-permute-start.41) | collective-permute-done | bytes 196640 | tf_op jit(solution)/shard_map/ppermute | solution.py:569
  312.5 7.6 %mix_rows.1.base_ref = f32[16,256,512]{2,1,0:T(8,128)S(1)} custom-call(bf16[512,512]{1,0:T(8,128)(2,1)S(1)} %get-tuple-element.86.col_ref.rest_2_, bf16[256,64]{1,0:T(8,128)(2,1)S(1)} %get-tuple-element.87.rest_0_, bf16[256,128]{1,0:T(8,128)(2,1)S(1)} %get-tuple-element.88.rest_1_, bf16[256,128]{1,0:T(8,128)(2,1)S(1)} %get-tuple-element.89.rest_2_, ...), custom_call_target="tpu_custom_call" | custom-call | flops 4026531840 | bytes 13631488 | tf_op jit(solution)/shard_map/mix_rows/pallas_call | solution.py:498
  (92 shorter events, 67.3 us)
Async XLA Ops:
  11.0 108.2 %collective-permute-start.1 = (f32[128,8,512]{2,1,0:T(8,128)}, f32[128,8,512]{2,1,0:T(8,128)}, u32[]{:S(2)}, u32[]{:S(2)}) collective-permute-start(f32[128,8,512]{2,1,0:T(8,128)} %bitcast.10), channel_id=1, source_target_pairs={{8,0},{16,8},{24,16},{9,1},{17,9},{25,17},{10,2},{18,10},{26,18},{... | collective-permute-start | bytes 6291464 | tf_op jit(solution)/shard_map/ppermute | solution.py:556
  13.0 35.0 %collective-permute-start = (f32[64,8,512]{2,1,0:T(8,128)}, f32[64,8,512]{2,1,0:T(8,128)}, u32[]{:S(2)}, u32[]{:S(2)}) collective-permute-start(f32[64,8,512]{2,1,0:T(8,128)} %bitcast.20), channel_id=1, source_target_pairs={{8,0},{16,8},{24,16},{9,1},{17,9},{25,17},{10,2},{18,10},{26,18},{... | collective-permute-start | bytes 3145736 | tf_op jit(solution)/shard_map/ppermute | solution.py:556
  20.8 126.2 %collective-permute-start.24 = (f32[97,8,512]{2,1,0:T(8,128)}, f32[97,8,512]{2,1,0:T(8,128)}, u32[]{:S(2)}, u32[]{:S(2)}) collective-permute-start(f32[97,8,512]{2,1,0:T(8,128)} %far_edge.1.rest_3_.rest_2_), channel_id=1, source_target_pairs={{1,2},{3,4},{5,6},{2,1},{4,3},{6,5},{9,10},{11,12},{13,14},{10,9},... | collective-permute-start | bytes 4767752 | tf_op jit(solution)/shard_map/ppermute | solution.py:559
  49.7 120.2 %collective-permute-start.16 = (f32[128,8,512]{2,1,0:T(8,128)S(1)}, f32[128,8,512]{2,1,0:T(8,128)S(1)}, u32[]{:S(2)}, u32[]{:S(2)}) collective-permute-start(f32[128,8,512]{2,1,0:T(8,128)S(1)} %bitcast.16), channel_id=1, source_target_pairs={{8,0},{16,8},{24,16},{9,1},{17,9},{25,17},{10,2},{18,10},{26,18},{... | collective-permute-start | bytes 6291464 | tf_op jit(solution)/shard_map/ppermute | solution.py:556
  53.9 94.3 %collective-permute-start.25 = (f32[97,8,512]{2,1,0:T(8,128)S(1)}, f32[97,8,512]{2,1,0:T(8,128)S(1)}, u32[]{:S(2)}, u32[]{:S(2)}) collective-permute-start(f32[97,8,512]{2,1,0:T(8,128)S(1)} %copy-done.3), channel_id=1, source_target_pairs={{0,1},{1,0},{2,3},{3,2},{4,5},{5,4},{6,7},{7,6},{8,9},{9,8},{10,11... | collective-permute-start | bytes 4767752 | tf_op jit(solution)/shard_map/ppermute | solution.py:562
  55.4 42.9 %collective-permute-start.2 = (f32[4,16,512]{2,1,0:T(8,128)S(1)}, f32[4,16,512]{2,1,0:T(8,128)S(1)}, u32[]{:S(2)}, u32[]{:S(2)}) collective-permute-start(f32[4,16,512]{2,1,0:T(8,128)S(1)} %get-tuple-element.90), channel_id=1, source_target_pairs={{0,1},{1,0},{2,3},{3,2},{4,5},{5,4},{6,7},{7,6},{8,9},{9,8},{10,11... | collective-permute-start | bytes 393224 | tf_op jit(solution)/shard_map/ppermute | solution.py:569
  115.9 17.5 %collective-permute-start.6 = (f32[4,16,512]{2,1,0:T(8,128)S(1)}, f32[4,16,512]{2,1,0:T(8,128)S(1)}, u32[]{:S(2)}, u32[]{:S(2)}) collective-permute-start(f32[4,16,512]{2,1,0:T(8,128)S(1)} %get-tuple-element.94), channel_id=1, source_target_pairs={{0,5},{1,4},{2,7},{3,6},{4,1},{5,0},{6,3},{7,2},{8,13},{9,12},{10,... | collective-permute-start | bytes 393224 | tf_op jit(solution)/shard_map/ppermute | solution.py:569
  119.2 16.1 %collective-permute-start.7 = (f32[4,16,512]{2,1,0:T(8,128)S(1)}, f32[4,16,512]{2,1,0:T(8,128)S(1)}, u32[]{:S(2)}, u32[]{:S(2)}) collective-permute-start(f32[4,16,512]{2,1,0:T(8,128)S(1)} %get-tuple-element.95), channel_id=1, source_target_pairs={{0,6},{1,7},{2,4},{3,5},{4,2},{5,3},{6,0},{7,1},{8,14},{9,15},{10,... | collective-permute-start | bytes 393224 | tf_op jit(solution)/shard_map/ppermute | solution.py:569
  133.4 76.0 %collective-permute-start.26 = (f32[97,8,512]{2,1,0:T(8,128)S(1)}, f32[97,8,512]{2,1,0:T(8,128)S(1)}, u32[]{:S(2)}, u32[]{:S(2)}) collective-permute-start(f32[97,8,512]{2,1,0:T(8,128)S(1)} %copy-done.2), channel_id=1, source_target_pairs={{8,0},{16,8},{24,16},{9,1},{17,9},{25,17},{10,2},{18,10},{26,18},{... | collective-permute-start | bytes 4767752 | tf_op jit(solution)/shard_map/ppermute | solution.py:556
  145.1 65.7 %collective-permute-start.27 = (f32[97,8,512]{2,1,0:T(8,128)S(1)}, f32[97,8,512]{2,1,0:T(8,128)S(1)}, u32[]{:S(2)}, u32[]{:S(2)}) collective-permute-start(f32[97,8,512]{2,1,0:T(8,128)S(1)} %copy-done.3), channel_id=1, source_target_pairs={{8,0},{16,8},{24,16},{9,1},{17,9},{25,17},{10,2},{18,10},{26,18},{... | collective-permute-start | bytes 4767752 | tf_op jit(solution)/shard_map/ppermute | solution.py:556
  156.7 27.8 %collective-permute-start.12 = (f32[8,16,512]{2,1,0:T(8,128)S(1)}, f32[8,16,512]{2,1,0:T(8,128)S(1)}, u32[]{:S(2)}, u32[]{:S(2)}) collective-permute-start(f32[8,16,512]{2,1,0:T(8,128)S(1)} %get-tuple-element.100), channel_id=1, source_target_pairs={{0,4},{1,5},{2,6},{3,7},{4,0},{5,1},{6,2},{7,3},{8,12},{9,13},{10,... | collective-permute-start | bytes 786440 | tf_op jit(solution)/shard_map/ppermute | solution.py:569
  167.6 27.1 %collective-permute-start.13 = (f32[8,16,512]{2,1,0:T(8,128)S(1)}, f32[8,16,512]{2,1,0:T(8,128)S(1)}, u32[]{:S(2)}, u32[]{:S(2)}) collective-permute-start(f32[8,16,512]{2,1,0:T(8,128)S(1)} %get-tuple-element.101), channel_id=1, source_target_pairs={{0,5},{1,4},{2,7},{3,6},{4,1},{5,0},{6,3},{7,2},{8,13},{9,12},{10,... | collective-permute-start | bytes 786440 | tf_op jit(solution)/shard_map/ppermute | solution.py:569
  170.0 30.4 %collective-permute-start.14 = (f32[8,16,512]{2,1,0:T(8,128)S(1)}, f32[8,16,512]{2,1,0:T(8,128)S(1)}, u32[]{:S(2)}, u32[]{:S(2)}) collective-permute-start(f32[8,16,512]{2,1,0:T(8,128)S(1)} %get-tuple-element.102), channel_id=1, source_target_pairs={{0,6},{1,7},{2,4},{3,5},{4,2},{5,3},{6,0},{7,1},{8,14},{9,15},{10,... | collective-permute-start | bytes 786440 | tf_op jit(solution)/shard_map/ppermute | solution.py:569
  184.5 20.9 %collective-permute-start.15 = (f32[8,16,512]{2,1,0:T(8,128)S(1)}, f32[8,16,512]{2,1,0:T(8,128)S(1)}, u32[]{:S(2)}, u32[]{:S(2)}) collective-permute-start(f32[8,16,512]{2,1,0:T(8,128)S(1)} %get-tuple-element.103), channel_id=1, source_target_pairs={{0,7},{1,6},{2,5},{3,4},{4,3},{5,2},{6,1},{7,0},{8,15},{9,14},{10,... | collective-permute-start | bytes 786440 | tf_op jit(solution)/shard_map/ppermute | solution.py:569
  194.7 12.0 %collective-permute-start.17 = (f32[8,16,512]{2,1,0:T(8,128)S(1)}, f32[8,16,512]{2,1,0:T(8,128)S(1)}, u32[]{:S(2)}, u32[]{:S(2)}) collective-permute-start(f32[8,16,512]{2,1,0:T(8,128)S(1)} %get-tuple-element.110), channel_id=1, source_target_pairs={{0,1},{1,0},{2,3},{3,2},{4,5},{5,4},{6,7},{7,6},{8,9},{9,8},{10,11... | collective-permute-start | bytes 786440 | tf_op jit(solution)/shard_map/ppermute | solution.py:569
  205.4 31.7 %collective-permute-start.19 = (f32[8,16,512]{2,1,0:T(8,128)S(1)}, f32[8,16,512]{2,1,0:T(8,128)S(1)}, u32[]{:S(2)}, u32[]{:S(2)}) collective-permute-start(f32[8,16,512]{2,1,0:T(8,128)S(1)} %get-tuple-element.112), channel_id=1, source_target_pairs={{0,3},{1,2},{2,1},{3,0},{4,7},{5,6},{6,5},{7,4},{8,11},{9,10},{10,... | collective-permute-start | bytes 786440 | tf_op jit(solution)/shard_map/ppermute | solution.py:569
  206.7 31.8 %collective-permute-start.20 = (f32[8,16,512]{2,1,0:T(8,128)S(1)}, f32[8,16,512]{2,1,0:T(8,128)S(1)}, u32[]{:S(2)}, u32[]{:S(2)}) collective-permute-start(f32[8,16,512]{2,1,0:T(8,128)S(1)} %get-tuple-element.113), channel_id=1, source_target_pairs={{0,4},{1,5},{2,6},{3,7},{4,0},{5,1},{6,2},{7,3},{8,12},{9,13},{10,... | collective-permute-start | bytes 786440 | tf_op jit(solution)/shard_map/ppermute | solution.py:569
  209.3 34.8 %collective-permute-start.21 = (f32[8,16,512]{2,1,0:T(8,128)S(1)}, f32[8,16,512]{2,1,0:T(8,128)S(1)}, u32[]{:S(2)}, u32[]{:S(2)}) collective-permute-start(f32[8,16,512]{2,1,0:T(8,128)S(1)} %get-tuple-element.114), channel_id=1, source_target_pairs={{0,5},{1,4},{2,7},{3,6},{4,1},{5,0},{6,3},{7,2},{8,13},{9,12},{10,... | collective-permute-start | bytes 786440 | tf_op jit(solution)/shard_map/ppermute | solution.py:569
  209.4 41.1 %collective-permute-start.22 = (f32[8,16,512]{2,1,0:T(8,128)S(1)}, f32[8,16,512]{2,1,0:T(8,128)S(1)}, u32[]{:S(2)}, u32[]{:S(2)}) collective-permute-start(f32[8,16,512]{2,1,0:T(8,128)S(1)} %get-tuple-element.115), channel_id=1, source_target_pairs={{0,6},{1,7},{2,4},{3,5},{4,2},{5,3},{6,0},{7,1},{8,14},{9,15},{10,... | collective-permute-start | bytes 786440 | tf_op jit(solution)/shard_map/ppermute | solution.py:569
  210.8 44.3 %collective-permute-start.23 = (f32[8,16,512]{2,1,0:T(8,128)S(1)}, f32[8,16,512]{2,1,0:T(8,128)S(1)}, u32[]{:S(2)}, u32[]{:S(2)}) collective-permute-start(f32[8,16,512]{2,1,0:T(8,128)S(1)} %get-tuple-element.116), channel_id=1, source_target_pairs={{0,7},{1,6},{2,5},{3,4},{4,3},{5,2},{6,1},{7,0},{8,15},{9,14},{10,... | collective-permute-start | bytes 786440 | tf_op jit(solution)/shard_map/ppermute | solution.py:569
  237.1 18.0 %collective-permute-start.28 = (f32[12,8,512]{2,1,0:T(8,128)S(1)}, f32[12,8,512]{2,1,0:T(8,128)S(1)}, u32[]{:S(2)}, u32[]{:S(2)}) collective-permute-start(f32[12,8,512]{2,1,0:T(8,128)S(1)} %get-tuple-element.122), channel_id=1, source_target_pairs={{0,1},{1,0},{2,3},{3,2},{4,5},{5,4},{6,7},{7,6},{8,9},{9,8},{10,11... | collective-permute-start | bytes 589832 | tf_op jit(solution)/shard_map/ppermute | solution.py:569
  238.5 19.1 %collective-permute-start.29 = (f32[12,8,512]{2,1,0:T(8,128)S(1)}, f32[12,8,512]{2,1,0:T(8,128)S(1)}, u32[]{:S(2)}, u32[]{:S(2)}) collective-permute-start(f32[12,8,512]{2,1,0:T(8,128)S(1)} %get-tuple-element.123), channel_id=1, source_target_pairs={{0,2},{1,3},{2,0},{3,1},{4,6},{5,7},{6,4},{7,5},{8,10},{9,11},{10,... | collective-permute-start | bytes 589832 | tf_op jit(solution)/shard_map/ppermute | solution.py:569
  244.1 14.6 %collective-permute-start.35 = (f32[12,8,512]{2,1,0:T(8,128)S(1)}, f32[12,8,512]{2,1,0:T(8,128)S(1)}, u32[]{:S(2)}, u32[]{:S(2)}) collective-permute-start(f32[12,8,512]{2,1,0:T(8,128)S(1)} %get-tuple-element.130), channel_id=1, source_target_pairs={{0,1},{1,0},{2,3},{3,2},{4,5},{5,4},{6,7},{7,6},{8,9},{9,8},{10,11... | collective-permute-start | bytes 589832 | tf_op jit(solution)/shard_map/ppermute | solution.py:569
  255.1 24.2 %collective-permute-start.38 = (f32[12,8,512]{2,1,0:T(8,128)S(1)}, f32[12,8,512]{2,1,0:T(8,128)S(1)}, u32[]{:S(2)}, u32[]{:S(2)}) collective-permute-start(f32[12,8,512]{2,1,0:T(8,128)S(1)} %get-tuple-element.133), channel_id=1, source_target_pairs={{0,4},{1,5},{2,6},{3,7},{4,0},{5,1},{6,2},{7,3},{8,12},{9,13},{10,... | collective-permute-start | bytes 589832 | tf_op jit(solution)/shard_map/ppermute | solution.py:569
  257.6 36.7 %collective-permute-start.39 = (f32[12,8,512]{2,1,0:T(8,128)S(1)}, f32[12,8,512]{2,1,0:T(8,128)S(1)}, u32[]{:S(2)}, u32[]{:S(2)}) collective-permute-start(f32[12,8,512]{2,1,0:T(8,128)S(1)} %get-tuple-element.134), channel_id=1, source_target_pairs={{0,5},{1,4},{2,7},{3,6},{4,1},{5,0},{6,3},{7,2},{8,13},{9,12},{10,... | collective-permute-start | bytes 589832 | tf_op jit(solution)/shard_map/ppermute | solution.py:569
  258.7 47.9 %collective-permute-start.40 = (f32[12,8,512]{2,1,0:T(8,128)S(1)}, f32[12,8,512]{2,1,0:T(8,128)S(1)}, u32[]{:S(2)}, u32[]{:S(2)}) collective-permute-start(f32[12,8,512]{2,1,0:T(8,128)S(1)} %get-tuple-element.135), channel_id=1, source_target_pairs={{0,6},{1,7},{2,4},{3,5},{4,2},{5,3},{6,0},{7,1},{8,14},{9,15},{10,... | collective-permute-start | bytes 589832 | tf_op jit(solution)/shard_map/ppermute | solution.py:569
  259.6 51.2 %collective-permute-start.41 = (f32[12,8,512]{2,1,0:T(8,128)S(1)}, f32[12,8,512]{2,1,0:T(8,128)S(1)}, u32[]{:S(2)}, u32[]{:S(2)}) collective-permute-start(f32[12,8,512]{2,1,0:T(8,128)S(1)} %get-tuple-element.136), channel_id=1, source_target_pairs={{0,7},{1,6},{2,5},{3,4},{4,3},{5,2},{6,1},{7,0},{8,15},{9,14},{10,... | collective-permute-start | bytes 589832 | tf_op jit(solution)/shard_map/ppermute | solution.py:569
  263.8 59.4 %collective-permute-start.30 = (f32[12,8,512]{2,1,0:T(8,128)S(1)}, f32[12,8,512]{2,1,0:T(8,128)S(1)}, u32[]{:S(2)}, u32[]{:S(2)}) collective-permute-start(f32[12,8,512]{2,1,0:T(8,128)S(1)} %get-tuple-element.124), channel_id=1, source_target_pairs={{0,3},{1,2},{2,1},{3,0},{4,7},{5,6},{6,5},{7,4},{8,11},{9,10},{10,... | collective-permute-start | bytes 589832 | tf_op jit(solution)/shard_map/ppermute | solution.py:569
  279.3 43.9 %collective-permute-start.31 = (f32[12,8,512]{2,1,0:T(8,128)S(1)}, f32[12,8,512]{2,1,0:T(8,128)S(1)}, u32[]{:S(2)}, u32[]{:S(2)}) collective-permute-start(f32[12,8,512]{2,1,0:T(8,128)S(1)} %get-tuple-element.125), channel_id=1, source_target_pairs={{0,4},{1,5},{2,6},{3,7},{4,0},{5,1},{6,2},{7,3},{8,12},{9,13},{10,... | collective-permute-start | bytes 589832 | tf_op jit(solution)/shard_map/ppermute | solution.py:569
  294.4 28.8 %collective-permute-start.32 = (f32[12,8,512]{2,1,0:T(8,128)S(1)}, f32[12,8,512]{2,1,0:T(8,128)S(1)}, u32[]{:S(2)}, u32[]{:S(2)}) collective-permute-start(f32[12,8,512]{2,1,0:T(8,128)S(1)} %get-tuple-element.126), channel_id=1, source_target_pairs={{0,5},{1,4},{2,7},{3,6},{4,1},{5,0},{6,3},{7,2},{8,13},{9,12},{10,... | collective-permute-start | bytes 589832 | tf_op jit(solution)/shard_map/ppermute | solution.py:569
  306.6 16.9 %collective-permute-start.33 = (f32[12,8,512]{2,1,0:T(8,128)S(1)}, f32[12,8,512]{2,1,0:T(8,128)S(1)}, u32[]{:S(2)}, u32[]{:S(2)}) collective-permute-start(f32[12,8,512]{2,1,0:T(8,128)S(1)} %get-tuple-element.127), channel_id=1, source_target_pairs={{0,6},{1,7},{2,4},{3,5},{4,2},{5,3},{6,0},{7,1},{8,14},{9,15},{10,... | collective-permute-start | bytes 589832 | tf_op jit(solution)/shard_map/ppermute | solution.py:569
  310.7 15.2 %collective-permute-start.34 = (f32[12,8,512]{2,1,0:T(8,128)S(1)}, f32[12,8,512]{2,1,0:T(8,128)S(1)}, u32[]{:S(2)}, u32[]{:S(2)}) collective-permute-start(f32[12,8,512]{2,1,0:T(8,128)S(1)} %get-tuple-element.128), channel_id=1, source_target_pairs={{0,7},{1,6},{2,5},{3,4},{4,3},{5,2},{6,1},{7,0},{8,15},{9,14},{10,... | collective-permute-start | bytes 589832 | tf_op jit(solution)/shard_map/ppermute | solution.py:569
  (20 other events, 314.6 us)
